TPU v7x, 128 devices: a whole 4x4x4 slice. The times are simulated.
128 devices in a mesh: gx: 16 (over x_hi, y, core), gy: 8 (over z, x_lo).
Axes of the slice: x: 4 (x_hi: 2, x_lo: 2; x = x_hi * 2 + x_lo), y: 4, z: 4, core: 2. Of those that a mesh axis runs over, the one named last changes fastest.
Arguments:
- labels: int32 [128, 256, 64], P('gx', 'gy'), may hold values from 0 to 3
- seed_noise: float32 [4, 128, 256, 64], P(None, 'gx', 'gy'), may hold values from 0.05 to 1
- conc: float32 [128, 256, 64], P('gx', 'gy'), may hold values from 0.1 to 0.9
- curvature: float32 [4], replicated, may hold values from 1 to 4
- quartic: float32 [4], replicated, may hold values from 2 to 16
- wells: float32 [4], replicated, may hold values from 0.1 to 0.9
- lame: float32 [2, 4], replicated, may hold values from 0.5 to 2
- eigen: float32 [4, 6], replicated, may hold values from -3 to 3
Outputs:
- phase_next: float32 [4, 128, 256, 64], P(None, 'gx', 'gy')
- conc_next: float32 [128, 256, 64], P('gx', 'gy')
- stress: float32 [6, 128, 256, 64], P(None, 'gx', 'gy')
All inputs are finite; a program needn't handle non-finite values.
Results may differ from a plain program's by a relative error of at most 0.0003.
Values sent between devices are 32-bit elements; how exact they have to be, the bound alone decides.
No kernel may reach another device: no remote copies, remote signals or barrier semaphores. Data moves between devices by JAX's collectives and lax.ppermute only.
A program may use at most 128 MiB of HBM per device.

v0:
```python
import math

import jax
import jax.numpy as jnp
from jax import lax
from jax.sharding import PartitionSpec as P

NEWTON = 5
ITERS = 2


step_phase = 0.06
step_conc = 0.005


def padded_2(x, sides, width):
    edges = {}
    for axis, dim in sides:
        count, length = (lax.axis_size(axis), x.shape[dim])
        up = [(i, (i + 1) % count) for i in range(count)]
        last = lax.slice_in_dim(x, length - width, length, axis=dim)
        initial = lax.slice_in_dim(x, 0, width, axis=dim)
        edges[dim] = (
            lax.ppermute(last, axis, up),
            lax.ppermute(initial, axis, [(b, a) for a, b in up]),
        )
    done = []
    for _, dim in sides:
        low, high = edges[dim]
        around = [(width, width) if d in done else (0, 0) for d in range(x.ndim)]
        x = jnp.concatenate([jnp.pad(low, around), x, jnp.pad(high, around)], axis=dim)
        done.append(dim)
    return x


def column(values):
    return values.reshape(4, 1, 1, 1)


def phases_from(labels, seed_noise):
    marks = lax.broadcasted_iota(jnp.int32, (4, 1, 1, 1), 0)
    raw = seed_noise + 2.0 * (labels[None] == marks).astype(seed_noise.dtype)
    return raw / jnp.sum(raw, axis=0, keepdims=True)


def partition(phase, conc, curvature, quartic, wells):
    coef_a = column(curvature)
    coef_b = column(quartic)
    centre = column(wells)
    part = jnp.broadcast_to(conc[None], phase.shape)
    deviate = part - centre
    chem = jnp.sum(phase * (coef_a * deviate + coef_b * deviate**3), axis=0)
    for _ in range(NEWTON):
        deviate = part - centre
        slope = coef_a * deviate + coef_b * deviate**3 - chem[None]
        stiff = coef_a + 3.0 * coef_b * deviate * deviate
        shift = (
            conc - jnp.sum(phase * part, axis=0) + jnp.sum(phase * slope / stiff, axis=0)
        ) / jnp.sum(phase / stiff, axis=0)
        part = part + (shift[None] - slope) / stiff
        chem = chem + shift
    return (part, chem)


def stress_of(strain, eigen_field, lam_field, shear_field):
    elastic = strain - eigen_field
    trace = elastic[0] + elastic[1] + elastic[2]
    normal = (lax.broadcasted_iota(jnp.int32, (6, 1, 1, 1), 0) < 3).astype(strain.dtype)
    return 2.0 * shear_field[None] * elastic + (lam_field * trace)[None] * normal


def green(tau, freq_x, freq_y, freq_z, zero, lam0, mu0):
    vec_x = tau[0] * freq_x + tau[5] * freq_y + tau[4] * freq_z
    vec_y = tau[5] * freq_x + tau[1] * freq_y + tau[3] * freq_z
    vec_z = tau[4] * freq_x + tau[3] * freq_y + tau[2] * freq_z
    inner = freq_x * vec_x + freq_y * vec_y + freq_z * vec_z
    square = freq_x * freq_x + freq_y * freq_y + freq_z * freq_z + zero
    first = 1.0 / (2.0 * mu0 * square)
    second = (lam0 + mu0) / (mu0 * (lam0 + 2.0 * mu0)) * inner / (square * square)
    pairs = (
        (freq_x, vec_x, freq_x, vec_x),
        (freq_y, vec_y, freq_y, vec_y),
        (freq_z, vec_z, freq_z, vec_z),
        (freq_y, vec_y, freq_z, vec_z),
        (freq_x, vec_x, freq_z, vec_z),
        (freq_x, vec_x, freq_y, vec_y),
    )
    result = [(fk * vh + fh * vk) * first - fk * fh * second for fk, vk, fh, vh in pairs]
    return jnp.stack(result, axis=0)


def tables(length):
    grid = lax.broadcasted_iota(jnp.int32, (length, length), 0) * lax.broadcasted_iota(
        jnp.int32, (length, length), 1
    )
    angle = (grid % length).astype(jnp.float32) * (2.0 * math.pi / length)
    return (jnp.cos(angle), jnp.sin(angle))


def apply_table(table, data, axis):
    if axis == 3:
        flat = data.reshape(-1, data.shape[3])
        result = jnp.dot(
            flat, table.T, precision=lax.Precision.HIGHEST, preferred_element_type=jnp.float32
        )
        return result.reshape(data.shape[:3] + (table.shape[0],))
    moved = jnp.moveaxis(data, axis, 0)
    rest = moved.shape[1:]
    flat = moved.reshape(moved.shape[0], -1)
    result = jnp.dot(
        table, flat, precision=lax.Precision.HIGHEST, preferred_element_type=jnp.float32
    )
    return jnp.moveaxis(result.reshape((table.shape[0],) + rest), 0, axis)


def transform(pair, axis, inverse):
    real, imag = pair
    length = real.shape[axis]
    cosine, sine = tables(length)
    if inverse:
        new_real = (apply_table(cosine, real, axis) - apply_table(sine, imag, axis)) / length
        new_imag = (apply_table(cosine, imag, axis) + apply_table(sine, real, axis)) / length
    else:
        new_real = apply_table(cosine, real, axis) + apply_table(sine, imag, axis)
        new_imag = apply_table(cosine, imag, axis) - apply_table(sine, real, axis)
    return (new_real, new_imag)


def spectrum(stress):
    length = stress.shape[3]
    cosine, sine = tables(length)
    real = apply_table(cosine, stress, 3)
    imag = -apply_table(sine, stress, 3)
    real, imag = transform(
        (
            lax.all_to_all(real, "gx", split_axis=3, concat_axis=1, tiled=True),
            lax.all_to_all(imag, "gx", split_axis=3, concat_axis=1, tiled=True),
        ),
        axis=1,
        inverse=False,
    )
    real, imag = transform(
        (
            lax.all_to_all(real, "gy", split_axis=1, concat_axis=2, tiled=True),
            lax.all_to_all(imag, "gy", split_axis=1, concat_axis=2, tiled=True),
        ),
        axis=2,
        inverse=False,
    )
    return (real, imag)


def recover(pair):
    pair = transform(pair, 2, True)
    pair = transform(
        (
            lax.all_to_all(pair[0], "gy", split_axis=2, concat_axis=1, tiled=True),
            lax.all_to_all(pair[1], "gy", split_axis=2, concat_axis=1, tiled=True),
        ),
        axis=1,
        inverse=True,
    )
    result = transform(
        (
            lax.all_to_all(pair[0], "gx", split_axis=1, concat_axis=3, tiled=True),
            lax.all_to_all(pair[1], "gx", split_axis=1, concat_axis=3, tiled=True),
        ),
        axis=3,
        inverse=True,
    )
    return result


def frequencies(count, offset, length, axis):
    index = lax.iota(jnp.int32, count) + offset
    index = jnp.where(index >= length // 2, index - length, index)
    kept = jnp.where(index == -(length // 2), 0, index)
    dims_shape = [1, 1, 1]
    dims_shape[axis] = count
    return (kept.astype(jnp.float32) / length).reshape(dims_shape)


def wave_numbers(dims, full_x, full_y, full_z):
    offsets = (lax.axis_index("gy") * dims[1], jnp.int32(0), lax.axis_index("gx") * dims[3])
    freq_x = frequencies(dims[1], offsets[0], full_x, 0)
    freq_y = frequencies(dims[2], offsets[1], full_y, 1)
    freq_z = frequencies(dims[3], offsets[2], full_z, 2)
    zero = ((freq_x == 0.0) & (freq_y == 0.0) & (freq_z == 0.0)).astype(jnp.float32)
    return (freq_x, freq_y, freq_z, zero)


def laplace_padded(padded):
    centre = padded[:, 1:-1, 1:-1, :]
    total = -6.0 * centre
    total = total + padded[:, 2:, 1:-1, :] + padded[:, :-2, 1:-1, :]
    total = total + padded[:, 1:-1, 2:, :] + padded[:, 1:-1, :-2, :]
    total = total + jnp.roll(centre, 1, 3) + jnp.roll(centre, -1, 3)
    return total


def shards(labels, seed_noise, conc, curvature, quartic, wells, lame, eigen):
    phase = phases_from(labels, seed_noise)
    part, chem = partition(phase, conc, curvature, quartic, wells)
    stacked = jnp.concatenate([phase, chem[None]], axis=0)
    padded = padded_2(stacked, (("gx", 1), ("gy", 2)), 1)
    lam_field = jnp.sum(phase * column(lame[0]), axis=0)
    shear_field = jnp.sum(phase * column(lame[1]), axis=0)
    eigen_field = jnp.einsum("ap,axyz->pxyz", eigen, phase, precision=lax.Precision.HIGHEST)
    lam0 = 0.5 * (jnp.max(lame[0]) + jnp.min(lame[0]))
    mu0 = 0.5 * (jnp.max(lame[1]) + jnp.min(lame[1]))
    full_x = labels.shape[0] * lax.axis_size("gx")
    full_y = labels.shape[1] * lax.axis_size("gy")
    full_z = labels.shape[2]
    strain = jnp.zeros((6,) + labels.shape, jnp.float32)
    for _ in range(ITERS):
        stress = stress_of(strain, eigen_field, lam_field, shear_field)
        real, imag = spectrum(stress)
        freq_x, freq_y, freq_z, zero = wave_numbers(real.shape, full_x, full_y, full_z)
        upd_real = green(real, freq_x, freq_y, freq_z, zero, lam0, mu0)
        upd_imag = green(imag, freq_x, freq_y, freq_z, zero, lam0, mu0)
        packed = (upd_real[0::2] - upd_imag[1::2], upd_imag[0::2] + upd_real[1::2])
        back_real, back_imag = recover(packed)
        change = jnp.stack([back_real, back_imag], axis=1).reshape(strain.shape)
        strain = strain - change
    stress = stress_of(strain, eigen_field, lam_field, shear_field)
    deviate = part - column(wells)
    energy = 0.5 * column(curvature) * deviate**2 + 0.25 * column(quartic) * deviate**4
    chemical = energy - chem[None] * part
    elastic = strain - eigen_field
    trace = elastic[0] + elastic[1] + elastic[2]
    squares = (
        elastic[0] ** 2
        + elastic[1] ** 2
        + elastic[2] ** 2
        + 2.0 * (elastic[3] ** 2 + elastic[4] ** 2 + elastic[5] ** 2)
    )
    weight = jnp.array([1.0, 1.0, 1.0, 2.0, 2.0, 2.0], jnp.float32)
    coupling = jnp.einsum(
        "ap,pxyz->axyz", eigen * weight[None], stress, precision=lax.Precision.HIGHEST
    )
    stored = (
        0.5 * (column(lame[0]) * trace[None] ** 2 + 2.0 * column(lame[1]) * squares[None])
        - coupling
    )
    total_sq = jnp.sum(phase * phase, axis=0)
    barrier = 2.0 * phase * (total_sq[None] - phase * phase)
    laplacian = laplace_padded(padded)
    force = chemical + stored + barrier - laplacian[:4]
    phase_next = phase - step_phase * (force - jnp.mean(force, axis=0, keepdims=True))
    conc_next = conc + step_conc * laplacian[4]
    return (phase_next, conc_next, stress)


def solution(mesh):
    in_specs = (
        P("gx", "gy", None),
        P(None, "gx", "gy", None),
        P("gx", "gy", None),
        P(),
        P(),
        P(),
        P(),
        P(),
    )
    out_specs = (P(None, "gx", "gy", None), P("gx", "gy", None), P(None, "gx", "gy", None))
    return jax.shard_map(shards, mesh=mesh, in_specs=in_specs, out_specs=out_specs, check_vma=False)
```

profile of v0, /device:TPU:7, one launch (start us, length us, event | category | flops | bytes accessed | tf_op | source)
XLA Modules:
  0.0 446.8 jit_solution(10765165447574417818)
XLA Ops:
  10.7 2.6 multiply_reduce_fusion.5
  13.4 2.9 multiply_reduce_fusion.4
  16.4 3.4 multiply_reduce_fusion.3
  19.9 4.4 multiply_reduce_fusion.2
  27.7 2.9 reshape.488
  30.6 7.9 %all-to-all-start = ((f32[16,1,6144]{2,1,0:T(1,128)}), f32[16,1,6144]{2,1,0:T(1,128)}, u32[]{:S(2)}, u32[]{:S(2)}) async-start(f32[16,1,6144]{2,1,0:T(1,128)} %reshape.488), calls=%async_computation | async-start | bytes 786432 | tf_op jit(solution)/shard_map/all_to_all | solution.py:136
  62.0 10.3 %all-to-all-start.1 = ((f32[16,1,6144]{2,1,0:T(1,128)}), f32[16,1,6144]{2,1,0:T(1,128)}, u32[]{:S(2)}, u32[]{:S(2)}) async-start(f32[16,1,6144]{2,1,0:T(1,128)} %reshape.490), calls=%async_computation.1 | async-start | bytes 786432 | tf_op jit(solution)/shard_map/all_to_all | solution.py:137
  75.0 3.3 reduce.5
  84.6 3.3 reduce.4
  98.3 7.6 %all-to-all-start.2 = ((f32[8,1,12288]{2,1,0:T(1,128)}), f32[8,1,12288]{2,1,0:T(1,128)}, u32[]{:S(2)}, u32[]{:S(2)}) async-start(f32[8,1,12288]{2,1,0:T(1,128)} %reshape.492), calls=%async_computation.2 | async-start | bytes 786432 | tf_op jit(solution)/shard_map/all_to_all | solution.py:144
  113.0 5.5 %all-to-all-start.3 = ((f32[8,1,12288]{2,1,0:T(1,128)}), f32[8,1,12288]{2,1,0:T(1,128)}, u32[]{:S(2)}, u32[]{:S(2)}) async-start(f32[8,1,12288]{2,1,0:T(1,128)} %reshape.494), calls=%async_computation.3 | async-start | bytes 786432 | tf_op jit(solution)/shard_map/all_to_all | solution.py:145
  119.1 3.3 reduce.7
  130.2 3.3 reduce.6
  140.6 2.7 fusion.13
  155.4 5.2 %all-to-all-start.4 = ((f32[8,1,6144]{2,1,0:T(1,128)}), f32[8,1,6144]{2,1,0:T(1,128)}, u32[]{:S(2)}, u32[]{:S(2)}) async-start(f32[8,1,6144]{2,1,0:T(1,128)} %reshape.498), calls=%async_computation.4 | async-start | bytes 393216 | tf_op jit(solution)/shard_map/all_to_all | solution.py:157
  160.6 3.1 fusion.35
  167.2 5.4 %all-to-all-start.5 = ((f32[8,1,6144]{2,1,0:T(1,128)}), f32[8,1,6144]{2,1,0:T(1,128)}, u32[]{:S(2)}, u32[]{:S(2)}) async-start(f32[8,1,6144]{2,1,0:T(1,128)} %reshape.496), calls=%async_computation.5 | async-start | bytes 393216 | tf_op jit(solution)/shard_map/all_to_all | solution.py:158
  172.6 2.7 reduce.9
  181.4 2.7 reduce.8
  192.6 9.8 %all-to-all-start.6 = ((f32[16,1,3072]{2,1,0:T(1,128)}), f32[16,1,3072]{2,1,0:T(1,128)S(1)}, u32[]{:S(2)}, u32[]{:S(2)}) async-start(f32[16,1,3072]{2,1,0:T(1,128)} %reshape.502), calls=%async_computation.6 | async-start | bytes 393216 | tf_op jit(solution)/shard_map/all_to_all | solution.py:165
  204.5 3.8 all-to-all-done.6
  208.3 7.5 %all-to-all-start.7 = ((f32[16,1,3072]{2,1,0:T(1,128)}), f32[16,1,3072]{2,1,0:T(1,128)}, u32[]{:S(2)}, u32[]{:S(2)}) async-start(f32[16,1,3072]{2,1,0:T(1,128)} %reshape.500), calls=%async_computation.7 | async-start | bytes 393216 | tf_op jit(solution)/shard_map/all_to_all | solution.py:166
  218.4 3.3 all-to-all-done.7
  234.0 2.9 copy.286
  236.9 2.8 reshape.504
  239.8 7.0 %all-to-all-start.8 = ((f32[16,1,6144]{2,1,0:T(1,128)}), f32[16,1,6144]{2,1,0:T(1,128)}, u32[]{:S(2)}, u32[]{:S(2)}) async-start(f32[16,1,6144]{2,1,0:T(1,128)} %reshape.504), calls=%async_computation.8 | async-start | bytes 786432 | tf_op jit(solution)/shard_map/all_to_all | solution.py:136
  250.7 2.9 copy.291
  253.6 2.8 reshape.506
  256.5 7.5 %all-to-all-start.9 = ((f32[16,1,6144]{2,1,0:T(1,128)}), f32[16,1,6144]{2,1,0:T(1,128)S(1)}, u32[]{:S(2)}, u32[]{:S(2)}) async-start(f32[16,1,6144]{2,1,0:T(1,128)} %reshape.506), calls=%async_computation.9 | async-start | bytes 786432 | tf_op jit(solution)/shard_map/all_to_all | solution.py:137
  264.0 4.7 %fusion.48 = f32[5,8,32,64]{3,0,2,1:T(8,128)} fusion(f32[1,8,32,64]{3,0,2,1:T(1,128)S(1)} %bitcast.454, f32[4,8,32,64]{3,0,2,1:T(4,128)S(1)} %get-tuple-element.69, f32[5,8,1,64]{3,0,2,1:T(8,128)} %collective-permute-done.3, f32[5,1,32,64]{3,0,2,1:T(8,128)} %collective-permute-done, f32[5,1,32,64]{3,0,2,1:T(8,128)} %collective-permute-done.1, ...), kind=kLoop, calls=%fused_computation.97 | loop fusion | flops 2293760 | bytes 1413120 | tf_op jit(solution)/shard_map/add | solution.py:197
  268.7 2.6 reduce.13
  273.0 2.7 copy.447
  281.4 2.7 reshape.507
  284.1 2.7 copy.446
  293.6 3.2 reshape.508
  296.8 5.1 %all-to-all-start.10 = ((f32[8,1,12288]{2,1,0:T(1,128)}), f32[8,1,12288]{2,1,0:T(1,128)}, u32[]{:S(2)}, u32[]{:S(2)}) async-start(f32[8,1,12288]{2,1,0:T(1,128)} %reshape.508), calls=%async_computation.10 | async-start | bytes 786432 | tf_op jit(solution)/shard_map/all_to_all | solution.py:144
  305.0 3.2 reshape.510
  309.1 5.2 %all-to-all-start.11 = ((f32[8,1,12288]{2,1,0:T(1,128)}), f32[8,1,12288]{2,1,0:T(1,128)}, u32[]{:S(2)}, u32[]{:S(2)}) async-start(f32[8,1,12288]{2,1,0:T(1,128)} %reshape.510), calls=%async_computation.11 | async-start | bytes 786432 | tf_op jit(solution)/shard_map/all_to_all | solution.py:145
  316.4 2.6 reduce.15
  329.1 2.6 reduce.14
  343.0 3.0 fusion.11
  356.6 3.3 reshape.514
  359.9 5.2 %all-to-all-start.12 = ((f32[8,1,6144]{2,1,0:T(1,128)}), f32[8,1,6144]{2,1,0:T(1,128)S(1)}, u32[]{:S(2)}, u32[]{:S(2)}) async-start(f32[8,1,6144]{2,1,0:T(1,128)} %reshape.514), calls=%async_computation.12 | async-start | bytes 393216 | tf_op jit(solution)/shard_map/all_to_all | solution.py:157
  368.0 3.3 reshape.512
  371.3 5.4 %all-to-all-start.13 = ((f32[8,1,6144]{2,1,0:T(1,128)}), f32[8,1,6144]{2,1,0:T(1,128)}, u32[]{:S(2)}, u32[]{:S(2)}) async-start(f32[8,1,6144]{2,1,0:T(1,128)} %reshape.512), calls=%async_computation.13 | async-start | bytes 393216 | tf_op jit(solution)/shard_map/all_to_all | solution.py:158
  398.6 9.8 %all-to-all-start.14 = ((f32[16,1,3072]{2,1,0:T(1,128)}), f32[16,1,3072]{2,1,0:T(1,128)}, u32[]{:S(2)}, u32[]{:S(2)}) async-start(f32[16,1,3072]{2,1,0:T(1,128)} %reshape.518), calls=%async_computation.14 | async-start | bytes 393216 | tf_op jit(solution)/shard_map/all_to_all | solution.py:165
  414.4 7.3 %all-to-all-start.15 = ((f32[16,1,3072]{2,1,0:T(1,128)}), f32[16,1,3072]{2,1,0:T(1,128)}, u32[]{:S(2)}, u32[]{:S(2)}) async-start(f32[16,1,3072]{2,1,0:T(1,128)} %reshape.516), calls=%async_computation.15 | async-start | bytes 393216 | tf_op jit(solution)/shard_map/all_to_all | solution.py:166
  442.7 2.7 fusion.505
  (399 shorter events, 231.3 us)
Async XLA Ops:
  0.6 6.8 %copy-start.74 = (f32[4,6]{1,0:T(4,128)S(1)}, f32[4,6]{1,0:T(4,128)}, u32[]{:S(2)}) copy-start(f32[4,6]{1,0:T(4,128)} %param.16) | copy-start | bytes 292
  0.7 44.3 %copy-start.70 = (f32[6]{0:T(128)}, f32[6]{0:T(128)S(1)}, u32[]{:S(2)}) copy-start(f32[6]{0:T(128)S(1)} %compare_convert_fusion) | copy-start | bytes 76
  1.9 18.0 %copy-start.68 = (f32[4]{0:T(128)}, f32[4]{0:T(128)S(1)}, u32[]{:S(2)}) copy-start(f32[4]{0:T(128)S(1)} %get-tuple-element.108) | copy-start | bytes 52
  3.4 16.5 %copy-start.76 = (f32[4]{0:T(128)}, f32[4]{0:T(128)S(1)}, u32[]{:S(2)}) copy-start(f32[4]{0:T(128)S(1)} %get-tuple-element.106) | copy-start | bytes 52
  19.9 4.4 copy-start.13
  27.7 10.8 %copy-start.14 = (f32[8,32,64]{2,1,0:T(8,128)S(1)}, f32[8,32,64]{2,1,0:T(8,128)}, u32[]{:S(2)}) copy-start(f32[8,32,64]{2,1,0:T(8,128)} %copy-done.13) | copy-start | bytes 196612
  27.7 10.8 %copy-start.23 = (f32[8,32,64]{2,1,0:T(8,128)S(1)}, f32[8,32,64]{2,1,0:T(8,128)}, u32[]{:S(2)}) copy-start(f32[8,32,64]{2,1,0:T(8,128)} %get-tuple-element.17) | copy-start | bytes 196612
  27.7 10.8 %copy-start.24 = (f32[8,32,64]{2,1,0:T(8,128)S(1)}, f32[8,32,64]{2,1,0:T(8,128)}, u32[]{:S(2)}) copy-start(f32[8,32,64]{2,1,0:T(8,128)} %get-tuple-element.18) | copy-start | bytes 196612
  27.7 10.8 %copy-start.25 = (f32[8,32,64]{2,1,0:T(8,128)S(1)}, f32[8,32,64]{2,1,0:T(8,128)}, u32[]{:S(2)}) copy-start(f32[8,32,64]{2,1,0:T(8,128)} %get-tuple-element.27) | copy-start | bytes 196612
  30.6 14.3 %copy-start.17 = (f32[8,32,64]{2,1,0:T(8,128)S(1)}, f32[8,32,64]{2,1,0:T(8,128)}, u32[]{:S(2)}) copy-start(f32[8,32,64]{2,1,0:T(8,128)} %copy-done.16) | copy-start | bytes 196612
  30.6 31.4 %all-to-all-start = ((f32[16,1,6144]{2,1,0:T(1,128)}), f32[16,1,6144]{2,1,0:T(1,128)}, u32[]{:S(2)}, u32[]{:S(2)}) async-start(f32[16,1,6144]{2,1,0:T(1,128)} %reshape.488), calls=%async_computation | async-start | bytes 786432 | tf_op jit(solution)/shard_map/all_to_all | solution.py:136
  40.0 224.0 %collective-permute-start = (f32[5,1,32,64]{3,0,2,1:T(8,128)}, f32[5,1,32,64]{3,0,2,1:T(8,128)}, u32[]{:S(2)}, u32[]{:S(2)}) collective-permute-start(f32[5,1,32,64]{3,0,2,1:T(8,128)} %get-tuple-element.84), channel_id=1, source_target_pairs={{8,0},{16,8},{24,16},{32,24},{40,32},{48,40},{56,48},{64,56},{72,6... | collective-permute-start | bytes 122888 | tf_op jit(solution)/shard_map/ppermute | solution.py:25
  40.4 223.7 %collective-permute-start.1 = (f32[5,1,32,64]{3,0,2,1:T(8,128)}, f32[5,1,32,64]{3,0,2,1:T(8,128)}, u32[]{:S(2)}, u32[]{:S(2)}) collective-permute-start(f32[5,1,32,64]{3,0,2,1:T(8,128)} %get-tuple-element.83), channel_id=1, source_target_pairs={{0,8},{8,16},{16,24},{24,32},{32,40},{40,48},{48,56},{56,64},{64,7... | collective-permute-start | bytes 122888 | tf_op jit(solution)/shard_map/ppermute | solution.py:24
  42.4 221.6 %collective-permute-start.2 = (f32[5,8,1,64]{3,0,2,1:T(8,128)}, f32[5,8,1,64]{3,0,2,1:T(8,128)}, u32[]{:S(2)}, u32[]{:S(2)}) collective-permute-start(f32[5,8,1,64]{3,0,2,1:T(8,128)} %get-tuple-element.81), channel_id=1, source_target_pairs={{1,0},{2,1},{3,2},{4,3},{5,4},{6,5},{7,6},{0,7},{9,8},{10,9},{11,1... | collective-permute-start | bytes 30728 | tf_op jit(solution)/shard_map/ppermute | solution.py:25
  42.9 221.1 %collective-permute-start.3 = (f32[5,8,1,64]{3,0,2,1:T(8,128)}, f32[5,8,1,64]{3,0,2,1:T(8,128)}, u32[]{:S(2)}, u32[]{:S(2)}) collective-permute-start(f32[5,8,1,64]{3,0,2,1:T(8,128)} %get-tuple-element.82), channel_id=1, source_target_pairs={{0,1},{1,2},{2,3},{3,4},{4,5},{5,6},{6,7},{7,0},{8,9},{9,10},{10,1... | collective-permute-start | bytes 30728 | tf_op jit(solution)/shard_map/ppermute | solution.py:24
  62.0 22.6 %all-to-all-start.1 = ((f32[16,1,6144]{2,1,0:T(1,128)}), f32[16,1,6144]{2,1,0:T(1,128)}, u32[]{:S(2)}, u32[]{:S(2)}) async-start(f32[16,1,6144]{2,1,0:T(1,128)} %reshape.490), calls=%async_computation.1 | async-start | bytes 786432 | tf_op jit(solution)/shard_map/all_to_all | solution.py:137
  98.3 9.3 %copy-start.4 = (f32[128,6,32,4]{0,3,2,1:T(4,128)S(1)}, f32[128,6,32,4]{0,3,2,1:T(4,128)}, u32[]{:S(2)}) copy-start(f32[128,6,32,4]{0,3,2,1:T(4,128)} %copy-done.3) | copy-start | bytes 1179652
  98.3 14.7 %all-to-all-start.2 = ((f32[8,1,12288]{2,1,0:T(1,128)}), f32[8,1,12288]{2,1,0:T(1,128)}, u32[]{:S(2)}, u32[]{:S(2)}) async-start(f32[8,1,12288]{2,1,0:T(1,128)} %reshape.492), calls=%async_computation.2 | async-start | bytes 786432 | tf_op jit(solution)/shard_map/all_to_all | solution.py:144
  113.0 17.2 %all-to-all-start.3 = ((f32[8,1,12288]{2,1,0:T(1,128)}), f32[8,1,12288]{2,1,0:T(1,128)}, u32[]{:S(2)}, u32[]{:S(2)}) async-start(f32[8,1,12288]{2,1,0:T(1,128)} %reshape.494), calls=%async_computation.3 | async-start | bytes 786432 | tf_op jit(solution)/shard_map/all_to_all | solution.py:145
  138.9 4.4 copy-start.30
  140.5 4.3 copy-start.20
  155.4 11.7 %all-to-all-start.4 = ((f32[8,1,6144]{2,1,0:T(1,128)}), f32[8,1,6144]{2,1,0:T(1,128)}, u32[]{:S(2)}, u32[]{:S(2)}) async-start(f32[8,1,6144]{2,1,0:T(1,128)} %reshape.498), calls=%async_computation.4 | async-start | bytes 393216 | tf_op jit(solution)/shard_map/all_to_all | solution.py:157
  167.2 14.2 %all-to-all-start.5 = ((f32[8,1,6144]{2,1,0:T(1,128)}), f32[8,1,6144]{2,1,0:T(1,128)}, u32[]{:S(2)}, u32[]{:S(2)}) async-start(f32[8,1,6144]{2,1,0:T(1,128)} %reshape.496), calls=%async_computation.5 | async-start | bytes 393216 | tf_op jit(solution)/shard_map/all_to_all | solution.py:158
  189.5 12.9 %copy-start.10 = (f32[128,3,32,4]{0,3,2,1:T(4,128)S(1)}, f32[128,3,32,4]{0,3,2,1:T(4,128)}, u32[]{:S(2)}) copy-start(f32[128,3,32,4]{0,3,2,1:T(4,128)} %copy-done.9) | copy-start | bytes 589828
  192.6 15.7 %all-to-all-start.6 = ((f32[16,1,3072]{2,1,0:T(1,128)}), f32[16,1,3072]{2,1,0:T(1,128)S(1)}, u32[]{:S(2)}, u32[]{:S(2)}) async-start(f32[16,1,3072]{2,1,0:T(1,128)} %reshape.502), calls=%async_computation.6 | async-start | bytes 393216 | tf_op jit(solution)/shard_map/all_to_all | solution.py:165
  208.3 13.4 %all-to-all-start.7 = ((f32[16,1,3072]{2,1,0:T(1,128)}), f32[16,1,3072]{2,1,0:T(1,128)}, u32[]{:S(2)}, u32[]{:S(2)}) async-start(f32[16,1,3072]{2,1,0:T(1,128)} %reshape.500), calls=%async_computation.7 | async-start | bytes 393216 | tf_op jit(solution)/shard_map/all_to_all | solution.py:166
  239.8 16.7 %all-to-all-start.8 = ((f32[16,1,6144]{2,1,0:T(1,128)}), f32[16,1,6144]{2,1,0:T(1,128)}, u32[]{:S(2)}, u32[]{:S(2)}) async-start(f32[16,1,6144]{2,1,0:T(1,128)} %reshape.504), calls=%async_computation.8 | async-start | bytes 786432 | tf_op jit(solution)/shard_map/all_to_all | solution.py:136
  256.5 22.6 %all-to-all-start.9 = ((f32[16,1,6144]{2,1,0:T(1,128)}), f32[16,1,6144]{2,1,0:T(1,128)S(1)}, u32[]{:S(2)}, u32[]{:S(2)}) async-start(f32[16,1,6144]{2,1,0:T(1,128)} %reshape.506), calls=%async_computation.9 | async-start | bytes 786432 | tf_op jit(solution)/shard_map/all_to_all | solution.py:137
  296.8 12.3 %all-to-all-start.10 = ((f32[8,1,12288]{2,1,0:T(1,128)}), f32[8,1,12288]{2,1,0:T(1,128)}, u32[]{:S(2)}, u32[]{:S(2)}) async-start(f32[8,1,12288]{2,1,0:T(1,128)} %reshape.508), calls=%async_computation.10 | async-start | bytes 786432 | tf_op jit(solution)/shard_map/all_to_all | solution.py:144
  309.1 20.1 %all-to-all-start.11 = ((f32[8,1,12288]{2,1,0:T(1,128)}), f32[8,1,12288]{2,1,0:T(1,128)}, u32[]{:S(2)}, u32[]{:S(2)}) async-start(f32[8,1,12288]{2,1,0:T(1,128)} %reshape.510), calls=%async_computation.11 | async-start | bytes 786432 | tf_op jit(solution)/shard_map/all_to_all | solution.py:145
  339.5 6.5 %copy-start.21 = (pred[16,256]{1,0:T(8,128)(4,1)S(1)}, pred[16,256]{1,0:T(8,128)(4,1)}, u32[]{:S(2)}) copy-start(pred[16,256]{1,0:T(8,128)(4,1)} %broadcast_and_fusion) | copy-start | bytes 12292
  339.5 6.5 %copy-start.34 = (f32[256]{0:T(256)S(1)}, f32[256]{0:T(256)}, u32[]{:S(2)}) copy-start(f32[256]{0:T(256)} %copy-done.32) | copy-start | bytes 3076
  339.5 6.5 %copy-start.40 = (f32[4]{0:T(128)S(1)}, f32[4]{0:T(128)}, u32[]{:S(2)}) copy-start(f32[4]{0:T(128)} %get-tuple-element.114) | copy-start | bytes 52
  339.5 6.5 %copy-start.43 = (pred[4]{0:T(512)(128)(4,1)S(1)}, pred[4]{0:T(512)(128)(4,1)}, u32[]{:S(2)}) copy-start(pred[4]{0:T(512)(128)(4,1)} %broadcast_compare_fusion.1) | copy-start | bytes 16
  339.5 6.5 %copy-start.47 = (f32[4]{0:T(128)S(1)}, f32[4]{0:T(128)}, u32[]{:S(2)}) copy-start(f32[4]{0:T(128)} %copy-done.45) | copy-start | bytes 52
  339.5 6.5 %copy-start.51 = (f32[16]{0:T(128)S(1)}, f32[16]{0:T(128)}, u32[]{:S(2)}) copy-start(f32[16]{0:T(128)} %copy-done.49) | copy-start | bytes 196
  339.5 6.5 %copy-start.66 = (f32[16]{0:T(128)S(1)}, f32[16]{0:T(128)}, u32[]{:S(2)}) copy-start(f32[16]{0:T(128)} %get-tuple-element.112) | copy-start | bytes 196
  340.4 5.9 %copy-start.28 = (f32[6,16,4,256]{3,2,1,0:T(4,128)S(1)}, f32[6,16,4,256]{3,2,1,0:T(4,128)}, u32[]{:S(2)}) copy-start(f32[6,16,4,256]{3,2,1,0:T(4,128)} %copy-done.27) | copy-start | bytes 1179652
  342.9 4.8 %copy-start.35 = (f32[256]{0:T(256)S(1)}, f32[256]{0:T(256)}, u32[]{:S(2)}) copy-start(f32[256]{0:T(256)} %copy-done.32) | copy-start | bytes 3076
  342.9 4.8 %copy-start.41 = (f32[4]{0:T(128)S(1)}, f32[4]{0:T(128)}, u32[]{:S(2)}) copy-start(f32[4]{0:T(128)} %get-tuple-element.114) | copy-start | bytes 52
  343.0 4.8 %copy-start.44 = (pred[4]{0:T(512)(128)(4,1)S(1)}, pred[4]{0:T(512)(128)(4,1)}, u32[]{:S(2)}) copy-start(pred[4]{0:T(512)(128)(4,1)} %broadcast_compare_fusion.1) | copy-start | bytes 16
  343.0 4.8 %copy-start.48 = (f32[4]{0:T(128)S(1)}, f32[4]{0:T(128)}, u32[]{:S(2)}) copy-start(f32[4]{0:T(128)} %copy-done.45) | copy-start | bytes 52
  343.0 4.8 %copy-start.52 = (f32[16]{0:T(128)S(1)}, f32[16]{0:T(128)}, u32[]{:S(2)}) copy-start(f32[16]{0:T(128)} %copy-done.49) | copy-start | bytes 196
  343.0 4.8 %copy-start.67 = (f32[16]{0:T(128)S(1)}, f32[16]{0:T(128)}, u32[]{:S(2)}) copy-start(f32[16]{0:T(128)} %get-tuple-element.112) | copy-start | bytes 196
  359.9 11.4 %all-to-all-start.12 = ((f32[8,1,6144]{2,1,0:T(1,128)}), f32[8,1,6144]{2,1,0:T(1,128)S(1)}, u32[]{:S(2)}, u32[]{:S(2)}) async-start(f32[8,1,6144]{2,1,0:T(1,128)} %reshape.514), calls=%async_computation.12 | async-start | bytes 393216 | tf_op jit(solution)/shard_map/all_to_all | solution.py:157
  371.3 13.5 %all-to-all-start.13 = ((f32[8,1,6144]{2,1,0:T(1,128)}), f32[8,1,6144]{2,1,0:T(1,128)}, u32[]{:S(2)}, u32[]{:S(2)}) async-start(f32[8,1,6144]{2,1,0:T(1,128)} %reshape.512), calls=%async_computation.13 | async-start | bytes 393216 | tf_op jit(solution)/shard_map/all_to_all | solution.py:158
  398.6 15.8 %all-to-all-start.14 = ((f32[16,1,3072]{2,1,0:T(1,128)}), f32[16,1,3072]{2,1,0:T(1,128)}, u32[]{:S(2)}, u32[]{:S(2)}) async-start(f32[16,1,3072]{2,1,0:T(1,128)} %reshape.518), calls=%async_computation.14 | async-start | bytes 393216 | tf_op jit(solution)/shard_map/all_to_all | solution.py:165
  414.4 15.6 %all-to-all-start.15 = ((f32[16,1,3072]{2,1,0:T(1,128)}), f32[16,1,3072]{2,1,0:T(1,128)}, u32[]{:S(2)}, u32[]{:S(2)}) async-start(f32[16,1,3072]{2,1,0:T(1,128)} %reshape.516), calls=%async_computation.15 | async-start | bytes 393216 | tf_op jit(solution)/shard_map/all_to_all | solution.py:166
  (55 other events, 107.9 us)
where the time goes:
time: 455 us; the launch traced here: 447 us
  local copies, waits for them, and re-layouts  154 us (34%)
  starting transfers between devices  116 us (25%)
  other arithmetic  87.6 us (19%)
  matrix products  74.1 us (16%)
  waiting for transfers between devices  9.94 us (2%)
  between operations  5.47 us (1%)
    unnamed x199, local copies, waits for them, and re-layouts  68.9 us
    dot_general x32, matrix products, apply_table(): jnp.dot(table, flat, precision=lax.Precision.HIGHEST, preferred_element_t...  57.4 us
    all_to_all x2, starting transfers between devices, recover(): lax.all_to_all(pair[0], 'gx', split_axis=1, concat_axis=3, tiled=True)  19.5 us
    all_to_all x2, starting transfers between devices, spectrum(): lax.all_to_all(imag, 'gx', split_axis=3, concat_axis=1, tiled=True)  17.8 us
    transpose x16, local copies, waits for them, and re-layouts, apply_table(): moved = jnp.moveaxis(data, axis, 0)  15.7 us
    reduce_sum x5, other arithmetic, partition(): jnp.sum(phase * part, axis=0)  15.2 us
    all_to_all x2, starting transfers between devices, spectrum(): lax.all_to_all(real, 'gx', split_axis=3, concat_axis=1, tiled=True)  14.9 us
    all_to_all x2, starting transfers between devices, recover(): lax.all_to_all(pair[1], 'gx', split_axis=1, concat_axis=3, tiled=True)  14.8 us
  transfers between devices with their start and end apart: 20, of which 5 were waited for; matrix products, arithmetic and copies ran while one was open for 45% of the time, Pallas kernels for 0%

commit v1 on v0

v1 whole, which is shorter than its diff:
```python
import numpy as np

import jax
import jax.numpy as jnp
from jax import lax
from jax.experimental import pallas as pl
from jax.experimental.pallas import tpu as pltpu
from jax.sharding import PartitionSpec as P

NEWTON = 5
STEP_PHASE = 0.06
STEP_CONC = 0.005

F32 = jnp.float32
BF16 = jnp.bfloat16

EVEN = (0, 1, 2, 5)
ODD = (3, 4)
ORDER = EVEN + ODD
BOTH = ("gx", "gy")


def split_np(table):
    high = table.astype(np.float32).astype(BF16)
    low = (table - high.astype(np.float64)).astype(np.float32).astype(BF16)
    return high, low


def z_tables():
    slab = np.arange(64)[:, None]
    z = np.arange(64)[None, :]
    freq = np.where(slab <= 32, slab, slab - 32)
    angle = 2.0 * np.pi * ((freq * z) % 64) / 64.0
    cos, sin = np.cos(angle), np.sin(angle)
    edge = (slab == 0) | (slab == 32)
    first = slab < 32
    even = np.where(edge | first, cos, sin)
    odd = np.where(edge | ~first, cos, sin)
    weight = np.where(edge, 1.0, 2.0) / 64.0

    def double(t):
        return np.kron(np.eye(2), t)

    return double(even), double(odd), double(even * weight), double(odd * weight)


def x_tables():
    order = np.array([8 * g + 4 * par + p for par in range(2) for p in range(4) for g in range(16)])
    k = np.arange(64)[:, None]
    angle = 2.0 * np.pi * ((k * order[None, :]) % 128) / 128.0
    real = np.cos(angle)
    imag = -np.sin(angle)
    imag[0] = np.where(order % 2 == 0, 1.0, -1.0)
    forward = np.concatenate([real, imag], axis=0)
    weight = np.where(np.arange(128) % 64 == 0, 1.0, 2.0) / (128.0 * 256.0)
    inverse = (forward * weight[:, None]).T
    return forward, inverse


def y_table():
    y = np.arange(256)
    angle = 2.0 * np.pi * ((y[:, None] * y[None, :]) % 256) / 256.0
    return np.concatenate([np.cos(angle), np.sin(angle)], axis=1)


def split(value):
    high = value.astype(BF16)
    low = (value - high.astype(F32)).astype(BF16)
    return high, low


def dot(a, b, dims=((1,), (0,))):
    return lax.dot_general(a, b, (dims, ((), ())), preferred_element_type=F32)


def dense(low, high):
    return jnp.concatenate([low, high], axis=-1)


def material(phase, lame, eigen):
    lam = sum(phase[a] * lame[0, a] for a in range(4))
    shear2 = sum(phase[a] * (2.0 * lame[1, a]) for a in range(4))
    eig = [sum(phase[a] * eigen[a, p] for a in range(4)) for p in range(6)]
    return lam, shear2, eig


def stress_from(elastic, lam, shear2):
    trace = lam * (elastic[0] + elastic[1] + elastic[2])
    return [shear2 * elastic[p] + trace if p < 3 else shear2 * elastic[p] for p in range(6)]


def put_split(values, row, size, high_ref, low_ref):
    for i, p in enumerate(ORDER):
        high, low = split(values[p])
        high_ref[pl.ds(i * 128 + row, size), :] = high
        low_ref[pl.ds(i * 128 + row, size), :] = low


NT = ((1,), (1,))


def z_forward(tab_ref, high_ref, low_ref, send_ref):
    for which, (start, comps) in enumerate(((0, EVEN), (512, ODD))):
        rows = 128 * len(comps)
        high = high_ref[pl.ds(start, rows), :]
        low = low_ref[pl.ds(start, rows), :]
        t_high, t_low = tab_ref[2 * which], tab_ref[2 * which + 1]
        out = dot(t_high, high, NT) + dot(t_high, low, NT) + dot(t_low, high, NT)
        for i, c in enumerate(comps):
            for par in range(2):
                piece = out[par * 64 : par * 64 + 64, i * 128 : i * 128 + 128]
                for r in range(2):
                    send_ref[pl.ds(r * 768 + c * 2 + par, 64, stride=12), :] = piece


def z_inverse(tab_ref, recv_ref, c):
    r, k = divmod(c, 3)
    pieces = [recv_ref[pl.ds(r * 384 + k * 2 + par, 64, stride=6), :] for par in range(2)]
    data = jnp.concatenate(pieces, axis=0).T
    which = 4 + 2 * (c in ODD)
    t_high, t_low = tab_ref[which], tab_ref[which + 1]
    high, low = split(data)
    return dot(high, t_high) + dot(low, t_high) + dot(high, t_low)


def first_kernel(labels_ref, noise_ref, lame, eigen, tab_ref, phase_ref, send_ref, high_ref, low_ref):
    for p in range(4):
        label = dense(labels_ref[p], labels_ref[p + 4])
        raw = [
            dense(noise_ref[a, p], noise_ref[a, p + 4]) + jnp.where(label == a, 2.0, 0.0).astype(F32)
            for a in range(4)
        ]
        inverse = 1.0 / (raw[0] + raw[1] + raw[2] + raw[3])
        phase = [raw[a] * inverse for a in range(4)]
        for a in range(4):
            phase_ref[a, pl.ds(p * 32, 32), :] = phase[a]
        lam, shear2, eig = material(phase, lame, eigen)
        stress = stress_from([-v for v in eig], lam, shear2)
        put_split(stress, p * 32, 32, high_ref, low_ref)
    z_forward(tab_ref, high_ref, low_ref, send_ref)


def middle_kernel(recv_ref, phase_ref, lame, eigen, tab_ref, strain_ref, send_ref, high_ref, low_ref):
    for c in range(6):
        strain_ref[c] = -z_inverse(tab_ref, recv_ref, c)
    for p in range(4):
        rows = pl.ds(p * 32, 32)
        phase = [phase_ref[a, rows, :] for a in range(4)]
        lam, shear2, eig = material(phase, lame, eigen)
        stress = stress_from([strain_ref[c, rows, :] - eig[c] for c in range(6)], lam, shear2)
        put_split(stress, p * 32, 32, high_ref, low_ref)
    z_forward(tab_ref, high_ref, low_ref, send_ref)


def last_kernel(recv_ref, phase_ref, strain_ref, force_ref, lame, eigen, tab_ref, next_ref, stress_ref, work_ref):
    for c in range(6):
        work_ref[c] = strain_ref[c] - z_inverse(tab_ref, recv_ref, c)
    for p in range(4):
        rows = pl.ds(p * 32, 32)
        phase = [phase_ref[a, rows, :] for a in range(4)]
        lam, shear2, eig = material(phase, lame, eigen)
        elastic = [work_ref[c, rows, :] - eig[c] for c in range(6)]
        stress = stress_from(elastic, lam, shear2)
        for c in range(6):
            stress_ref[c, p] = stress[c][:, :64]
            stress_ref[c, p + 4] = stress[c][:, 64:]
        trace = elastic[0] + elastic[1] + elastic[2]
        trace = 0.5 * trace * trace
        squares = (
            elastic[0] * elastic[0]
            + elastic[1] * elastic[1]
            + elastic[2] * elastic[2]
            + 2.0 * (elastic[3] * elastic[3] + elastic[4] * elastic[4] + elastic[5] * elastic[5])
        )
        force = []
        for a in range(4):
            coupling = sum(stress[c] * (eigen[a, c] * (1.0 if c < 3 else 2.0)) for c in range(6))
            force.append(force_ref[a, rows, :] + lame[0, a] * trace + lame[1, a] * squares - coupling)
        mean = 0.25 * (force[0] + force[1] + force[2] + force[3])
        for a in range(4):
            new = phase[a] - STEP_PHASE * (force[a] - mean)
            next_ref[a, p] = new[:, :64]
            next_ref[a, p + 4] = new[:, 64:]


def swap_blocks(x):
    lane = lax.broadcasted_iota(jnp.int32, x[0].shape, 1)
    wide = lane < 64
    narrow = (lane & 32) == 0
    a = [jnp.where(wide, x[i], pltpu.roll(x[i + 2], 64, 1)) for i in range(2)]
    b = [jnp.where(wide, pltpu.roll(x[i], 64, 1), x[i + 2]) for i in range(2)]
    out = []
    for first, second in (a, b):
        out.append(jnp.where(narrow, first, pltpu.roll(second, 32, 1)))
        out.append(jnp.where(narrow, pltpu.roll(first, 96, 1), second))
    return out


def slab_kernel(recv_ref, lame, xf_ref, xi_ref, y_ref, send_ref, in_ref, high_ref, low_ref, mid_ref):
    device = lax.axis_index("gx") * 8 + lax.axis_index("gy")
    slab = lax.rem(device, 64)
    upper = device >= 64
    omega = jnp.where(slab < 32, slab, 32 - slab).astype(F32) * (1.0 / 64.0)
    lam = [lame[0, a] for a in range(4)]
    mu = [lame[1, a] for a in range(4)]

    def middle(v):
        top = jnp.maximum(jnp.maximum(v[0], v[1]), jnp.maximum(v[2], v[3]))
        least = jnp.minimum(jnp.minimum(v[0], v[1]), jnp.minimum(v[2], v[3]))
        return 0.5 * (top + least)

    lam0, mu0 = middle(lam), middle(mu)

    for c in range(6):
        for par in range(2):
            for gh in range(2):
                pieces = [
                    recv_ref[pl.ds((4 * gh + i) * 12 + c * 2 + par, 16, stride=96), :] for i in range(4)
                ]
                for p, value in enumerate(swap_blocks(pieces)):
                    in_ref[c, pl.ds(par * 64 + p * 16, 16), pl.ds(gh * 128, 128)] = value
    xf_high, xf_low = xf_ref[0], xf_ref[1]
    for c in range(6):
        high, low = split(in_ref[c])
        out = dot(xf_high, high) + dot(xf_high, low) + dot(xf_low, high)
        high, low = split(out)
        high_ref[pl.ds(c * 128, 128), :] = high
        low_ref[pl.ds(c * 128, 128), :] = low
    y_high, y_low = y_ref[0], y_ref[1]
    mid_ref[...] = dot(high_ref[...], y_high) + dot(low_ref[...], y_high) + dot(high_ref[...], y_low)
    lane = lax.broadcasted_iota(jnp.int32, (8, 256), 1)
    index = jnp.where(lane >= 128, lane - 256, lane)
    wy = jnp.where(lane == 128, 0, index).astype(F32) * (1.0 / 256.0)
    row = lax.broadcasted_iota(jnp.int32, (8, 256), 0)
    half_mu = jnp.full((8, 256), 2.0 * mu0, F32)
    ratio = (lam0 + mu0) / jnp.full((8, 256), mu0 * (lam0 + 2.0 * mu0), F32)
    for tile in range(8):
        wx = (row + tile * 8).astype(F32) * (1.0 / 128.0)
        q = wx * wx + wy * wy + omega * omega
        q = jnp.where(q == 0.0, 1.0, q)
        first = 1.0 / (half_mu * q)
        second = ratio / (q * q)
        re, im = [], []
        for c in range(6):
            r_rows = pl.ds(c * 128 + tile * 8, 8)
            i_rows = pl.ds(c * 128 + 64 + tile * 8, 8)
            re.append(mid_ref[r_rows, :256] + mid_ref[i_rows, 256:])
            im.append(mid_ref[i_rows, :256] - mid_ref[r_rows, 256:])
        xx, yy, zz, yz, xz, xy = range(6)
        vx = (re[xx] * wx + re[xy] * wy + omega * im[xz], im[xx] * wx + im[xy] * wy - omega * re[xz])
        vy = (re[xy] * wx + re[yy] * wy + omega * im[yz], im[xy] * wx + im[yy] * wy - omega * re[yz])
        vz = (re[xz] * wx + re[yz] * wy - omega * im[zz], im[xz] * wx + im[yz] * wy + omega * re[zz])
        inner = (wx * vx[0] + wy * vy[0] + omega * vz[1], wx * vx[1] + wy * vy[1] - omega * vz[0])
        out = []
        for part in range(2):
            s = inner[part] * second
            fx, fy = vx[part] * first, vy[part] * first
            out_xx = wx * (2.0 * fx - wx * s)
            out_yy = wy * (2.0 * fy - wy * s)
            out_xy = wx * fy + wy * fx - wx * wy * s
            turned = vz[1] if part == 0 else -vz[0]
            out_zz = omega * (2.0 * turned * first - omega * s)
            sign = -1.0 if part == 0 else 1.0
            other = 1 - part
            s_other = inner[other] * second
            fz = vz[part] * first
            out_xz = wx * fz + sign * omega * (vx[other] * first - wx * s_other)
            out_yz = wy * fz + sign * omega * (vy[other] * first - wy * s_other)
            out.append((out_xx, out_yy, out_zz, out_yz, out_xz, out_xy))
        for k in range(3):
            for part in range(2):
                value = jnp.where(upper, out[part][3 + k], out[part][k])
                high, low = split(value)
                at = pl.ds(k * 128 + part * 64 + tile * 8, 8)
                high_ref[at, :] = high
                low_ref[at, :] = low
    high, low = high_ref[pl.ds(0, 384), :], low_ref[pl.ds(0, 384), :]
    mid_ref[pl.ds(0, 384), :] = dot(high, y_high) + dot(low, y_high) + dot(high, y_low)
    xi_high, xi_low = xi_ref[0], xi_ref[1]
    for k in range(3):
        r_rows, i_rows = pl.ds(k * 128, 64), pl.ds(k * 128 + 64, 64)
        real = mid_ref[r_rows, :256] - mid_ref[i_rows, 256:]
        imag = mid_ref[i_rows, :256] + mid_ref[r_rows, 256:]
        high, low = split(jnp.concatenate([real, imag], axis=0))
        out = dot(xi_high, high) + dot(xi_high, low) + dot(xi_low, high)
        for par in range(2):
            for gh in range(2):
                lanes = slice(gh * 128, gh * 128 + 128)
                pieces = [out[par * 64 + p * 16 : par * 64 + p * 16 + 16, lanes] for p in range(4)]
                for i, value in enumerate(swap_blocks(pieces)):
                    send_ref[pl.ds((4 * gh + i) * 6 + k * 2 + par, 16, stride=48), :] = value


def newton_kernel(conc_ref, phase_ref, curvature, quartic, wells, chem_ref, chemical_ref):
    for p in range(4):
        rows = pl.ds(p * 32, 32)
        conc = dense(conc_ref[p], conc_ref[p + 4])
        phase = [phase_ref[a, rows, :] for a in range(4)]
        part = [conc] * 4
        chem = jnp.zeros_like(conc)
        for a in range(4):
            dev = conc - wells[a]
            chem = chem + phase[a] * (dev * (curvature[a] + quartic[a] * dev * dev))
        for _ in range(NEWTON):
            top = conc
            bottom = jnp.zeros_like(conc)
            slope, recip = [], []
            for a in range(4):
                dev = part[a] - wells[a]
                square = quartic[a] * dev * dev
                g = dev * (curvature[a] + square) - chem
                d = 1.0 / (curvature[a] + 3.0 * square)
                slope.append(g)
                recip.append(d)
                top = top + phase[a] * (g * d - part[a])
                bottom = bottom + phase[a] * d
            shift = top / bottom
            part = [part[a] + (shift - slope[a]) * recip[a] for a in range(4)]
            chem = chem + shift
        chem_ref[0, p] = chem[:, :64]
        chem_ref[0, p + 4] = chem[:, 64:]
        total = sum(phase[a] * phase[a] for a in range(4))
        for a in range(4):
            dev = part[a] - wells[a]
            square = dev * dev
            energy = square * (0.5 * curvature[a] + 0.25 * quartic[a] * square)
            chemical_ref[a, rows, :] = energy - chem * part[a] + 2.0 * phase[a] * (total - phase[a] * phase[a])


def faces_kernel(phase_ref, chem_ref, xlow_ref, xhigh_ref, ylow_ref, yhigh_ref):
    for a in range(4):
        xlow_ref[a] = phase_ref[a, pl.ds(0, 32), :][:, :64]
        xhigh_ref[a] = phase_ref[a, pl.ds(96, 32), :][:, 64:]
        for p in range(4):
            first = phase_ref[a, pl.ds(p * 32, 8), :][0:1]
            last = phase_ref[a, pl.ds(p * 32 + 24, 8), :][7:8]
            ylow_ref[a, pl.ds(p, 1), :] = first[:, :64]
            ylow_ref[a, pl.ds(p + 4, 1), :] = first[:, 64:]
            yhigh_ref[a, pl.ds(p, 1), :] = last[:, :64]
            yhigh_ref[a, pl.ds(p + 4, 1), :] = last[:, 64:]
    xlow_ref[4] = chem_ref[0, 0]
    xhigh_ref[4] = chem_ref[0, 7]
    for x in range(8):
        ylow_ref[4, pl.ds(x, 1), :] = chem_ref[0, x, pl.ds(0, 1), :]
        yhigh_ref[4, pl.ds(x, 1), :] = chem_ref[0, x, pl.ds(31, 1), :]


def laplace_kernel(
    phase_ref, chem_ref, chemical_ref, conc_ref, xlow_ref, xhigh_ref, ylow_ref, yhigh_ref, force_ref, conc_out_ref
):
    lane = lax.broadcasted_iota(jnp.int32, (32, 128), 1)
    row = lax.broadcasted_iota(jnp.int32, (32, 128), 0)
    first_z = (lane & 63) == 0
    last_z = (lane & 63) == 63
    low_half = lane < 64
    for f in range(5):
        if f < 4:
            block = [phase_ref[f, pl.ds(p * 32, 32), :] for p in range(4)]
        else:
            block = [dense(chem_ref[0, p], chem_ref[0, p + 4]) for p in range(4)]
        before = xlow_ref[f]
        after = xhigh_ref[f]
        before = dense(before, before)
        after = dense(after, after)
        for p in range(4):
            here = block[p]
            total = -6.0 * here
            if p > 0:
                total = total + block[p - 1]
            else:
                total = total + jnp.where(low_half, before, pltpu.roll(block[3], 64, 1))
            if p < 3:
                total = total + block[p + 1]
            else:
                total = total + jnp.where(low_half, pltpu.roll(block[0], 64, 1), after)
            y_before = dense(ylow_ref[f, pl.ds(p, 1), :], ylow_ref[f, pl.ds(p + 4, 1), :])
            y_after = dense(yhigh_ref[f, pl.ds(p, 1), :], yhigh_ref[f, pl.ds(p + 4, 1), :])
            total = total + jnp.where(row == 0, y_before, pltpu.roll(here, 1, 0))
            total = total + jnp.where(row == 31, y_after, pltpu.roll(here, 31, 0))
            total = total + jnp.where(first_z, pltpu.roll(here, 65, 1), pltpu.roll(here, 1, 1))
            total = total + jnp.where(last_z, pltpu.roll(here, 63, 1), pltpu.roll(here, 127, 1))
            if f < 4:
                rows = pl.ds(p * 32, 32)
                force_ref[f, rows, :] = chemical_ref[f, rows, :] - total
            else:
                conc_out_ref[p] = conc_ref[p] + STEP_CONC * total[:, :64]
                conc_out_ref[p + 4] = conc_ref[p + 4] + STEP_CONC * total[:, 64:]


VMEM = pl.BlockSpec(memory_space=pltpu.VMEM)
SMEM = pl.BlockSpec(memory_space=pltpu.SMEM)
LIMIT = 12 * 1024 * 1024


def call(kernel, args, out, scratch=(), scalars=(), cost=4e6, name=None):
    specs = [SMEM if i in scalars else VMEM for i in range(len(args))]
    shapes = [jax.ShapeDtypeStruct(s, F32) for s in out]
    return pl.pallas_call(
        kernel,
        out_shape=shapes,
        in_specs=specs,
        out_specs=[VMEM] * len(out),
        scratch_shapes=list(scratch),
        compiler_params=pltpu.CompilerParams(vmem_limit_bytes=LIMIT),
        cost_estimate=pl.CostEstimate(flops=int(cost), bytes_accessed=int(cost), transcendentals=0),
        name=name,
    )(*args)


def exchange(x, rows):
    y = lax.all_to_all(x.reshape(128, 1, rows * 128), BOTH, 0, 0, tiled=True)
    return y.reshape(128 * rows, 128)


def shards(labels, seed_noise, conc, curvature, quartic, wells, lame, eigen):
    tables = [half for t in z_tables() for half in split_np(t)]
    z_tab = jnp.asarray(np.stack(tables))
    x_forward, x_inverse = x_tables()
    xf = jnp.asarray(np.stack(split_np(x_forward)))
    xi = jnp.asarray(np.stack(split_np(x_inverse)))
    yt = jnp.asarray(np.stack(split_np(y_table())))

    halves = [pltpu.VMEM((768, 128), BF16), pltpu.VMEM((768, 128), BF16)]
    plane_scratch = [
        pltpu.VMEM((6, 128, 256), F32),
        pltpu.VMEM((768, 256), BF16),
        pltpu.VMEM((768, 256), BF16),
        pltpu.VMEM((768, 512), F32),
    ]

    def plane(recv):
        (back,) = call(
            slab_kernel, (recv, lame, xf, xi, yt), [(768, 128)], plane_scratch, scalars=(1,), name="slab"
        )
        return back

    phase, send = call(
        first_kernel,
        (labels, seed_noise, lame, eigen, z_tab),
        [(4, 128, 128), (1536, 128)],
        halves,
        scalars=(2, 3),
        name="first",
    )
    recv = exchange(send, 12)

    chem, chemical = call(
        newton_kernel,
        (conc, phase, curvature, quartic, wells),
        [(1, 8, 32, 64), (4, 128, 128)],
        scalars=(2, 3, 4),
        cost=2e7,
        name="newton",
    )
    xlow, xhigh, ylow, yhigh = call(
        faces_kernel, (phase, chem), [(5, 32, 64), (5, 32, 64), (5, 8, 64), (5, 8, 64)], name="faces"
    )

    def shift(value, axis, step):
        count = lax.axis_size(axis)
        return lax.ppermute(value, axis, [(i, (i + step) % count) for i in range(count)])

    from_low = shift(xhigh, "gx", 1)
    from_high = shift(xlow, "gx", -1)
    y_from_low = shift(yhigh, "gy", 1)
    y_from_high = shift(ylow, "gy", -1)
    force, conc_next = call(
        laplace_kernel,
        (phase, chem, chemical, conc, from_low, from_high, y_from_low, y_from_high),
        [(4, 128, 128), (8, 32, 64)],
        name="laplace",
    )

    back = exchange(plane(recv), 6)
    strain, send = call(
        middle_kernel,
        (back, phase, lame, eigen, z_tab),
        [(6, 128, 128), (1536, 128)],
        halves,
        scalars=(2, 3),
        name="middle",
    )
    back = exchange(plane(exchange(send, 12)), 6)
    phase_next, stress = call(
        last_kernel,
        (back, phase, strain, force, lame, eigen, z_tab),
        [(4, 8, 32, 64), (6, 8, 32, 64)],
        [pltpu.VMEM((6, 128, 128), F32)],
        scalars=(4, 5),
        name="last",
    )
    return (phase_next, conc_next, stress)


def solution(mesh):
    in_specs = (
        P("gx", "gy", None),
        P(None, "gx", "gy", None),
        P("gx", "gy", None),
        P(),
        P(),
        P(),
        P(),
        P(),
    )
    out_specs = (P(None, "gx", "gy", None), P("gx", "gy", None), P(None, "gx", "gy", None))
    return jax.shard_map(shards, mesh=mesh, in_specs=in_specs, out_specs=out_specs, check_vma=False)
```

time: 455 us -> 104 us (0.23)
  the two profiles are of different devices: /device:TPU:7 before, /device:TPU:0 now
where the time goes in v1:
time: 104 us
  blocking collectives  64.6 us (62%)
  Pallas kernels  16.4 us (16%)
  starting transfers between devices  14.3 us (14%)
  local copies, waits for them, and re-layouts  5.64 us (5%)
  waiting for transfers between devices  2.25 us (2%)
    all_to_all x3, blocking collectives, exchange(): y = lax.all_to_all(x.reshape(128, 1, rows * 128), BOTH, 0, 0, tiled=True)  64.6 us
    pallas_call x8, Pallas kernels, call(): pl.pallas_call(kernel, out_shape=shapes, in_specs=specs, out_specs=[VMEM]...  16.4 us
    ppermute x4, starting transfers between devices, shift(): lax.ppermute(value, axis, [(i, (i + step) % count) for i in range(count)])  9.56 us
    unnamed x30, local copies, waits for them, and re-layouts  5.64 us
    all_to_all x1, starting transfers between devices, exchange(): y = lax.all_to_all(x.reshape(128, 1, rows * 128), BOTH, 0, 0, tiled=True)  4.78 us
    ppermute x4, waiting for transfers between devices, shift(): lax.ppermute(value, axis, [(i, (i + step) % count) for i in range(count)])  2.25 us
  transfers between devices with their start and end apart: 5, of which 1 were waited for; matrix products, arithmetic and copies ran while one was open for 0% of the time, Pallas kernels for 3%

profile of v1, /device:TPU:0, one launch (start us, length us, event | category | flops | bytes accessed | tf_op | source)
XLA Modules:
  0.0 103.9 jit_solution(4744529333033267232)
XLA Ops:
  0.6 0.0 copy-start
  0.6 0.9 copy-done
  1.6 0.0 copy-start.4
  1.6 1.0 %copy-done.4 = f32[4,8,32,64]{3,2,1,0:T(8,128)S(1)} copy-done((f32[4,8,32,64]{3,2,1,0:T(8,128)S(1)}, f32[4,8,32,64]{3,2,1,0:T(8,128)}, u32[]{:S(2)}) %copy-start.4) | copy-done | bytes 262168
  2.6 0.0 copy-start.7
  2.6 0.9 copy-done.7
  3.5 0.0 copy-start.8
  3.5 0.7 copy-done.8
  4.2 0.0 copy-start.10
  4.2 0.7 copy-done.10
  4.9 1.2 %first.1 = (f32[4,128,128]{2,1,0:T(8,128)S(1)}, f32[1536,128]{1,0:T(8,128)S(1)}) custom-call(s32[8,32,64]{2,1,0:T(8,128)S(1)} %copy-done.7, f32[4,8,32,64]{3,2,1,0:T(8,128)S(1)} %copy-done.4, f32[2,4]{1,0:T(2,128)S(1)} %copy-done.8, f32[4,6]{1,0:T(4,128)S(1)} %copy-done.10, bf16[8,128,128]{2,1,0:T(8,128)(2,1)S(1)} %copy-done), custom_call_target="tpu_custom_call" | custom-call | flops 4000000 | bytes 4000000 | tf_op jit(solution)/shard_map/first/pallas_call | solution.py:398
  6.1 0.0 copy-start.2
  6.1 0.0 copy-start.5
  6.1 0.0 copy-start.6
  6.1 27.2 %all_to_all.20 = f32[128,1,1536]{2,1,0:T(1,128)S(1)} all-to-all(f32[128,1,1536]{2,1,0:T(1,128)S(1)} %bitcast.14), channel_id=1, replica_groups=mesh['gx'=16,'gy'=8] {'gx','gy'}, dimensions={0} | all-to-all | bytes 1572864 | tf_op jit(solution)/shard_map/all_to_all | solution.py:411
  33.3 0.0 copy-start.9
  33.3 0.0 copy-done.2
  33.3 0.0 copy-done.5
  33.3 0.0 copy-done.6
  33.3 0.7 copy-done.9
  34.0 3.9 %slab.2 = f32[768,128]{1,0:T(8,128)S(1)} custom-call(f32[1536,128]{1,0:T(8,128)S(1)} %bitcast.9, f32[2,4]{1,0:T(2,128)S(1)} %copy-done.9, bf16[2,128,128]{2,1,0:T(8,128)(2,1)S(1)} %copy-done.6, bf16[2,128,128]{2,1,0:T(8,128)(2,1)S(1)} %copy-done.5, bf16[2,256,512]{2,1,0:T(8,128)(2,1)S(1)} %copy-done.2), custom_call_target="tpu_custom_call" | custom-call | flops 4000000 | bytes 4000000 | tf_op jit(solution)/shard_map/slab/pallas_call | solution.py:398
  37.9 0.0 copy-start.1
  37.9 16.7 %all_to_all.21 = f32[128,1,768]{2,1,0:T(1,128)S(1)} all-to-all(f32[128,1,768]{2,1,0:T(1,128)S(1)} %bitcast.12), channel_id=1, replica_groups=mesh['gx'=16,'gy'=8] {'gx','gy'}, dimensions={0} | all-to-all | bytes 786432 | tf_op jit(solution)/shard_map/all_to_all | solution.py:411
  54.6 0.0 copy-start.11
  54.6 0.0 copy-done.1
  54.6 0.7 copy-done.11
  55.3 1.3 %middle.1 = (f32[6,128,128]{2,1,0:T(8,128)S(1)}, f32[1536,128]{1,0:T(8,128)S(1)}) custom-call(f32[768,128]{1,0:T(8,128)S(1)} %bitcast.10, f32[4,128,128]{2,1,0:T(8,128)S(1)} %get-tuple-element.18.phase_ref, f32[2,4]{1,0:T(2,128)S(1)} %copy-done.9, f32[4,6]{1,0:T(4,128)S(1)} %copy-done.11, bf16[8,128,128]{2,1,0:T(8,128)(2,1)S(1)} %copy-done.1), custom_call_target="tpu_custom_call" | custom-call | flops 4000000 | bytes 4000000 | tf_op jit(solution)/shard_map/middle/pallas_call | solution.py:398
  56.6 20.7 %all_to_all.22 = f32[128,1,1536]{2,1,0:T(1,128)S(1)} all-to-all(f32[128,1,1536]{2,1,0:T(1,128)S(1)} %bitcast.13), channel_id=1, replica_groups=mesh['gx'=16,'gy'=8] {'gx','gy'}, dimensions={0} | all-to-all | bytes 1572864 | tf_op jit(solution)/shard_map/all_to_all | solution.py:411
  77.3 4.7 %slab.3 = f32[768,128]{1,0:T(8,128)} custom-call(f32[1536,128]{1,0:T(8,128)S(1)} %bitcast.8, f32[2,4]{1,0:T(2,128)S(1)} %copy-done.9, bf16[2,128,128]{2,1,0:T(8,128)(2,1)S(1)} %copy-done.6, bf16[2,128,128]{2,1,0:T(8,128)(2,1)S(1)} %copy-done.5, bf16[2,256,512]{2,1,0:T(8,128)(2,1)S(1)} %copy-done.2), custom_call_target="tpu_custom_call" | custom-call | flops 4000000 | bytes 4000000 | tf_op jit(solution)/shard_map/slab/pallas_call | solution.py:398
  81.9 0.0 copy-start.3
  81.9 4.8 %all-to-all-start.3 = ((f32[128,1,768]{2,1,0:T(1,128)}), f32[128,1,768]{2,1,0:T(1,128)S(1)}, u32[]{:S(2)}, u32[]{:S(2)}) async-start(f32[128,1,768]{2,1,0:T(1,128)} %bitcast.6), calls=%async_computation.3 | async-start | bytes 786432 | tf_op jit(solution)/shard_map/all_to_all | solution.py:411
  86.7 0.0 copy-done.3
  86.7 0.0 copy-done.12
  86.7 0.0 copy-done.13
  86.8 0.0 copy-done.14
  86.8 1.6 %newton.1 = (f32[1,8,32,64]{3,2,1,0:T(8,128)S(1)}, f32[4,128,128]{2,1,0:T(8,128)S(1)}) custom-call(f32[8,32,64]{2,1,0:T(8,128)S(1)} %copy-done.3, f32[4,128,128]{2,1,0:T(8,128)S(1)} %get-tuple-element.18.phase_ref, f32[4]{0:T(128)S(1)} %copy-done.12, f32[4]{0:T(128)S(1)} %copy-done.13, f32[4]{0:T(128)S(1)} %copy-done.14), custom_call_target="tpu_custom_call" | custom-call | flops 20000000 | bytes 20000000 | tf_op jit(solution)/shard_map/newton/pallas_call | solution.py:398
  88.3 0.1 faces.1
  88.5 0.1 collective-permute-start
  88.5 5.3 %collective-permute-start.1 = (f32[5,32,64]{2,1,0:T(8,128)S(1)}, f32[5,32,64]{2,1,0:T(8,128)S(1)}, u32[]{:S(2)}, u32[]{:S(2)}) collective-permute-start(f32[5,32,64]{2,1,0:T(8,128)S(1)} %get-tuple-element.24), channel_id=1, source_target_pairs={{0,120},{8,0},{16,8},{24,16},{32,24},{40,32},{48,40},{56,48},{64,5... | collective-permute-start | bytes 122888 | tf_op jit(solution)/shard_map/ppermute | solution.py:461
  93.9 1.0 collective-permute-start.2
  94.8 3.2 %collective-permute-start.3 = (f32[5,8,64]{2,1,0:T(8,128)S(1)}, f32[5,8,64]{2,1,0:T(8,128)S(1)}, u32[]{:S(2)}, u32[]{:S(2)}) collective-permute-start(f32[5,8,64]{2,1,0:T(8,128)S(1)} %get-tuple-element.26), channel_id=1, source_target_pairs={{0,7},{1,0},{2,1},{3,2},{4,3},{5,4},{6,5},{7,6},{8,15},{9,8},{10,9... | collective-permute-start | bytes 30728 | tf_op jit(solution)/shard_map/ppermute | solution.py:461
  98.0 2.2 %collective-permute-done.2.ylow_ref = f32[5,8,64]{2,1,0:T(8,128)S(1)} collective-permute-done((f32[5,8,64]{2,1,0:T(8,128)S(1)}, f32[5,8,64]{2,1,0:T(8,128)S(1)}, u32[]{:S(2)}, u32[]{:S(2)}) %collective-permute-start.2) | collective-permute-done | bytes 10272 | tf_op jit(solution)/shard_map/ppermute | solution.py:461
  100.3 0.0 collective-permute-done.3.yhigh_ref
  100.3 0.0 collective-permute-done.xlow_ref
  100.3 0.0 collective-permute-done.1.xhigh_ref
  100.3 1.4 %laplace.1 = (f32[4,128,128]{2,1,0:T(8,128)S(1)}, f32[8,32,64]{2,1,0:T(8,128)}) custom-call(f32[4,128,128]{2,1,0:T(8,128)S(1)} %get-tuple-element.18.phase_ref, f32[1,8,32,64]{3,2,1,0:T(8,128)S(1)} %get-tuple-element.21.chem_ref, f32[4,128,128]{2,1,0:T(8,128)S(1)} %get-tuple-element.22.chemical_ref, f32[8,32,64]{2,1,0:T(8,128)S(1)} %copy-done.3, ...), custom_call_target="tpu_custom_call" | custom-call | flops 4000000 | bytes 4000000 | tf_op jit(solution)/shard_map/laplace/pallas_call | solution.py:398
  101.7 0.0 all-to-all-done.3
  101.7 2.3 %last.1 = (f32[4,8,32,64]{3,2,1,0:T(8,128)}, f32[6,8,32,64]{3,2,1,0:T(8,128)}) custom-call(f32[768,128]{1,0:T(8,128)S(1)} %bitcast.11, f32[4,128,128]{2,1,0:T(8,128)S(1)} %get-tuple-element.18.phase_ref, f32[6,128,128]{2,1,0:T(8,128)S(1)} %get-tuple-element.20.strain_ref, f32[4,128,128]{2,1,0:T(8,128)S(1)} %get-tuple-element.27.force_ref, ...), custom_call_target="tpu_custom_call" | custom-call | flops 4000000 | bytes 4000000 | tf_op jit(solution)/shard_map/last/pallas_call | solution.py:398
  (3 shorter events, 0.0 us)
Async XLA Ops:
  0.6 1.0 copy-start
  1.6 1.0 %copy-start.4 = (f32[4,8,32,64]{3,2,1,0:T(8,128)S(1)}, f32[4,8,32,64]{3,2,1,0:T(8,128)}, u32[]{:S(2)}) copy-start(f32[4,8,32,64]{3,2,1,0:T(8,128)} %noise_ref.1) | copy-start | bytes 786436
  2.6 0.9 copy-start.7
  3.5 0.7 copy-start.8
  4.2 0.7 copy-start.10
  6.1 27.2 %copy-start.2 = (bf16[2,256,512]{2,1,0:T(8,128)(2,1)S(1)}, bf16[2,256,512]{2,1,0:T(8,128)(2,1)}, u32[]{:S(2)}) copy-start(bf16[2,256,512]{2,1,0:T(8,128)(2,1)} %constant.11.clone.y_ref) | copy-start | bytes 1572868
  6.1 27.2 %copy-start.5 = (bf16[2,128,128]{2,1,0:T(8,128)(2,1)S(1)}, bf16[2,128,128]{2,1,0:T(8,128)(2,1)}, u32[]{:S(2)}) copy-start(bf16[2,128,128]{2,1,0:T(8,128)(2,1)} %constant.10.clone.xi_ref) | copy-start | bytes 196612
  6.1 27.2 %copy-start.6 = (bf16[2,128,128]{2,1,0:T(8,128)(2,1)S(1)}, bf16[2,128,128]{2,1,0:T(8,128)(2,1)}, u32[]{:S(2)}) copy-start(bf16[2,128,128]{2,1,0:T(8,128)(2,1)} %constant.9.clone.xf_ref) | copy-start | bytes 196612
  33.3 0.7 copy-start.9
  37.9 16.7 %copy-start.1 = (bf16[8,128,128]{2,1,0:T(8,128)(2,1)S(1)}, bf16[8,128,128]{2,1,0:T(8,128)(2,1)}, u32[]{:S(2)}) copy-start(bf16[8,128,128]{2,1,0:T(8,128)(2,1)} %constant.8.clone.tab_ref) | copy-start | bytes 786436
  54.6 0.7 copy-start.11
  81.9 4.8 %copy-start.3 = (f32[8,32,64]{2,1,0:T(8,128)S(1)}, f32[8,32,64]{2,1,0:T(8,128)}, u32[]{:S(2)}) copy-start(f32[8,32,64]{2,1,0:T(8,128)} %conc_ref.3) | copy-start | bytes 196612
  81.9 4.8 %copy-start.12 = (f32[4]{0:T(128)S(1)}, f32[4]{0:T(128)}, u32[]{:S(2)}) copy-start(f32[4]{0:T(128)} %curvature.1) | copy-start | bytes 52
  81.9 4.8 %copy-start.13 = (f32[4]{0:T(128)S(1)}, f32[4]{0:T(128)}, u32[]{:S(2)}) copy-start(f32[4]{0:T(128)} %quartic.1) | copy-start | bytes 52
  81.9 4.8 %copy-start.14 = (f32[4]{0:T(128)S(1)}, f32[4]{0:T(128)}, u32[]{:S(2)}) copy-start(f32[4]{0:T(128)} %wells.1) | copy-start | bytes 52
  81.9 19.8 %all-to-all-start.3 = ((f32[128,1,768]{2,1,0:T(1,128)}), f32[128,1,768]{2,1,0:T(1,128)S(1)}, u32[]{:S(2)}, u32[]{:S(2)}) async-start(f32[128,1,768]{2,1,0:T(1,128)} %bitcast.6), calls=%async_computation.3 | async-start | bytes 786432 | tf_op jit(solution)/shard_map/all_to_all | solution.py:411
  88.5 11.8 %collective-permute-start = (f32[5,32,64]{2,1,0:T(8,128)S(1)}, f32[5,32,64]{2,1,0:T(8,128)S(1)}, u32[]{:S(2)}, u32[]{:S(2)}) collective-permute-start(f32[5,32,64]{2,1,0:T(8,128)S(1)} %get-tuple-element.23), channel_id=1, source_target_pairs={{0,8},{8,16},{16,24},{24,32},{32,40},{40,48},{48,56},{56,64},{64,7... | collective-permute-start | bytes 122888 | tf_op jit(solution)/shard_map/ppermute | solution.py:461
  88.5 11.7 %collective-permute-start.1 = (f32[5,32,64]{2,1,0:T(8,128)S(1)}, f32[5,32,64]{2,1,0:T(8,128)S(1)}, u32[]{:S(2)}, u32[]{:S(2)}) collective-permute-start(f32[5,32,64]{2,1,0:T(8,128)S(1)} %get-tuple-element.24), channel_id=1, source_target_pairs={{0,120},{8,0},{16,8},{24,16},{32,24},{40,32},{48,40},{56,48},{64,5... | collective-permute-start | bytes 122888 | tf_op jit(solution)/shard_map/ppermute | solution.py:461
  93.9 6.4 %collective-permute-start.2 = (f32[5,8,64]{2,1,0:T(8,128)S(1)}, f32[5,8,64]{2,1,0:T(8,128)S(1)}, u32[]{:S(2)}, u32[]{:S(2)}) collective-permute-start(f32[5,8,64]{2,1,0:T(8,128)S(1)} %get-tuple-element.25), channel_id=1, source_target_pairs={{0,1},{1,2},{2,3},{3,4},{4,5},{5,6},{6,7},{7,0},{8,9},{9,10},{10,1... | collective-permute-start | bytes 30728 | tf_op jit(solution)/shard_map/ppermute | solution.py:461
  94.8 5.4 %collective-permute-start.3 = (f32[5,8,64]{2,1,0:T(8,128)S(1)}, f32[5,8,64]{2,1,0:T(8,128)S(1)}, u32[]{:S(2)}, u32[]{:S(2)}) collective-permute-start(f32[5,8,64]{2,1,0:T(8,128)S(1)} %get-tuple-element.26), channel_id=1, source_target_pairs={{0,7},{1,0},{2,1},{3,2},{4,3},{5,4},{6,5},{7,6},{8,15},{9,8},{10,9... | collective-permute-start | bytes 30728 | tf_op jit(solution)/shard_map/ppermute | solution.py:461

commit v2 on v1

v2 whole, which is shorter than its diff:
```python
import numpy as np

import jax
import jax.numpy as jnp
from jax import lax
from jax.experimental import pallas as pl
from jax.experimental.pallas import tpu as pltpu
from jax.sharding import PartitionSpec as P

NEWTON = 5
STEP_PHASE = 0.06
STEP_CONC = 0.005

F32 = jnp.float32
BF16 = jnp.bfloat16

EVEN = (0, 1, 2, 5)
ODD = (3, 4)
ORDER = EVEN + ODD
BOTH = ("gx", "gy")


def split_np(table):
    high = table.astype(np.float32).astype(BF16)
    low = (table - high.astype(np.float64)).astype(np.float32).astype(BF16)
    return high, low


def z_tables():
    slab = np.arange(64)[:, None]
    z = np.arange(64)[None, :]
    freq = np.where(slab <= 32, slab, slab - 32)
    angle = 2.0 * np.pi * ((freq * z) % 64) / 64.0
    cos, sin = np.cos(angle), np.sin(angle)
    edge = (slab == 0) | (slab == 32)
    first = slab < 32
    even = np.where(edge | first, cos, sin)
    odd = np.where(edge | ~first, cos, sin)
    weight = np.where(edge, 1.0, 2.0) / 64.0

    def double(t):
        return np.kron(np.eye(2), t)

    return double(even), double(odd), double(even * weight), double(odd * weight)


def x_tables():
    order = np.array([8 * g + 4 * par + p for par in range(2) for p in range(4) for g in range(16)])
    k = np.arange(64)[:, None]
    angle = 2.0 * np.pi * ((k * order[None, :]) % 128) / 128.0
    real = np.cos(angle)
    imag = -np.sin(angle)
    imag[0] = np.where(order % 2 == 0, 1.0, -1.0)
    forward = np.concatenate([real, imag], axis=0)
    weight = np.where(np.arange(128) % 64 == 0, 1.0, 2.0) / (128.0 * 256.0)
    inverse = (forward * weight[:, None]).T
    return forward, inverse


def y_table():
    y = np.arange(256)
    angle = 2.0 * np.pi * ((y[:, None] * y[None, :]) % 256) / 256.0
    return np.concatenate([np.cos(angle), np.sin(angle)], axis=1)


def split(value):
    high = value.astype(BF16)
    low = (value - high.astype(F32)).astype(BF16)
    return high, low


def dot(a, b, dims=((1,), (0,))):
    return lax.dot_general(a, b, (dims, ((), ())), preferred_element_type=F32)


def dense(low, high):
    return jnp.concatenate([low, high], axis=-1)


class Params:
    def __init__(self, ref):
        self.ref = ref

    def row(self, i):
        return self.ref[pl.ds(i, 1), :]

    def lame(self, i, a):
        return self.row(4 * i + a)

    def eigen(self, a, p):
        return self.row(8 + 6 * a + p)


def write_params(lame, eigen, ref):
    def middle(v):
        top = jnp.maximum(jnp.maximum(v[0], v[1]), jnp.maximum(v[2], v[3]))
        least = jnp.minimum(jnp.minimum(v[0], v[1]), jnp.minimum(v[2], v[3]))
        return 0.5 * (top + least)

    values = [lame[i, a] for i in range(2) for a in range(4)]
    values += [eigen[a, p] for a in range(4) for p in range(6)]
    values += [middle(values[0:4]), middle(values[4:8])]
    for i, value in enumerate(values):
        ref[pl.ds(i, 1), :] = jnp.full((1, 128), value, F32)


def material(phase, lame, eigen):
    lam = sum(phase[a] * lame(0, a) for a in range(4))
    shear2 = 2.0 * sum(phase[a] * lame(1, a) for a in range(4))
    eig = [sum(phase[a] * eigen(a, p) for a in range(4)) for p in range(6)]
    return lam, shear2, eig


def stress_from(elastic, lam, shear2):
    trace = lam * (elastic[0] + elastic[1] + elastic[2])
    return [shear2 * elastic[p] + trace if p < 3 else shear2 * elastic[p] for p in range(6)]


def put_split(values, row, size, high_ref, low_ref):
    for i, p in enumerate(ORDER):
        high, low = split(values[p])
        high_ref[pl.ds(i * 128 + row, size), :] = high
        low_ref[pl.ds(i * 128 + row, size), :] = low


NT = ((1,), (1,))


def z_forward(tab_ref, high_ref, low_ref, send_ref):
    for which, (start, comps) in enumerate(((0, EVEN), (512, ODD))):
        rows = 128 * len(comps)
        high = high_ref[pl.ds(start, rows), :]
        low = low_ref[pl.ds(start, rows), :]
        t_high, t_low = tab_ref[2 * which], tab_ref[2 * which + 1]
        out = dot(t_high, high, NT) + dot(t_high, low, NT) + dot(t_low, high, NT)
        for i, c in enumerate(comps):
            r, k = divmod(c, 3)
            for par in range(2):
                for sh in range(8):
                    at = par * 64 + sh * 8
                    piece = out[at : at + 8, i * 128 : i * 128 + 128]
                    send_ref[pl.ds((sh * 16 + r * 8) * 6 + k * 2 + par, 8, stride=6), :] = piece


def z_inverse(tab_ref, recv_ref, c):
    r, k = divmod(c, 3)
    pieces = [
        recv_ref[pl.ds((sh * 16 + r * 8) * 6 + k * 2 + par, 8, stride=6), :] for par in range(2) for sh in range(8)
    ]
    data = jnp.concatenate(pieces, axis=0).T
    which = 4 + 2 * (c in ODD)
    t_high, t_low = tab_ref[which], tab_ref[which + 1]
    high, low = split(data)
    return dot(high, t_high) + dot(low, t_high) + dot(high, t_low)


def first_kernel(
    labels_hbm,
    noise_hbm,
    lame_hbm,
    eigen_hbm,
    tab_hbm,
    phase_ref,
    send_ref,
    par_ref,
    labels_ref,
    noise_ref,
    lame_ref,
    eigen_ref,
    tab_ref,
    high_ref,
    low_ref,
    sem,
):
    copies = [
        pltpu.make_async_copy(source, target, sem.at[i])
        for i, (source, target) in enumerate(
            (
                (lame_hbm, lame_ref),
                (eigen_hbm, eigen_ref),
                (labels_hbm, labels_ref),
                (noise_hbm, noise_ref),
                (tab_hbm, tab_ref),
            )
        )
    ]
    for copy in copies:
        copy.start()
    for copy in copies[:4]:
        copy.wait()
    write_params(lame_ref, eigen_ref, par_ref)

    def lame(i, a):
        return lame_ref[i, a]

    def eigen(a, p):
        return eigen_ref[a, p]

    for p in range(4):
        label = dense(labels_ref[p], labels_ref[p + 4])
        raw = [
            dense(noise_ref[a, p], noise_ref[a, p + 4]) + jnp.where(label == a, 2.0, 0.0).astype(F32)
            for a in range(4)
        ]
        inverse = 1.0 / (raw[0] + raw[1] + raw[2] + raw[3])
        phase = [raw[a] * inverse for a in range(4)]
        for a in range(4):
            phase_ref[a, pl.ds(p * 32, 32), :] = phase[a]
        lam, shear2, eig = material(phase, lame, eigen)
        stress = stress_from([-v for v in eig], lam, shear2)
        put_split(stress, p * 32, 32, high_ref, low_ref)
    copies[4].wait()
    z_forward(tab_ref, high_ref, low_ref, send_ref)


def middle_kernel(recv_ref, phase_ref, par_ref, tab_ref, *refs):
    strain_ref, send_ref, high_ref, low_ref = refs[-4:]
    par = Params(par_ref)
    for c in range(6):
        strain_ref[c] = -z_inverse(tab_ref, recv_ref, c)
    for p in range(4):
        rows = pl.ds(p * 32, 32)
        phase = [phase_ref[a, rows, :] for a in range(4)]
        lam, shear2, eig = material(phase, par.lame, par.eigen)
        stress = stress_from([strain_ref[c, rows, :] - eig[c] for c in range(6)], lam, shear2)
        put_split(stress, p * 32, 32, high_ref, low_ref)
    z_forward(tab_ref, high_ref, low_ref, send_ref)


def last_kernel(
    recv_ref, phase_ref, strain_ref, force_ref, par_ref, tab_ref, next_hbm, stress_hbm, work_ref, next_ref, stress_ref, sem
):
    par = Params(par_ref)
    for c in range(6):
        work_ref[c] = strain_ref[c] - z_inverse(tab_ref, recv_ref, c)
    copies = []
    for p in range(4):
        rows = pl.ds(p * 32, 32)
        phase = [phase_ref[a, rows, :] for a in range(4)]
        lam, shear2, eig = material(phase, par.lame, par.eigen)
        elastic = [work_ref[c, rows, :] - eig[c] for c in range(6)]
        stress = stress_from(elastic, lam, shear2)
        for c in range(6):
            stress_ref[p, 0, c] = stress[c][:, :64]
            stress_ref[p, 1, c] = stress[c][:, 64:]
        trace = elastic[0] + elastic[1] + elastic[2]
        trace = 0.5 * trace * trace
        squares = (
            elastic[0] * elastic[0]
            + elastic[1] * elastic[1]
            + elastic[2] * elastic[2]
            + 2.0 * (elastic[3] * elastic[3] + elastic[4] * elastic[4] + elastic[5] * elastic[5])
        )
        doubled = [stress[c] if c < 3 else 2.0 * stress[c] for c in range(6)]
        force = []
        for a in range(4):
            coupling = sum(doubled[c] * par.eigen(a, c) for c in range(6))
            force.append(force_ref[a, rows, :] + par.lame(0, a) * trace + par.lame(1, a) * squares - coupling)
        mean = 0.25 * (force[0] + force[1] + force[2] + force[3])
        for a in range(4):
            new = phase[a] - STEP_PHASE * (force[a] - mean)
            next_ref[p, 0, a] = new[:, :64]
            next_ref[p, 1, a] = new[:, 64:]
        for half in range(2):
            x = p + 4 * half
            copies.append(pltpu.make_async_copy(stress_ref.at[p, half], stress_hbm.at[:, x], sem.at[2 * x]))
            copies.append(pltpu.make_async_copy(next_ref.at[p, half], next_hbm.at[:, x], sem.at[2 * x + 1]))
        for copy in copies[-4:]:
            copy.start()
    for copy in copies:
        copy.wait()


def swap_blocks(x):
    lane = lax.broadcasted_iota(jnp.int32, x[0].shape, 1)
    wide = lane < 64
    narrow = (lane & 32) == 0
    a = [jnp.where(wide, x[i], pltpu.roll(x[i + 2], 64, 1)) for i in range(2)]
    b = [jnp.where(wide, pltpu.roll(x[i], 64, 1), x[i + 2]) for i in range(2)]
    out = []
    for first, second in (a, b):
        out.append(jnp.where(narrow, first, pltpu.roll(second, 32, 1)))
        out.append(jnp.where(narrow, pltpu.roll(first, 96, 1), second))
    return out


def spectrum_kernel(recv_ref, xf_ref, y_ref, *refs):
    out_ref, high_ref, low_ref, mid_ref = refs[-4:]
    xf_high, xf_low = xf_ref[0], xf_ref[1]
    for k in range(3):
        rows = []
        for par in range(2):
            columns = []
            for gh in range(2):
                pieces = [
                    recv_ref[pl.ds((4 * gh + i) * 6 + k * 2 + par, 16, stride=48), :] for i in range(4)
                ]
                columns.append(swap_blocks(pieces))
            rows += [jnp.concatenate([columns[0][p], columns[1][p]], axis=1) for p in range(4)]
        high, low = split(jnp.concatenate(rows, axis=0))
        out = dot(xf_high, high) + dot(xf_high, low) + dot(xf_low, high)
        high, low = split(out)
        high_ref[pl.ds(k * 128, 128), :] = high
        low_ref[pl.ds(k * 128, 128), :] = low
    y_high, y_low = y_ref[0], y_ref[1]
    mid_ref[...] = dot(high_ref[...], y_high) + dot(low_ref[...], y_high) + dot(high_ref[...], y_low)
    for k in range(3):
        real, imag = pl.ds(k * 128, 64), pl.ds(k * 128 + 64, 64)
        out_ref[real, :] = mid_ref[real, :256] + mid_ref[imag, 256:]
        out_ref[imag, :] = mid_ref[imag, :256] - mid_ref[real, 256:]


def green_tile(re, im, wx, wy, omega, first, second, upper):
    xx, yy, zz, yz, xz, xy = range(6)
    vx = (re[xx] * wx + re[xy] * wy + omega * im[xz], im[xx] * wx + im[xy] * wy - omega * re[xz])
    vy = (re[xy] * wx + re[yy] * wy + omega * im[yz], im[xy] * wx + im[yy] * wy - omega * re[yz])
    vz = (re[xz] * wx + re[yz] * wy - omega * im[zz], im[xz] * wx + im[yz] * wy + omega * re[zz])
    inner = (wx * vx[0] + wy * vy[0] + omega * vz[1], wx * vx[1] + wy * vy[1] - omega * vz[0])
    s = [inner[part] * second for part in range(2)]
    fx = [vx[part] * first for part in range(2)]
    fy = [vy[part] * first for part in range(2)]
    fz = [vz[part] * first for part in range(2)]
    out = []
    for part in range(2):
        other = 1 - part
        if upper:
            sign = -omega if part == 0 else omega
            out.append(
                (
                    wy * fz[part] + sign * (fy[other] - wy * s[other]),
                    wx * fz[part] + sign * (fx[other] - wx * s[other]),
                    wx * (fy[part] - wy * s[part]) + wy * fx[part],
                )
            )
        else:
            turned = fz[1] if part == 0 else -fz[0]
            out.append(
                (
                    wx * (2.0 * fx[part] - wx * s[part]),
                    wy * (2.0 * fy[part] - wy * s[part]),
                    omega * (2.0 * turned - omega * s[part]),
                )
            )
    return out


def green_kernel(own_ref, other_ref, after_ref, par_ref, xi_ref, y_ref, send_ref, high_ref, low_ref, mid_ref):
    del after_ref
    x_index, y_index = lax.axis_index("gx"), lax.axis_index("gy")
    core = lax.rem(x_index, 2)
    slab = lax.div(x_index, 2) * 8 + y_index
    omega = jnp.where(slab < 32, slab, 32 - slab).astype(F32) * (1.0 / 64.0)
    par = Params(par_ref)
    lam0 = jnp.concatenate([par.row(32), par.row(32)], axis=1)
    mu0 = jnp.concatenate([par.row(33), par.row(33)], axis=1)
    half_mu = 0.5 / mu0
    ratio = (lam0 + mu0) / (mu0 * (lam0 + 2.0 * mu0))
    lane = lax.broadcasted_iota(jnp.int32, (8, 256), 1)
    index = jnp.where(lane >= 128, lane - 256, lane)
    wy = jnp.where(lane == 128, 0, index).astype(F32) * (1.0 / 256.0)
    row = lax.broadcasted_iota(jnp.int32, (8, 256), 0)

    def green(upper):
        for tile in range(8):
            wx = (row + tile * 8).astype(F32) * (1.0 / 128.0)
            q = wx * wx + wy * wy + omega * omega
            inverse = 1.0 / jnp.where(q == 0.0, 1.0, q)
            first = half_mu * inverse
            second = ratio * inverse * inverse

            def get(ref, part):
                return [ref[pl.ds(k * 128 + part * 64 + tile * 8, 8), :] for k in range(3)]

            low, high = (other_ref, own_ref) if upper else (own_ref, other_ref)
            re, im = (get(low, part) + get(high, part) for part in range(2))
            out = green_tile(re, im, wx, wy, omega, first, second, upper)
            for part in range(2):
                for k in range(3):
                    high, low = split(out[part][k])
                    at = pl.ds(k * 128 + part * 64 + tile * 8, 8)
                    high_ref[at, :] = high
                    low_ref[at, :] = low

    @pl.when(core == 0)
    def _():
        green(False)

    @pl.when(core == 1)
    def _():
        green(True)

    y_high, y_low = y_ref[0], y_ref[1]
    mid_ref[...] = dot(high_ref[...], y_high) + dot(low_ref[...], y_high) + dot(high_ref[...], y_low)
    xi_high, xi_low = xi_ref[0], xi_ref[1]
    for k in range(3):
        r_rows, i_rows = pl.ds(k * 128, 64), pl.ds(k * 128 + 64, 64)
        real = mid_ref[r_rows, :256] - mid_ref[i_rows, 256:]
        imag = mid_ref[i_rows, :256] + mid_ref[r_rows, 256:]
        high, low = split(jnp.concatenate([real, imag], axis=0))
        out = dot(xi_high, high) + dot(xi_high, low) + dot(xi_low, high)
        for parity in range(2):
            for gh in range(2):
                lanes = slice(gh * 128, gh * 128 + 128)
                pieces = [out[parity * 64 + p * 16 : parity * 64 + p * 16 + 16, lanes] for p in range(4)]
                for i, value in enumerate(swap_blocks(pieces)):
                    send_ref[pl.ds((4 * gh + i) * 6 + k * 2 + parity, 16, stride=48), :] = value


def newton_kernel(
    conc_ref, phase_ref, curvature, quartic, wells, chem_ref, chemical_ref, xlow_ref, xhigh_ref, ylow_ref, yhigh_ref
):
    for p in range(4):
        rows = pl.ds(p * 32, 32)
        conc = dense(conc_ref[p], conc_ref[p + 4])
        phase = [phase_ref[a, rows, :] for a in range(4)]
        part = [conc] * 4
        chem = jnp.zeros_like(conc)
        for a in range(4):
            dev = conc - wells[a]
            chem = chem + phase[a] * (dev * (curvature[a] + quartic[a] * dev * dev))
        for _ in range(NEWTON):
            top = conc
            bottom = jnp.zeros_like(conc)
            slope, recip = [], []
            for a in range(4):
                dev = part[a] - wells[a]
                square = quartic[a] * dev * dev
                g = dev * (curvature[a] + square) - chem
                d = 1.0 / (curvature[a] + 3.0 * square)
                slope.append(g)
                recip.append(d)
                top = top + phase[a] * (g * d - part[a])
                bottom = bottom + phase[a] * d
            shift = top / bottom
            part = [part[a] + (shift - slope[a]) * recip[a] for a in range(4)]
            chem = chem + shift
        chem_ref[rows, :] = chem
        total = sum(phase[a] * phase[a] for a in range(4))
        for a in range(4):
            dev = part[a] - wells[a]
            square = dev * dev
            energy = square * (0.5 * curvature[a] + 0.25 * quartic[a] * square)
            chemical_ref[a, rows, :] = energy - chem * part[a] + 2.0 * phase[a] * (total - phase[a] * phase[a])
    low_half = lax.broadcasted_iota(jnp.int32, (32, 128), 1) < 64

    def field(f, rows):
        return phase_ref[f, rows, :] if f < 4 else chem_ref[rows, :]

    first, last = pl.ds(0, 32), pl.ds(96, 32)
    for j in range(2):
        at = pl.ds(j * 32, 32)
        xlow_ref[at, :] = jnp.where(low_half, field(2 * j, first), pltpu.roll(field(2 * j + 1, first), 64, 1))
        xhigh_ref[at, :] = jnp.where(low_half, pltpu.roll(field(2 * j, last), 64, 1), field(2 * j + 1, last))
    xlow_ref[pl.ds(64, 32), :] = field(4, first)
    xhigh_ref[pl.ds(64, 32), :] = pltpu.roll(field(4, last), 64, 1)
    for f in range(5):
        for p in range(4):
            ylow_ref[pl.ds(f * 4 + p, 1), :] = field(f, pl.ds(p * 32, 1))
            yhigh_ref[pl.ds(f * 4 + p, 1), :] = field(f, pl.ds(p * 32 + 31, 1))
    pad = jnp.zeros((4, 128), F32)
    ylow_ref[pl.ds(20, 4), :] = pad
    yhigh_ref[pl.ds(20, 4), :] = pad


def laplace_kernel(
    phase_ref,
    chem_ref,
    chemical_ref,
    conc_ref,
    xlow_ref,
    xhigh_ref,
    ylow_ref,
    yhigh_ref,
    after_ref,
    force_ref,
    conc_out_ref,
):
    del after_ref
    lane = lax.broadcasted_iota(jnp.int32, (32, 128), 1)
    row = lax.broadcasted_iota(jnp.int32, (32, 128), 0)
    first_z = (lane & 63) == 0
    last_z = (lane & 63) == 63
    low_half = lane < 64
    for f in range(5):
        block = [phase_ref[f, pl.ds(p * 32, 32), :] if f < 4 else chem_ref[pl.ds(p * 32, 32), :] for p in range(4)]
        at = pl.ds(f // 2 * 32, 32)
        before, after = xlow_ref[at, :], xhigh_ref[at, :]
        if f % 2 == 0:
            after = pltpu.roll(after, 64, 1)
        else:
            before = pltpu.roll(before, 64, 1)
        for p in range(4):
            here = block[p]
            total = -6.0 * here
            if p > 0:
                total = total + block[p - 1]
            else:
                total = total + jnp.where(low_half, before, pltpu.roll(block[3], 64, 1))
            if p < 3:
                total = total + block[p + 1]
            else:
                total = total + jnp.where(low_half, pltpu.roll(block[0], 64, 1), after)
            y_before = ylow_ref[pl.ds(f * 4 + p, 1), :]
            y_after = yhigh_ref[pl.ds(f * 4 + p, 1), :]
            total = total + jnp.where(row == 0, y_before, pltpu.roll(here, 1, 0))
            total = total + jnp.where(row == 31, y_after, pltpu.roll(here, 31, 0))
            total = total + jnp.where(first_z, pltpu.roll(here, 65, 1), pltpu.roll(here, 1, 1))
            total = total + jnp.where(last_z, pltpu.roll(here, 63, 1), pltpu.roll(here, 127, 1))
            if f < 4:
                rows = pl.ds(p * 32, 32)
                force_ref[f, rows, :] = chemical_ref[f, rows, :] - total
            else:
                conc_out_ref[p] = conc_ref[p] + STEP_CONC * total[:, :64]
                conc_out_ref[p + 4] = conc_ref[p + 4] + STEP_CONC * total[:, 64:]


VMEM = pl.BlockSpec(memory_space=pltpu.VMEM)
SMEM = pl.BlockSpec(memory_space=pltpu.SMEM)
HBM = pl.BlockSpec(memory_space=pltpu.HBM)
ANY = pl.BlockSpec(memory_space=pl.ANY)
LIMIT = 12 * 1024 * 1024


def call(kernel, args, out, scratch=(), special=None, out_spec=VMEM, cost=4e6, name=None):
    special = special or {}
    specs = [special.get(i, VMEM) for i in range(len(args))]
    shapes = [jax.ShapeDtypeStruct(s, F32) for s in out]
    return pl.pallas_call(
        kernel,
        out_shape=shapes,
        in_specs=specs,
        out_specs=[out_spec] * len(out),
        scratch_shapes=list(scratch),
        compiler_params=pltpu.CompilerParams(vmem_limit_bytes=LIMIT),
        cost_estimate=pl.CostEstimate(flops=int(cost), bytes_accessed=int(cost), transcendentals=0),
        name=name,
    )(*args)


def exchange(x):
    y = lax.all_to_all(x.reshape(128, 1, 768), BOTH, 0, 0, tiled=True)
    return y.reshape(768, 128)


def shards(labels, seed_noise, conc, curvature, quartic, wells, lame, eigen):
    tables = [half for t in z_tables() for half in split_np(t)]
    z_tab = jnp.asarray(np.stack(tables))
    x_forward, x_inverse = x_tables()
    xf = jnp.asarray(np.stack(split_np(x_forward)))
    xi = jnp.asarray(np.stack(split_np(x_inverse)))
    yt = jnp.asarray(np.stack(split_np(y_table())))

    halves = [pltpu.VMEM((768, 128), BF16), pltpu.VMEM((768, 128), BF16)]
    plane_scratch = [
        pltpu.VMEM((384, 256), BF16),
        pltpu.VMEM((384, 256), BF16),
        pltpu.VMEM((384, 512), F32),
    ]

    def shift(value, axis, step):
        count = lax.axis_size(axis)
        return lax.ppermute(value, axis, [(i, (i + step) % count) for i in range(count)])

    def spectrum(recv, after):
        (own,) = call(
            spectrum_kernel,
            (recv, xf, yt, *after),
            [(384, 256)],
            plane_scratch,
            {3 + i: ANY for i in range(len(after))},
            name="spectrum",
        )
        return own, lax.ppermute(own, "gx", [(i, i ^ 1) for i in range(16)])

    def update(own, other, after, par):
        (back,) = call(
            green_kernel,
            (own, other, after, par, xi, yt),
            [(768, 128)],
            plane_scratch,
            {2: ANY},
            name="green",
        )
        return exchange(back)

    def in_hbm(*arrays):
        return tuple(pltpu.with_memory_space_constraint(a, pltpu.HBM) for a in arrays)

    phase, send, par = call(
        first_kernel,
        in_hbm(labels, seed_noise, lame, eigen, z_tab),
        [(4, 128, 128), (768, 128), (40, 128)],
        [
            pltpu.VMEM((8, 32, 64), jnp.int32),
            pltpu.VMEM((4, 8, 32, 64), F32),
            pltpu.SMEM((2, 4), F32),
            pltpu.SMEM((4, 6), F32),
            pltpu.VMEM((8, 128, 128), BF16),
            *halves,
            pltpu.SemaphoreType.DMA((5,)),
        ],
        {i: HBM for i in range(5)},
        name="first",
    )
    recv = exchange(send)

    chem, chemical, xlow, xhigh, ylow, yhigh = call(
        newton_kernel,
        (conc, phase, curvature, quartic, wells),
        [(128, 128), (4, 128, 128), (96, 128), (96, 128), (24, 128), (24, 128)],
        special={2: SMEM, 3: SMEM, 4: SMEM},
        name="newton",
    )
    halo = [shift(xhigh, "gx", 1), shift(yhigh, "gy", 1), shift(xlow, "gx", -1), shift(ylow, "gy", -1)]
    halo = [halo[0], halo[2], halo[1], halo[3]]

    own, other = spectrum(recv, (ylow,))
    back = update(own, other, par, par)
    strain, send = call(
        middle_kernel,
        (back, phase, par, z_tab, *halo),
        [(6, 128, 128), (768, 128)],
        halves,
        {4 + i: ANY for i in range(4)},
        name="middle",
    )
    own, other = spectrum(exchange(send), ())
    force, conc_next = call(
        laplace_kernel,
        (phase, chem, chemical, conc, *halo, own),
        [(4, 128, 128), (8, 32, 64)],
        special={8: ANY},
        name="laplace",
    )
    back = update(own, other, force, par)
    phase_next, stress = call(
        last_kernel,
        (back, phase, strain, force, par, z_tab),
        [(4, 8, 32, 64), (6, 8, 32, 64)],
        [
            pltpu.VMEM((6, 128, 128), F32),
            pltpu.VMEM((4, 2, 4, 32, 64), F32),
            pltpu.VMEM((4, 2, 6, 32, 64), F32),
            pltpu.SemaphoreType.DMA((16,)),
        ],
        out_spec=HBM,
        name="last",
    )
    return (phase_next, conc_next, stress)


def solution(mesh):
    in_specs = (
        P("gx", "gy", None),
        P(None, "gx", "gy", None),
        P("gx", "gy", None),
        P(),
        P(),
        P(),
        P(),
        P(),
    )
    out_specs = (P(None, "gx", "gy", None), P("gx", "gy", None), P(None, "gx", "gy", None))
    return jax.shard_map(shards, mesh=mesh, in_specs=in_specs, out_specs=out_specs, check_vma=False)
```

time: 104 us -> 90.7 us (0.87)
  blocking collectives: 64.6 us -> 35 us
  waiting for transfers between devices: 2.25 us -> 14.8 us
  starting transfers between devices: 14.3 us -> 25.7 us
  local copies, waits for them, and re-layouts: 5.64 us -> 0.68 us
  Pallas kernels: 16.4 us -> 13.5 us
    all_to_all x3 -> x2, blocking collectives: 64.6 us -> 35 us  [exchange(): y = lax.all_to_all(x.reshape(128, 1, 768), BOTH, 0, 0, tiled=True)]
    all_to_all x1 -> x2, starting transfers between devices: 4.78 us -> 15.9 us  [exchange(): y = lax.all_to_all(x.reshape(128, 1, 768), BOTH, 0, 0, tiled=True)]
    all_to_all x1 -> x2, waiting for transfers between devices: 0.01 us -> 10.8 us  [exchange(): y = lax.all_to_all(x.reshape(128, 1, 768), BOTH, 0, 0, tiled=True)]
    unnamed x30 -> x16, local copies, waits for them, and re-layouts: 5.64 us -> 0.68 us
    pallas_call x8 -> x9, Pallas kernels: 16.4 us -> 13.5 us  [call(): pl.pallas_call(kernel, out_shape=shapes, in_specs=specs, out_specs=[out_s...]
    ppermute x0 -> x2, waiting for transfers between devices: none -> 2.22 us  [spectrum(): return (own, lax.ppermute(own, 'gx', [(i, i ^ 1) for i in range(16)]))]
  transfers between devices with their start and end apart: 5 -> 8, of which waited for: 1 -> 5; matrix products, arithmetic and copies ran while one was open for 0% -> 0% of each run, Pallas kernels for 3% -> 3%
where the time goes in v2:
time: 90.7 us; the launch traced here: 90.4 us
  blocking collectives  35 us (39%)
  starting transfers between devices  25.7 us (28%)
  waiting for transfers between devices  14.8 us (16%)
  Pallas kernels  13.5 us (15%)
    all_to_all x2, blocking collectives, exchange(): y = lax.all_to_all(x.reshape(128, 1, 768), BOTH, 0, 0, tiled=True)  35 us
    all_to_all x2, starting transfers between devices, exchange(): y = lax.all_to_all(x.reshape(128, 1, 768), BOTH, 0, 0, tiled=True)  15.9 us
    pallas_call x9, Pallas kernels, call(): pl.pallas_call(kernel, out_shape=shapes, in_specs=specs, out_specs=[out_s...  13.5 us
    all_to_all x2, waiting for transfers between devices, exchange(): y = lax.all_to_all(x.reshape(128, 1, 768), BOTH, 0, 0, tiled=True)  10.8 us
    ppermute x4, starting transfers between devices, shift(): lax.ppermute(value, axis, [(i, (i + step) % count) for i in range(count)])  9.56 us
    ppermute x2, waiting for transfers between devices, spectrum(): return (own, lax.ppermute(own, 'gx', [(i, i ^ 1) for i in range(16)]))  2.22 us
    ppermute x4, waiting for transfers between devices, shift(): lax.ppermute(value, axis, [(i, (i + step) % count) for i in range(count)])  1.83 us
  transfers between devices with their start and end apart: 8, of which 5 were waited for; matrix products, arithmetic and copies ran while one was open for 0% of the time, Pallas kernels for 3%

profile of v2, /device:TPU:0, one launch (start us, length us, event | category | flops | bytes accessed | tf_op | source)
XLA Modules:
  0.0 90.4 jit_solution(11099517479239044325)
XLA Ops:
  0.6 2.6 %first.1 = (f32[4,128,128]{2,1,0:T(8,128)S(1)}, f32[768,128]{1,0:T(8,128)}, f32[40,128]{1,0:T(8,128)S(1)}) custom-call(s32[8,32,64]{2,1,0:T(8,128)} %labels_hbm.1, f32[4,8,32,64]{3,2,1,0:T(8,128)} %noise_hbm.1, f32[2,4]{1,0:T(2,128)} %lame_hbm.1, f32[4,6]{1,0:T(4,128)} %eigen_hbm.1, bf16[8,128,128]{2,1,0:T(8,128)(2,1)} %constant.8.clone.tab_hbm.tab_ref), custom_call_target="tpu_custom_call" | custom-call | flops 4000000 | bytes 4000000 | tf_op jit(solution)/shard_map/first/pallas_call | solution.py:528
  3.2 0.0 copy-start.2
  3.2 0.0 copy-start
  3.3 11.2 %all-to-all-start = ((f32[128,1,768]{2,1,0:T(1,128)}), f32[128,1,768]{2,1,0:T(1,128)S(1)}, u32[]{:S(2)}, u32[]{:S(2)}) async-start(f32[128,1,768]{2,1,0:T(1,128)} %bitcast), calls=%async_computation | async-start | bytes 786432 | tf_op jit(solution)/shard_map/all_to_all | solution.py:541
  14.4 0.0 copy-start.5
  14.5 0.0 copy-start.6
  14.5 0.0 copy-start.7
  14.5 0.0 copy-done.2
  14.5 0.6 copy-done.5
  15.1 0.0 copy-done.6
  15.1 0.0 copy-done.7
  15.1 0.0 copy-start.4
  15.1 1.6 %newton.1 = (f32[128,128]{1,0:T(8,128)S(1)}, f32[4,128,128]{2,1,0:T(8,128)S(1)}, f32[96,128]{1,0:T(8,128)S(1)}, f32[96,128]{1,0:T(8,128)S(1)}, f32[24,128]{1,0:T(8,128)S(1)}, /*index=5*/f32[24,128]{1,0:T(8,128)S(1)}) custom-call(f32[8,32,64]{2,1,0:T(8,128)S(1)} %copy-done.2, f32[4,128,128]{2,1,0:T(8,128)S(1)} %get-tuple-element.19.phase_ref, ...), custom_call_target="tpu_custom_call" | custom-call | flops 4000000 | bytes 4000000 | tf_op jit(solution)/shard_map/newton/pallas_call | solution.py:528
  16.7 9.9 %all-to-all-done = f32[128,1,768]{2,1,0:T(1,128)S(1)} async-done(((f32[128,1,768]{2,1,0:T(1,128)}), f32[128,1,768]{2,1,0:T(1,128)S(1)}, u32[]{:S(2)}, u32[]{:S(2)}) %all-to-all-start) | async-done | bytes 393248 | tf_op jit(solution)/shard_map/all_to_all | solution.py:541
  26.6 0.0 copy-done
  26.6 0.0 copy-done.4
  26.6 0.0 copy-start.3
  26.6 1.0 %spectrum.2.own_ref = f32[384,256]{1,0:T(8,128)S(1)} custom-call(f32[768,128]{1,0:T(8,128)S(1)} %bitcast.9, bf16[2,128,128]{2,1,0:T(8,128)(2,1)S(1)} %copy-done.4, bf16[2,256,512]{2,1,0:T(8,128)(2,1)S(1)} %copy-done, f32[24,128]{1,0:T(8,128)S(1)} %get-tuple-element.20.refs_0_), custom_call_target="tpu_custom_call" | custom-call | flops 4000000 | bytes 4000000 | tf_op jit(solution)/shard_map/spectrum/pallas_call | solution.py:528
  27.6 0.1 collective-permute-start
  27.7 1.7 %collective-permute-done.other_ref = f32[384,256]{1,0:T(8,128)S(1)} collective-permute-done((f32[384,256]{1,0:T(8,128)S(1)}, f32[384,256]{1,0:T(8,128)S(1)}, u32[]{:S(2)}, u32[]{:S(2)}) %collective-permute-start) | collective-permute-done | bytes 393248 | tf_op jit(solution)/shard_map/ppermute | solution.py:573
  29.4 0.0 copy-done.3
  29.5 2.1 %green.2 = f32[768,128]{1,0:T(8,128)} custom-call(f32[384,256]{1,0:T(8,128)S(1)} %spectrum.2.own_ref, f32[384,256]{1,0:T(8,128)S(1)} %collective-permute-done.other_ref, f32[40,128]{1,0:T(8,128)S(1)} %get-tuple-element.21.after_ref.par_ref, f32[40,128]{1,0:T(8,128)S(1)} %get-tuple-element.21.after_ref.par_ref, bf16[2,128,128]{2,1,0:T(8,128)(2,1)S(1)} %copy-done.3, ...), custom_call_target="tpu_custom_call" | custom-call | flops 4000000 | bytes 4000000 | tf_op jit(solution)/shard_map/green/pallas_call | solution.py:528
  31.6 0.0 copy-start.1
  31.6 4.7 %all-to-all-start.1 = ((f32[128,1,768]{2,1,0:T(1,128)}), f32[128,1,768]{2,1,0:T(1,128)S(1)}, u32[]{:S(2)}, u32[]{:S(2)}) async-start(f32[128,1,768]{2,1,0:T(1,128)} %bitcast.2), calls=%async_computation.1 | async-start | bytes 786432 | tf_op jit(solution)/shard_map/all_to_all | solution.py:541
  36.3 0.1 collective-permute-start.1
  36.4 5.3 %collective-permute-start.2 = (f32[96,128]{1,0:T(8,128)S(1)}, f32[96,128]{1,0:T(8,128)S(1)}, u32[]{:S(2)}, u32[]{:S(2)}) collective-permute-start(f32[96,128]{1,0:T(8,128)S(1)} %get-tuple-element.23), channel_id=1, source_target_pairs={{0,120},{8,0},{16,8},{24,16},{32,24},{40,32},{48,40},{56,48},{64,5... | collective-permute-start | bytes 147464 | tf_op jit(solution)/shard_map/ppermute | solution.py:562
  41.8 0.9 collective-permute-start.3
  42.6 3.3 %collective-permute-start.4 = (f32[24,128]{1,0:T(8,128)S(1)}, f32[24,128]{1,0:T(8,128)S(1)}, u32[]{:S(2)}, u32[]{:S(2)}) collective-permute-start(f32[24,128]{1,0:T(8,128)S(1)} %get-tuple-element.20.refs_0_), channel_id=1, source_target_pairs={{0,7},{1,0},{2,1},{3,2},{4,3},{5,4},{6,5},{7,6},{8,15},{9,8},{10,9... | collective-permute-start | bytes 36872 | tf_op jit(solution)/shard_map/ppermute | solution.py:562
  45.9 1.8 %collective-permute-done.3.refs_2_.ylow_ref = f32[24,128]{1,0:T(8,128)S(1)} collective-permute-done((f32[24,128]{1,0:T(8,128)S(1)}, f32[24,128]{1,0:T(8,128)S(1)}, u32[]{:S(2)}, u32[]{:S(2)}) %collective-permute-start.3) | collective-permute-done | bytes 12320 | tf_op jit(solution)/shard_map/ppermute | solution.py:562
  47.7 0.0 collective-permute-done.4.refs_3_.yhigh_ref
  47.7 0.0 collective-permute-done.1.refs_0_.xlow_ref
  47.7 0.0 collective-permute-done.2.refs_1_.xhigh_ref
  47.7 0.9 %all-to-all-done.1 = f32[128,1,768]{2,1,0:T(1,128)S(1)} async-done(((f32[128,1,768]{2,1,0:T(1,128)}), f32[128,1,768]{2,1,0:T(1,128)S(1)}, u32[]{:S(2)}, u32[]{:S(2)}) %all-to-all-start.1) | async-done | bytes 393248 | tf_op jit(solution)/shard_map/all_to_all | solution.py:541
  48.7 0.0 copy-done.1
  48.7 0.7 middle.1
  49.4 18.3 %all_to_all.20 = f32[128,1,768]{2,1,0:T(1,128)S(1)} all-to-all(f32[128,1,768]{2,1,0:T(1,128)S(1)} %bitcast.13), channel_id=1, replica_groups=mesh['gx'=16,'gy'=8] {'gx','gy'}, dimensions={0} | all-to-all | bytes 786432 | tf_op jit(solution)/shard_map/all_to_all | solution.py:541
  67.7 1.0 %spectrum.3.after_ref.own_ref = f32[384,256]{1,0:T(8,128)S(1)} custom-call(f32[768,128]{1,0:T(8,128)S(1)} %bitcast.11, bf16[2,128,128]{2,1,0:T(8,128)(2,1)S(1)} %copy-done.4, bf16[2,256,512]{2,1,0:T(8,128)(2,1)S(1)} %copy-done), custom_call_target="tpu_custom_call" | custom-call | flops 4000000 | bytes 4000000 | tf_op jit(solution)/shard_map/spectrum/pallas_call | solution.py:528
  68.8 0.1 collective-permute-start.5
  68.8 1.2 %laplace.1 = (f32[4,128,128]{2,1,0:T(8,128)S(1)}, f32[8,32,64]{2,1,0:T(8,128)}) custom-call(f32[4,128,128]{2,1,0:T(8,128)S(1)} %get-tuple-element.19.phase_ref, f32[128,128]{1,0:T(8,128)S(1)} %get-tuple-element.26.chem_ref, f32[4,128,128]{2,1,0:T(8,128)S(1)} %get-tuple-element.27.chemical_ref, f32[8,32,64]{2,1,0:T(8,128)S(1)} %copy-done.2, ...), custom_call_target="tpu_custom_call" | custom-call | flops 4000000 | bytes 4000000 | tf_op jit(solution)/shard_map/laplace/pallas_call | solution.py:528
  70.0 0.5 collective-permute-done.5.other_ref
  70.6 1.4 %green.3 = f32[768,128]{1,0:T(8,128)S(1)} custom-call(f32[384,256]{1,0:T(8,128)S(1)} %spectrum.3.after_ref.own_ref, f32[384,256]{1,0:T(8,128)S(1)} %collective-permute-done.5.other_ref, f32[4,128,128]{2,1,0:T(8,128)S(1)} %get-tuple-element.28.after_ref.force_ref, f32[40,128]{1,0:T(8,128)S(1)} %get-tuple-element.21.after_ref.par_ref, ...), custom_call_target="tpu_custom_call" | custom-call | flops 4000000 | bytes 4000000 | tf_op jit(solution)/shard_map/green/pallas_call | solution.py:528
  71.9 16.6 %all_to_all.21 = f32[128,1,768]{2,1,0:T(1,128)S(1)} all-to-all(f32[128,1,768]{2,1,0:T(1,128)S(1)} %bitcast.12), channel_id=1, replica_groups=mesh['gx'=16,'gy'=8] {'gx','gy'}, dimensions={0} | all-to-all | bytes 786432 | tf_op jit(solution)/shard_map/all_to_all | solution.py:541
  88.6 1.8 %last.1 = (f32[4,8,32,64]{3,2,1,0:T(8,128)}, f32[6,8,32,64]{3,2,1,0:T(8,128)}) custom-call(f32[768,128]{1,0:T(8,128)S(1)} %bitcast.10, f32[4,128,128]{2,1,0:T(8,128)S(1)} %get-tuple-element.19.phase_ref, f32[6,128,128]{2,1,0:T(8,128)S(1)} %get-tuple-element.29.strain_ref, f32[4,128,128]{2,1,0:T(8,128)S(1)} %get-tuple-element.28.after_ref.force_ref, ...), custom_call_target="tpu_custom_call" | custom-call | flops 4000000 | bytes 4000000 | tf_op jit(solution)/shard_map/last/pallas_call | solution.py:528
Async XLA Ops:
  3.2 11.2 %copy-start.2 = (f32[8,32,64]{2,1,0:T(8,128)S(1)}, f32[8,32,64]{2,1,0:T(8,128)}, u32[]{:S(2)}) copy-start(f32[8,32,64]{2,1,0:T(8,128)} %conc_ref.3) | copy-start | bytes 196612
  3.2 23.4 %copy-start = (bf16[2,256,512]{2,1,0:T(8,128)(2,1)S(1)}, bf16[2,256,512]{2,1,0:T(8,128)(2,1)}, u32[]{:S(2)}) copy-start(bf16[2,256,512]{2,1,0:T(8,128)(2,1)} %constant.11.clone.y_ref) | copy-start | bytes 1572868
  3.3 23.3 %all-to-all-start = ((f32[128,1,768]{2,1,0:T(1,128)}), f32[128,1,768]{2,1,0:T(1,128)S(1)}, u32[]{:S(2)}, u32[]{:S(2)}) async-start(f32[128,1,768]{2,1,0:T(1,128)} %bitcast), calls=%async_computation | async-start | bytes 786432 | tf_op jit(solution)/shard_map/all_to_all | solution.py:541
  14.4 0.7 copy-start.5
  14.5 0.7 copy-start.6
  14.5 0.7 copy-start.7
  15.1 11.5 %copy-start.4 = (bf16[2,128,128]{2,1,0:T(8,128)(2,1)S(1)}, bf16[2,128,128]{2,1,0:T(8,128)(2,1)}, u32[]{:S(2)}) copy-start(bf16[2,128,128]{2,1,0:T(8,128)(2,1)} %constant.9.clone.xf_ref) | copy-start | bytes 196612
  26.6 2.8 %copy-start.3 = (bf16[2,128,128]{2,1,0:T(8,128)(2,1)S(1)}, bf16[2,128,128]{2,1,0:T(8,128)(2,1)}, u32[]{:S(2)}) copy-start(bf16[2,128,128]{2,1,0:T(8,128)(2,1)} %constant.10.clone.xi_ref) | copy-start | bytes 196612
  27.6 1.8 %collective-permute-start = (f32[384,256]{1,0:T(8,128)S(1)}, f32[384,256]{1,0:T(8,128)S(1)}, u32[]{:S(2)}, u32[]{:S(2)}) collective-permute-start(f32[384,256]{1,0:T(8,128)S(1)} %spectrum.2.own_ref), channel_id=1, source_target_pairs={{0,8},{8,0},{16,24},{24,16},{32,40},{40,32},{48,56},{56,48},{64,72... | collective-permute-start | bytes 1179656 | tf_op jit(solution)/shard_map/ppermute | solution.py:573
  31.6 17.1 %copy-start.1 = (bf16[8,128,128]{2,1,0:T(8,128)(2,1)S(1)}, bf16[8,128,128]{2,1,0:T(8,128)(2,1)}, u32[]{:S(2)}) copy-start(bf16[8,128,128]{2,1,0:T(8,128)(2,1)} %constant.8.clone.tab_hbm.tab_ref) | copy-start | bytes 786436
  31.6 17.1 %all-to-all-start.1 = ((f32[128,1,768]{2,1,0:T(1,128)}), f32[128,1,768]{2,1,0:T(1,128)S(1)}, u32[]{:S(2)}, u32[]{:S(2)}) async-start(f32[128,1,768]{2,1,0:T(1,128)} %bitcast.2), calls=%async_computation.1 | async-start | bytes 786432 | tf_op jit(solution)/shard_map/all_to_all | solution.py:541
  36.3 11.4 %collective-permute-start.1 = (f32[96,128]{1,0:T(8,128)S(1)}, f32[96,128]{1,0:T(8,128)S(1)}, u32[]{:S(2)}, u32[]{:S(2)}) collective-permute-start(f32[96,128]{1,0:T(8,128)S(1)} %get-tuple-element.22), channel_id=1, source_target_pairs={{0,8},{8,16},{16,24},{24,32},{32,40},{40,48},{48,56},{56,64},{64,7... | collective-permute-start | bytes 147464 | tf_op jit(solution)/shard_map/ppermute | solution.py:562
  36.4 11.3 %collective-permute-start.2 = (f32[96,128]{1,0:T(8,128)S(1)}, f32[96,128]{1,0:T(8,128)S(1)}, u32[]{:S(2)}, u32[]{:S(2)}) collective-permute-start(f32[96,128]{1,0:T(8,128)S(1)} %get-tuple-element.23), channel_id=1, source_target_pairs={{0,120},{8,0},{16,8},{24,16},{32,24},{40,32},{48,40},{56,48},{64,5... | collective-permute-start | bytes 147464 | tf_op jit(solution)/shard_map/ppermute | solution.py:562
  41.8 6.0 %collective-permute-start.3 = (f32[24,128]{1,0:T(8,128)S(1)}, f32[24,128]{1,0:T(8,128)S(1)}, u32[]{:S(2)}, u32[]{:S(2)}) collective-permute-start(f32[24,128]{1,0:T(8,128)S(1)} %get-tuple-element.24), channel_id=1, source_target_pairs={{0,1},{1,2},{2,3},{3,4},{4,5},{5,6},{6,7},{7,0},{8,9},{9,10},{10,1... | collective-permute-start | bytes 36872 | tf_op jit(solution)/shard_map/ppermute | solution.py:562
  42.6 5.1 %collective-permute-start.4 = (f32[24,128]{1,0:T(8,128)S(1)}, f32[24,128]{1,0:T(8,128)S(1)}, u32[]{:S(2)}, u32[]{:S(2)}) collective-permute-start(f32[24,128]{1,0:T(8,128)S(1)} %get-tuple-element.20.refs_0_), channel_id=1, source_target_pairs={{0,7},{1,0},{2,1},{3,2},{4,3},{5,4},{6,5},{7,6},{8,15},{9,8},{10,9... | collective-permute-start | bytes 36872 | tf_op jit(solution)/shard_map/ppermute | solution.py:562
  68.8 1.8 %collective-permute-start.5 = (f32[384,256]{1,0:T(8,128)S(1)}, f32[384,256]{1,0:T(8,128)S(1)}, u32[]{:S(2)}, u32[]{:S(2)}) collective-permute-start(f32[384,256]{1,0:T(8,128)S(1)} %spectrum.3.after_ref.own_ref), channel_id=1, source_target_pairs={{0,8},{8,0},{16,24},{24,16},{32,40},{40,32},{48,56},{56,48},{64,72... | collective-permute-start | bytes 1179656 | tf_op jit(solution)/shard_map/ppermute | solution.py:573

commit v3 on v2

--- a/solution.py
+++ b/solution.py
@@ -6,6 +6,7 @@
 from jax.experimental import pallas as pl
 from jax.experimental.pallas import tpu as pltpu
 from jax.sharding import PartitionSpec as P
+
 
 NEWTON = 5
 STEP_PHASE = 0.06
@@ -213,8 +214,7 @@
     z_forward(tab_ref, high_ref, low_ref, send_ref)
 
 
-def middle_kernel(recv_ref, phase_ref, par_ref, tab_ref, *refs):
-    strain_ref, send_ref, high_ref, low_ref = refs[-4:]
+def middle_kernel(recv_ref, phase_ref, par_ref, tab_ref, strain_ref, send_ref, high_ref, low_ref):
     par = Params(par_ref)
     for c in range(6):
         strain_ref[c] = -z_inverse(tab_ref, recv_ref, c)
@@ -407,8 +407,20 @@
 
 
 def newton_kernel(
-    conc_ref, phase_ref, curvature, quartic, wells, chem_ref, chemical_ref, xlow_ref, xhigh_ref, ylow_ref, yhigh_ref
+    conc_ref,
+    phase_ref,
+    curvature,
+    quartic,
+    wells,
+    after_ref,
+    chem_ref,
+    chemical_ref,
+    xlow_ref,
+    xhigh_ref,
+    ylow_ref,
+    yhigh_ref,
 ):
+    del after_ref
     for p in range(4):
         rows = pl.ds(p * 32, 32)
         conc = dense(conc_ref[p], conc_ref[p + 4])
@@ -521,7 +533,7 @@
 LIMIT = 12 * 1024 * 1024
 
 
-def call(kernel, args, out, scratch=(), special=None, out_spec=VMEM, cost=4e6, name=None):
+def call(kernel, args, out, scratch=(), special=None, out_spec=VMEM, cost=4e6):
     special = special or {}
     specs = [special.get(i, VMEM) for i in range(len(args))]
     shapes = [jax.ShapeDtypeStruct(s, F32) for s in out]
@@ -533,7 +545,6 @@
         scratch_shapes=list(scratch),
         compiler_params=pltpu.CompilerParams(vmem_limit_bytes=LIMIT),
         cost_estimate=pl.CostEstimate(flops=int(cost), bytes_accessed=int(cost), transcendentals=0),
-        name=name,
     )(*args)
 
 
@@ -542,7 +553,7 @@
     return y.reshape(768, 128)
 
 
-def shards(labels, seed_noise, conc, curvature, quartic, wells, lame, eigen):
+def step(labels, seed_noise, conc, curvature, quartic, wells, lame, eigen):
     tables = [half for t in z_tables() for half in split_np(t)]
     z_tab = jnp.asarray(np.stack(tables))
     x_forward, x_inverse = x_tables()
@@ -568,19 +579,11 @@
             [(384, 256)],
             plane_scratch,
             {3 + i: ANY for i in range(len(after))},
-            name="spectrum",
         )
         return own, lax.ppermute(own, "gx", [(i, i ^ 1) for i in range(16)])
 
     def update(own, other, after, par):
-        (back,) = call(
-            green_kernel,
-            (own, other, after, par, xi, yt),
-            [(768, 128)],
-            plane_scratch,
-            {2: ANY},
-            name="green",
-        )
+        (back,) = call(green_kernel, (own, other, after, par, xi, yt), [(768, 128)], plane_scratch, {2: ANY})
         return exchange(back)
 
     def in_hbm(*arrays):
@@ -600,37 +603,22 @@
             pltpu.SemaphoreType.DMA((5,)),
         ],
         {i: HBM for i in range(5)},
-        name="first",
     )
     recv = exchange(send)
 
+    own, other = spectrum(recv, ())
     chem, chemical, xlow, xhigh, ylow, yhigh = call(
         newton_kernel,
-        (conc, phase, curvature, quartic, wells),
+        (conc, phase, curvature, quartic, wells, own),
         [(128, 128), (4, 128, 128), (96, 128), (96, 128), (24, 128), (24, 128)],
-        special={2: SMEM, 3: SMEM, 4: SMEM},
-        name="newton",
+        special={2: SMEM, 3: SMEM, 4: SMEM, 5: ANY},
     )
-    halo = [shift(xhigh, "gx", 1), shift(yhigh, "gy", 1), shift(xlow, "gx", -1), shift(ylow, "gy", -1)]
-    halo = [halo[0], halo[2], halo[1], halo[3]]
-
-    own, other = spectrum(recv, (ylow,))
-    back = update(own, other, par, par)
-    strain, send = call(
-        middle_kernel,
-        (back, phase, par, z_tab, *halo),
-        [(6, 128, 128), (768, 128)],
-        halves,
-        {4 + i: ANY for i in range(4)},
-        name="middle",
-    )
+    halo = [shift(xhigh, "gx", 1), shift(xlow, "gx", -1), shift(yhigh, "gy", 1), shift(ylow, "gy", -1)]
+    back = update(own, other, ylow, par)
+    strain, send = call(middle_kernel, (back, phase, par, z_tab), [(6, 128, 128), (768, 128)], halves)
     own, other = spectrum(exchange(send), ())
     force, conc_next = call(
-        laplace_kernel,
-        (phase, chem, chemical, conc, *halo, own),
-        [(4, 128, 128), (8, 32, 64)],
-        special={8: ANY},
-        name="laplace",
+        laplace_kernel, (phase, chem, chemical, conc, *halo, own), [(4, 128, 128), (8, 32, 64)], special={8: ANY}
     )
     back = update(own, other, force, par)
     phase_next, stress = call(
@@ -644,7 +632,6 @@
             pltpu.SemaphoreType.DMA((16,)),
         ],
         out_spec=HBM,
-        name="last",
     )
     return (phase_next, conc_next, stress)
 
@@ -661,4 +648,4 @@
         P(),
     )
     out_specs = (P(None, "gx", "gy", None), P("gx", "gy", None), P(None, "gx", "gy", None))
-    return jax.shard_map(shards, mesh=mesh, in_specs=in_specs, out_specs=out_specs, check_vma=False)
+    return jax.shard_map(step, mesh=mesh, in_specs=in_specs, out_specs=out_specs, check_vma=False)

time: 90.7 us -> 99.5 us (1.097)
  blocking collectives: 35 us -> 74.4 us
  starting transfers between devices: 25.7 us -> 9.73 us
  waiting for transfers between devices: 14.8 us -> 1.68 us
  Pallas kernels: 13.5 us -> 12 us
    all_to_all x2 -> x4, blocking collectives: 35 us -> 74.4 us  [exchange(): y = lax.all_to_all(x.reshape(128, 1, 768), BOTH, 0, 0, tiled=True)]
    all_to_all x2 -> x0, starting transfers between devices: 15.9 us -> none  [exchange(): y = lax.all_to_all(x.reshape(128, 1, 768), BOTH, 0, 0, tiled=True)]
    all_to_all x2 -> x0, waiting for transfers between devices: 10.8 us -> none  [exchange(): y = lax.all_to_all(x.reshape(128, 1, 768), BOTH, 0, 0, tiled=True)]
    ppermute x2, waiting for transfers between devices: 2.22 us -> 0.01 us  [spectrum(): return (own, lax.ppermute(own, 'gx', [(i, i ^ 1) for i in range(16)]))]
    pallas_call x9, Pallas kernels: 13.5 us -> 12 us  [call(): pl.pallas_call(kernel, out_shape=shapes, in_specs=specs, out_specs=[out_s...]
  transfers between devices with their start and end apart: 8 -> 6, of which waited for: 5 -> 1; matrix products, arithmetic and copies ran while one was open for 0% -> 0% of each run, Pallas kernels for 3% -> 3%
where the time goes in v3:
time: 99.5 us; the launch traced here: 99.2 us
  blocking collectives  74.4 us (75%)
  Pallas kernels  12 us (12%)
  starting transfers between devices  9.73 us (10%)
  waiting for transfers between devices  1.68 us (2%)
    all_to_all x4, blocking collectives, exchange(): y = lax.all_to_all(x.reshape(128, 1, 768), BOTH, 0, 0, tiled=True)  74.4 us
    pallas_call x9, Pallas kernels, call(): pl.pallas_call(kernel, out_shape=shapes, in_specs=specs, out_specs=[out_s...  12 us
    ppermute x4, starting transfers between devices, shift(): lax.ppermute(value, axis, [(i, (i + step) % count) for i in range(count)])  9.56 us
  transfers between devices with their start and end apart: 6, of which 1 were waited for; matrix products, arithmetic and copies ran while one was open for 0% of the time, Pallas kernels for 3%

profile of v3, /device:TPU:0, one launch (start us, length us, event | category | flops | bytes accessed | tf_op | source)
XLA Modules:
  0.0 99.2 jit_solution(14308669041314982842)
XLA Ops:
  0.6 1.9 %shard_map.139 = (f32[4,128,128]{2,1,0:T(8,128)S(1)}, f32[768,128]{1,0:T(8,128)S(1)}, f32[40,128]{1,0:T(8,128)S(1)}) custom-call(s32[8,32,64]{2,1,0:T(8,128)} %labels_hbm.1, f32[4,8,32,64]{3,2,1,0:T(8,128)} %noise_hbm.1, f32[2,4]{1,0:T(2,128)} %lame_hbm.1, f32[4,6]{1,0:T(4,128)} %eigen_hbm.1, bf16[8,128,128]{2,1,0:T(8,128)(2,1)} %constant.8.clone.tab_hbm.tab_ref), custom_call_target="tpu_custom_call" | custom-call | flops 4000000 | bytes 4000000 | tf_op jit(solution)/shard_map/pallas_call | solution.py:540
  2.5 0.0 copy-start
  2.5 0.0 copy-start.4
  2.5 23.1 %all_to_all.20 = f32[128,1,768]{2,1,0:T(1,128)S(1)} all-to-all(f32[128,1,768]{2,1,0:T(1,128)S(1)} %bitcast.14), channel_id=1, replica_groups=mesh['gx'=16,'gy'=8] {'gx','gy'}, dimensions={0} | all-to-all | bytes 786432 | tf_op jit(solution)/shard_map/all_to_all | solution.py:552
  25.6 0.0 copy-done
  25.7 0.0 copy-done.4
  25.7 0.0 copy-start.2
  25.7 1.0 %shard_map.140.after_ref.own_ref = f32[384,256]{1,0:T(8,128)S(1)} custom-call(f32[768,128]{1,0:T(8,128)S(1)} %bitcast.12, bf16[2,128,128]{2,1,0:T(8,128)(2,1)S(1)} %copy-done.4, bf16[2,256,512]{2,1,0:T(8,128)(2,1)S(1)} %copy-done), custom_call_target="tpu_custom_call" | custom-call | flops 4000000 | bytes 4000000 | tf_op jit(solution)/shard_map/pallas_call | solution.py:540
  26.7 0.0 copy-start.5
  26.7 0.0 copy-start.6
  26.7 0.0 copy-start.7
  26.7 0.1 collective-permute-start
  26.8 0.0 copy-done.2
  26.8 0.5 copy-done.5
  27.3 0.0 copy-done.6
  27.4 0.0 copy-done.7
  27.4 0.0 copy-start.3
  27.4 1.6 %shard_map.141 = (f32[128,128]{1,0:T(8,128)S(1)}, f32[4,128,128]{2,1,0:T(8,128)S(1)}, f32[96,128]{1,0:T(8,128)S(1)}, f32[96,128]{1,0:T(8,128)S(1)}, f32[24,128]{1,0:T(8,128)S(1)}, /*index=5*/f32[24,128]{1,0:T(8,128)S(1)}) custom-call(f32[8,32,64]{2,1,0:T(8,128)S(1)} %copy-done.2, f32[4,128,128]{2,1,0:T(8,128)S(1)} %get-tuple-element.19.phase_ref, ...), custom_call_target="tpu_custom_call" | custom-call | flops 4000000 | bytes 4000000 | tf_op jit(solution)/shard_map/pallas_call | solution.py:540
  29.0 0.0 collective-permute-done.other_ref
  29.0 0.0 copy-done.3
  29.0 1.4 %shard_map.142 = f32[768,128]{1,0:T(8,128)S(1)} custom-call(f32[384,256]{1,0:T(8,128)S(1)} %shard_map.140.after_ref.own_ref, f32[384,256]{1,0:T(8,128)S(1)} %collective-permute-done.other_ref, f32[24,128]{1,0:T(8,128)S(1)} %get-tuple-element.20.after_ref, f32[40,128]{1,0:T(8,128)S(1)} %get-tuple-element.21.par_ref, bf16[2,128,128]{2,1,0:T(8,128)(2,1)S(1)} %copy-done.3, ...), custom_call_target="tpu_custom_call" | custom-call | flops 4000000 | bytes 4000000 | tf_op jit(solution)/shard_map/pallas_call | solution.py:540
  30.4 0.0 copy-start.1
  30.4 16.6 %all_to_all.21 = f32[128,1,768]{2,1,0:T(1,128)S(1)} all-to-all(f32[128,1,768]{2,1,0:T(1,128)S(1)} %bitcast.9), channel_id=1, replica_groups=mesh['gx'=16,'gy'=8] {'gx','gy'}, dimensions={0} | all-to-all | bytes 786432 | tf_op jit(solution)/shard_map/all_to_all | solution.py:552
  47.1 0.0 copy-done.1
  47.1 0.7 shard_map.143
  47.8 16.6 %all_to_all.22 = f32[128,1,768]{2,1,0:T(1,128)S(1)} all-to-all(f32[128,1,768]{2,1,0:T(1,128)S(1)} %bitcast.15), channel_id=1, replica_groups=mesh['gx'=16,'gy'=8] {'gx','gy'}, dimensions={0} | all-to-all | bytes 786432 | tf_op jit(solution)/shard_map/all_to_all | solution.py:552
  64.4 1.0 %shard_map.144.after_ref.own_ref = f32[384,256]{1,0:T(8,128)S(1)} custom-call(f32[768,128]{1,0:T(8,128)S(1)} %bitcast.11, bf16[2,128,128]{2,1,0:T(8,128)(2,1)S(1)} %copy-done.4, bf16[2,256,512]{2,1,0:T(8,128)(2,1)S(1)} %copy-done), custom_call_target="tpu_custom_call" | custom-call | flops 4000000 | bytes 4000000 | tf_op jit(solution)/shard_map/pallas_call | solution.py:540
  65.4 0.1 collective-permute-start.1
  65.5 0.5 collective-permute-start.2
  66.0 4.9 %collective-permute-start.3 = (f32[96,128]{1,0:T(8,128)S(1)}, f32[96,128]{1,0:T(8,128)S(1)}, u32[]{:S(2)}, u32[]{:S(2)}) collective-permute-start(f32[96,128]{1,0:T(8,128)S(1)} %get-tuple-element.26), channel_id=1, source_target_pairs={{0,120},{8,0},{16,8},{24,16},{32,24},{40,32},{48,40},{56,48},{64,5... | collective-permute-start | bytes 147464 | tf_op jit(solution)/shard_map/ppermute | solution.py:573
  71.0 0.6 collective-permute-start.4
  71.5 3.6 %collective-permute-start.5 = (f32[24,128]{1,0:T(8,128)S(1)}, f32[24,128]{1,0:T(8,128)S(1)}, u32[]{:S(2)}, u32[]{:S(2)}) collective-permute-start(f32[24,128]{1,0:T(8,128)S(1)} %get-tuple-element.20.after_ref), channel_id=1, source_target_pairs={{0,7},{1,0},{2,1},{3,2},{4,3},{5,4},{6,5},{7,6},{8,15},{9,8},{10,9... | collective-permute-start | bytes 36872 | tf_op jit(solution)/shard_map/ppermute | solution.py:573
  75.1 1.7 %collective-permute-done.4.ylow_ref = f32[24,128]{1,0:T(8,128)S(1)} collective-permute-done((f32[24,128]{1,0:T(8,128)S(1)}, f32[24,128]{1,0:T(8,128)S(1)}, u32[]{:S(2)}, u32[]{:S(2)}) %collective-permute-start.4) | collective-permute-done | bytes 12320 | tf_op jit(solution)/shard_map/ppermute | solution.py:573
  76.8 0.0 collective-permute-done.5.yhigh_ref
  76.8 0.0 collective-permute-done.2.xlow_ref
  76.8 0.0 collective-permute-done.3.xhigh_ref
  76.8 1.2 %shard_map.145 = (f32[4,128,128]{2,1,0:T(8,128)S(1)}, f32[8,32,64]{2,1,0:T(8,128)}) custom-call(f32[4,128,128]{2,1,0:T(8,128)S(1)} %get-tuple-element.19.phase_ref, f32[128,128]{1,0:T(8,128)S(1)} %get-tuple-element.23.chem_ref, f32[4,128,128]{2,1,0:T(8,128)S(1)} %get-tuple-element.24.chemical_ref, f32[8,32,64]{2,1,0:T(8,128)S(1)} %copy-done.2, ...), custom_call_target="tpu_custom_call" | custom-call | flops 4000000 | bytes 4000000 | tf_op jit(solution)/shard_map/pallas_call | solution.py:540
  78.0 0.0 collective-permute-done.1.other_ref
  78.0 1.4 %shard_map.146 = f32[768,128]{1,0:T(8,128)S(1)} custom-call(f32[384,256]{1,0:T(8,128)S(1)} %shard_map.144.after_ref.own_ref, f32[384,256]{1,0:T(8,128)S(1)} %collective-permute-done.1.other_ref, f32[4,128,128]{2,1,0:T(8,128)S(1)} %get-tuple-element.28.after_ref.force_ref, f32[40,128]{1,0:T(8,128)S(1)} %get-tuple-element.21.par_ref, ...), custom_call_target="tpu_custom_call" | custom-call | flops 4000000 | bytes 4000000 | tf_op jit(solution)/shard_map/pallas_call | solution.py:540
  79.4 18.0 %all_to_all.23 = f32[128,1,768]{2,1,0:T(1,128)S(1)} all-to-all(f32[128,1,768]{2,1,0:T(1,128)S(1)} %bitcast.13), channel_id=1, replica_groups=mesh['gx'=16,'gy'=8] {'gx','gy'}, dimensions={0} | all-to-all | bytes 786432 | tf_op jit(solution)/shard_map/all_to_all | solution.py:552
  97.4 1.8 %shard_map.147 = (f32[4,8,32,64]{3,2,1,0:T(8,128)}, f32[6,8,32,64]{3,2,1,0:T(8,128)}) custom-call(f32[768,128]{1,0:T(8,128)S(1)} %bitcast.10, f32[4,128,128]{2,1,0:T(8,128)S(1)} %get-tuple-element.19.phase_ref, f32[6,128,128]{2,1,0:T(8,128)S(1)} %get-tuple-element.29.strain_ref, f32[4,128,128]{2,1,0:T(8,128)S(1)} %get-tuple-element.28.after_ref.force_ref, ...), custom_call_target="tpu_custom_call" | custom-call | flops 4000000 | bytes 4000000 | tf_op jit(solution)/shard_map/pallas_call | solution.py:540
Async XLA Ops:
  2.5 23.2 %copy-start = (bf16[2,256,512]{2,1,0:T(8,128)(2,1)S(1)}, bf16[2,256,512]{2,1,0:T(8,128)(2,1)}, u32[]{:S(2)}) copy-start(bf16[2,256,512]{2,1,0:T(8,128)(2,1)} %constant.11.clone.y_ref) | copy-start | bytes 1572868
  2.5 23.2 %copy-start.4 = (bf16[2,128,128]{2,1,0:T(8,128)(2,1)S(1)}, bf16[2,128,128]{2,1,0:T(8,128)(2,1)}, u32[]{:S(2)}) copy-start(bf16[2,128,128]{2,1,0:T(8,128)(2,1)} %constant.9.clone.xf_ref) | copy-start | bytes 196612
  25.7 1.2 %copy-start.2 = (f32[8,32,64]{2,1,0:T(8,128)S(1)}, f32[8,32,64]{2,1,0:T(8,128)}, u32[]{:S(2)}) copy-start(f32[8,32,64]{2,1,0:T(8,128)} %conc_ref.3) | copy-start | bytes 196612
  26.7 0.7 copy-start.5
  26.7 0.7 copy-start.6
  26.7 0.7 copy-start.7
  26.7 2.3 %collective-permute-start = (f32[384,256]{1,0:T(8,128)S(1)}, f32[384,256]{1,0:T(8,128)S(1)}, u32[]{:S(2)}, u32[]{:S(2)}) collective-permute-start(f32[384,256]{1,0:T(8,128)S(1)} %shard_map.140.after_ref.own_ref), channel_id=1, source_target_pairs={{0,8},{8,0},{16,24},{24,16},{32,40},{40,32},{48,56},{56,48},{64,72... | collective-permute-start | bytes 1179656 | tf_op jit(solution)/shard_map/ppermute | solution.py:583
  27.4 1.6 %copy-start.3 = (bf16[2,128,128]{2,1,0:T(8,128)(2,1)S(1)}, bf16[2,128,128]{2,1,0:T(8,128)(2,1)}, u32[]{:S(2)}) copy-start(bf16[2,128,128]{2,1,0:T(8,128)(2,1)} %constant.10.clone.xi_ref) | copy-start | bytes 196612
  30.4 16.6 %copy-start.1 = (bf16[8,128,128]{2,1,0:T(8,128)(2,1)S(1)}, bf16[8,128,128]{2,1,0:T(8,128)(2,1)}, u32[]{:S(2)}) copy-start(bf16[8,128,128]{2,1,0:T(8,128)(2,1)} %constant.8.clone.tab_hbm.tab_ref) | copy-start | bytes 786436
  65.4 12.5 %collective-permute-start.1 = (f32[384,256]{1,0:T(8,128)S(1)}, f32[384,256]{1,0:T(8,128)S(1)}, u32[]{:S(2)}, u32[]{:S(2)}) collective-permute-start(f32[384,256]{1,0:T(8,128)S(1)} %shard_map.144.after_ref.own_ref), channel_id=1, source_target_pairs={{0,8},{8,0},{16,24},{24,16},{32,40},{40,32},{48,56},{56,48},{64,72... | collective-permute-start | bytes 1179656 | tf_op jit(solution)/shard_map/ppermute | solution.py:583
  65.5 11.2 %collective-permute-start.2 = (f32[96,128]{1,0:T(8,128)S(1)}, f32[96,128]{1,0:T(8,128)S(1)}, u32[]{:S(2)}, u32[]{:S(2)}) collective-permute-start(f32[96,128]{1,0:T(8,128)S(1)} %get-tuple-element.25), channel_id=1, source_target_pairs={{0,8},{8,16},{16,24},{24,32},{32,40},{40,48},{48,56},{56,64},{64,7... | collective-permute-start | bytes 147464 | tf_op jit(solution)/shard_map/ppermute | solution.py:573
  66.0 10.7 %collective-permute-start.3 = (f32[96,128]{1,0:T(8,128)S(1)}, f32[96,128]{1,0:T(8,128)S(1)}, u32[]{:S(2)}, u32[]{:S(2)}) collective-permute-start(f32[96,128]{1,0:T(8,128)S(1)} %get-tuple-element.26), channel_id=1, source_target_pairs={{0,120},{8,0},{16,8},{24,16},{32,24},{40,32},{48,40},{56,48},{64,5... | collective-permute-start | bytes 147464 | tf_op jit(solution)/shard_map/ppermute | solution.py:573
  71.0 5.8 %collective-permute-start.4 = (f32[24,128]{1,0:T(8,128)S(1)}, f32[24,128]{1,0:T(8,128)S(1)}, u32[]{:S(2)}, u32[]{:S(2)}) collective-permute-start(f32[24,128]{1,0:T(8,128)S(1)} %get-tuple-element.27), channel_id=1, source_target_pairs={{0,1},{1,2},{2,3},{3,4},{4,5},{5,6},{6,7},{7,0},{8,9},{9,10},{10,1... | collective-permute-start | bytes 36872 | tf_op jit(solution)/shard_map/ppermute | solution.py:573
  71.5 5.2 %collective-permute-start.5 = (f32[24,128]{1,0:T(8,128)S(1)}, f32[24,128]{1,0:T(8,128)S(1)}, u32[]{:S(2)}, u32[]{:S(2)}) collective-permute-start(f32[24,128]{1,0:T(8,128)S(1)} %get-tuple-element.20.after_ref), channel_id=1, source_target_pairs={{0,7},{1,0},{2,1},{3,2},{4,3},{5,4},{6,5},{7,6},{8,15},{9,8},{10,9... | collective-permute-start | bytes 36872 | tf_op jit(solution)/shard_map/ppermute | solution.py:573

commit v4 on v3

--- a/solution.py
+++ b/solution.py
@@ -18,13 +18,18 @@
 EVEN = (0, 1, 2, 5)
 ODD = (3, 4)
 ORDER = EVEN + ODD
-BOTH = ("gx", "gy")
+BOTH = ("gy", "gx")
 
 
 def split_np(table):
     high = table.astype(np.float32).astype(BF16)
     low = (table - high.astype(np.float64)).astype(np.float32).astype(BF16)
     return high, low
+
+
+def stack_k(table, axis):
+    high, low = split_np(table)
+    return np.concatenate([high, high, low], axis=axis)
 
 
 def z_tables():
@@ -42,26 +47,36 @@
     def double(t):
         return np.kron(np.eye(2), t)
 
-    return double(even), double(odd), double(even * weight), double(odd * weight)
+    forward = np.stack([stack_k(double(t), 1) for t in (even, odd)])
+    inverse = np.stack([stack_k(double(t * weight), 0) for t in (even, odd)])
+    return forward, inverse
 
 
 def x_tables():
-    order = np.array([8 * g + 4 * par + p for par in range(2) for p in range(4) for g in range(16)])
-    k = np.arange(64)[:, None]
-    angle = 2.0 * np.pi * ((k * order[None, :]) % 128) / 128.0
-    real = np.cos(angle)
-    imag = -np.sin(angle)
-    imag[0] = np.where(order % 2 == 0, 1.0, -1.0)
-    forward = np.concatenate([real, imag], axis=0)
-    weight = np.where(np.arange(128) % 64 == 0, 1.0, 2.0) / (128.0 * 256.0)
-    inverse = (forward * weight[:, None]).T
-    return forward, inverse
-
-
-def y_table():
-    y = np.arange(256)
-    angle = 2.0 * np.pi * ((y[:, None] * y[None, :]) % 256) / 256.0
-    return np.concatenate([np.cos(angle), np.sin(angle)], axis=1)
+    order = np.array([8 * g + 4 * par + p for par in range(2) for p in range(4) for g in range(8)])
+    forward, inverse = [], []
+    for parity in range(2):
+        k = 2 * np.arange(32)[:, None] + parity
+        angle = 2.0 * np.pi * ((k * order[None, :]) % 128) / 128.0
+        real, imag = np.cos(angle), -np.sin(angle)
+        weight = np.full((64, 1), 2.0)
+        if parity == 0:
+            imag[0] = np.where(order % 2 == 0, 1.0, -1.0)
+            weight[0] = weight[32] = 1.0
+        table = np.concatenate([real, imag], axis=0)
+        forward.append(stack_k(table, 1))
+        inverse.append(stack_k((table * weight / (128.0 * 256.0)).T, 1))
+    return np.stack(forward), np.stack(inverse)
+
+
+def y_tables():
+    y = np.arange(128)[:, None]
+    m = np.arange(128)[None, :]
+    tables = []
+    for k, n in ((2 * m, y), (2 * m + 1, y), (2 * y + 1, m)):
+        angle = 2.0 * np.pi * ((k * n) % 256) / 256.0
+        tables.append(stack_k(np.concatenate([np.cos(angle), np.sin(angle)], axis=1), 0))
+    return np.stack(tables)
 
 
 def split(value):
@@ -92,7 +107,7 @@
         return self.row(8 + 6 * a + p)
 
 
-def write_params(lame, eigen, ref):
+def write_params(lame, eigen, others, ref):
     def middle(v):
         top = jnp.maximum(jnp.maximum(v[0], v[1]), jnp.maximum(v[2], v[3]))
         least = jnp.minimum(jnp.minimum(v[0], v[1]), jnp.minimum(v[2], v[3]))
@@ -101,6 +116,7 @@
     values = [lame[i, a] for i in range(2) for a in range(4)]
     values += [eigen[a, p] for a in range(4) for p in range(6)]
     values += [middle(values[0:4]), middle(values[4:8])]
+    values += [v[a] for v in others for a in range(4)]
     for i, value in enumerate(values):
         ref[pl.ds(i, 1), :] = jnp.full((1, 128), value, F32)
 
@@ -117,79 +133,57 @@
     return [shear2 * elastic[p] + trace if p < 3 else shear2 * elastic[p] for p in range(6)]
 
 
-def put_split(values, row, size, high_ref, low_ref):
-    for i, p in enumerate(ORDER):
-        high, low = split(values[p])
-        high_ref[pl.ds(i * 128 + row, size), :] = high
-        low_ref[pl.ds(i * 128 + row, size), :] = low
+def cell_block(b):
+    return lax.rem(b + 4 - lax.rem(lax.axis_index("gy"), 4), 4)
+
+
+def block_rows(p):
+    return pl.ds(pl.multiple_of(p * 32, 32), 32)
+
+
+def put_split(values, b, data_ref):
+    for i, c in enumerate(ORDER):
+        high, low = split(values[c])
+        at = pl.ds(pl.multiple_of(i * 128 + b * 32, 32), 32)
+        data_ref[at, :128] = high
+        data_ref[at, 128:] = low
 
 
 NT = ((1,), (1,))
 
 
-def z_forward(tab_ref, high_ref, low_ref, send_ref):
+def stack3(value, axis):
+    high, low = split(value)
+    return jnp.concatenate([high, low, high], axis=axis)
+
+
+def z_forward(tab_ref, data_ref, send_ref):
     for which, (start, comps) in enumerate(((0, EVEN), (512, ODD))):
-        rows = 128 * len(comps)
-        high = high_ref[pl.ds(start, rows), :]
-        low = low_ref[pl.ds(start, rows), :]
-        t_high, t_low = tab_ref[2 * which], tab_ref[2 * which + 1]
-        out = dot(t_high, high, NT) + dot(t_high, low, NT) + dot(t_low, high, NT)
+        data = data_ref[pl.ds(start, 128 * len(comps)), :]
+        out = dot(tab_ref[which], jnp.concatenate([data, data[:, :128]], axis=1), NT)
         for i, c in enumerate(comps):
             r, k = divmod(c, 3)
             for par in range(2):
-                for sh in range(8):
-                    at = par * 64 + sh * 8
-                    piece = out[at : at + 8, i * 128 : i * 128 + 128]
-                    send_ref[pl.ds((sh * 16 + r * 8) * 6 + k * 2 + par, 8, stride=6), :] = piece
+                piece = out[par * 64 : par * 64 + 64, i * 128 : i * 128 + 128]
+                send_ref[pl.ds(r * 6 + k * 2 + par, 64, stride=12), :] = piece
 
 
 def z_inverse(tab_ref, recv_ref, c):
     r, k = divmod(c, 3)
-    pieces = [
-        recv_ref[pl.ds((sh * 16 + r * 8) * 6 + k * 2 + par, 8, stride=6), :] for par in range(2) for sh in range(8)
-    ]
+    pieces = [recv_ref[pl.ds(r * 6 + k * 2 + par, 64, stride=12), :] for par in range(2)]
     data = jnp.concatenate(pieces, axis=0).T
-    which = 4 + 2 * (c in ODD)
-    t_high, t_low = tab_ref[which], tab_ref[which + 1]
-    high, low = split(data)
-    return dot(high, t_high) + dot(low, t_high) + dot(high, t_low)
-
-
-def first_kernel(
-    labels_hbm,
-    noise_hbm,
-    lame_hbm,
-    eigen_hbm,
-    tab_hbm,
-    phase_ref,
-    send_ref,
-    par_ref,
-    labels_ref,
-    noise_ref,
-    lame_ref,
-    eigen_ref,
-    tab_ref,
-    high_ref,
-    low_ref,
-    sem,
-):
-    copies = [
-        pltpu.make_async_copy(source, target, sem.at[i])
-        for i, (source, target) in enumerate(
-            (
-                (lame_hbm, lame_ref),
-                (eigen_hbm, eigen_ref),
-                (labels_hbm, labels_ref),
-                (noise_hbm, noise_ref),
-                (tab_hbm, tab_ref),
-            )
-        )
-    ]
+    return dot(stack3(data, 1), tab_ref[int(c in ODD)])
+
+
+def first_kernel(*refs):
+    sources, (phase_ref, mat_ref, send_ref, par_ref), targets, (data_ref, sem) = refs[:8], refs[8:12], refs[12:20], refs[20:]
+    copies = [pltpu.make_async_copy(a, b, sem.at[i]) for i, (a, b) in enumerate(zip(sources, targets))]
     for copy in copies:
         copy.start()
+    labels_ref, noise_ref, lame_ref, eigen_ref, *others, tab_ref = targets
     for copy in copies[:4]:
         copy.wait()
-    write_params(lame_ref, eigen_ref, par_ref)
+    by = lax.rem(lax.axis_index("gy"), 4)
 
     def lame(i, a):
         return lame_ref[i, a]
@@ -198,6 +192,7 @@
         return eigen_ref[a, p]
 
     for p in range(4):
+        rows = pl.ds(p * 32, 32)
         label = dense(labels_ref[p], labels_ref[p + 4])
         raw = [
             dense(noise_ref[a, p], noise_ref[a, p + 4]) + jnp.where(label == a, 2.0, 0.0).astype(F32)
@@ -206,43 +201,61 @@
         inverse = 1.0 / (raw[0] + raw[1] + raw[2] + raw[3])
         phase = [raw[a] * inverse for a in range(4)]
         for a in range(4):
-            phase_ref[a, pl.ds(p * 32, 32), :] = phase[a]
+            phase_ref[a, rows, :] = phase[a]
         lam, shear2, eig = material(phase, lame, eigen)
-        stress = stress_from([-v for v in eig], lam, shear2)
-        put_split(stress, p * 32, 32, high_ref, low_ref)
-    copies[4].wait()
-    z_forward(tab_ref, high_ref, low_ref, send_ref)
-
-
-def middle_kernel(recv_ref, phase_ref, par_ref, tab_ref, strain_ref, send_ref, high_ref, low_ref):
-    par = Params(par_ref)
+        for i, value in enumerate([lam, shear2, *eig]):
+            mat_ref[i, rows, :] = value
+        put_split(stress_from([-v for v in eig], lam, shear2), lax.rem(p + by, 4), data_ref)
+    for copy in copies[4:]:
+        copy.wait()
+    z_forward(tab_ref, data_ref, send_ref)
+    write_params(lame_ref, eigen_ref, others, par_ref)
+
+
+def middle_kernel(recv_ref, mat_ref, tab_ref, inv_ref, strain_ref, send_ref, data_ref):
+    strain = []
     for c in range(6):
-        strain_ref[c] = -z_inverse(tab_ref, recv_ref, c)
-    for p in range(4):
-        rows = pl.ds(p * 32, 32)
-        phase = [phase_ref[a, rows, :] for a in range(4)]
-        lam, shear2, eig = material(phase, par.lame, par.eigen)
-        stress = stress_from([strain_ref[c, rows, :] - eig[c] for c in range(6)], lam, shear2)
-        put_split(stress, p * 32, 32, high_ref, low_ref)
-    z_forward(tab_ref, high_ref, low_ref, send_ref)
+        strain.append(-z_inverse(inv_ref, recv_ref, c))
+        strain_ref[c] = strain[c]
+    for b in range(4):
+        rows = block_rows(cell_block(b))
+        lam, shear2, *eig = [mat_ref[i, rows, :] for i in range(8)]
+        elastic = [strain[c][b * 32 : b * 32 + 32] - eig[c] for c in range(6)]
+        put_split(stress_from(elastic, lam, shear2), b, data_ref)
+    z_forward(tab_ref, data_ref, send_ref)
 
 
 def last_kernel(
-    recv_ref, phase_ref, strain_ref, force_ref, par_ref, tab_ref, next_hbm, stress_hbm, work_ref, next_ref, stress_ref, sem
+    recv_ref,
+    phase_ref,
+    mat_ref,
+    strain_ref,
+    force_ref,
+    par_ref,
+    inv_ref,
+    next_hbm,
+    stress_hbm,
+    next_ref,
+    stress_ref,
+    sem,
 ):
     par = Params(par_ref)
-    for c in range(6):
-        work_ref[c] = strain_ref[c] - z_inverse(tab_ref, recv_ref, c)
+    strain = [strain_ref[c] - z_inverse(inv_ref, recv_ref, c) for c in range(6)]
     copies = []
-    for p in range(4):
-        rows = pl.ds(p * 32, 32)
-        phase = [phase_ref[a, rows, :] for a in range(4)]
-        lam, shear2, eig = material(phase, par.lame, par.eigen)
-        elastic = [work_ref[c, rows, :] - eig[c] for c in range(6)]
+    for b in range(4):
+        p = cell_block(b)
+        rows = block_rows(p)
+        lam, shear2, *eig = [mat_ref[i, rows, :] for i in range(8)]
+        elastic = [strain[c][b * 32 : b * 32 + 32] - eig[c] for c in range(6)]
         stress = stress_from(elastic, lam, shear2)
         for c in range(6):
-            stress_ref[p, 0, c] = stress[c][:, :64]
-            stress_ref[p, 1, c] = stress[c][:, 64:]
+            stress_ref[b, 0, c] = stress[c][:, :64]
+            stress_ref[b, 1, c] = stress[c][:, 64:]
+        for half in range(2):
+            x = p + 4 * half
+            at = 4 * b + 2 * half
+            copies.append(pltpu.make_async_copy(stress_ref.at[b, half], stress_hbm.at[:, x], sem.at[at]))
+            copies[-1].start()
         trace = elastic[0] + elastic[1] + elastic[2]
         trace = 0.5 * trace * trace
         squares = (
@@ -258,56 +271,57 @@
             force.append(force_ref[a, rows, :] + par.lame(0, a) * trace + par.lame(1, a) * squares - coupling)
         mean = 0.25 * (force[0] + force[1] + force[2] + force[3])
         for a in range(4):
-            new = phase[a] - STEP_PHASE * (force[a] - mean)
-            next_ref[p, 0, a] = new[:, :64]
-            next_ref[p, 1, a] = new[:, 64:]
+            new = phase_ref[a, rows, :] - STEP_PHASE * (force[a] - mean)
+            next_ref[b, 0, a] = new[:, :64]
+            next_ref[b, 1, a] = new[:, 64:]
         for half in range(2):
             x = p + 4 * half
-            copies.append(pltpu.make_async_copy(stress_ref.at[p, half], stress_hbm.at[:, x], sem.at[2 * x]))
-            copies.append(pltpu.make_async_copy(next_ref.at[p, half], next_hbm.at[:, x], sem.at[2 * x + 1]))
-        for copy in copies[-4:]:
-            copy.start()
+            at = 4 * b + 2 * half + 1
+            copies.append(pltpu.make_async_copy(next_ref.at[b, half], next_hbm.at[:, x], sem.at[at]))
+            copies[-1].start()
     for copy in copies:
         copy.wait()
 
 
-def swap_blocks(x):
+def mix(x):
     lane = lax.broadcasted_iota(jnp.int32, x[0].shape, 1)
-    wide = lane < 64
-    narrow = (lane & 32) == 0
-    a = [jnp.where(wide, x[i], pltpu.roll(x[i + 2], 64, 1)) for i in range(2)]
-    b = [jnp.where(wide, pltpu.roll(x[i], 64, 1), x[i + 2]) for i in range(2)]
-    out = []
-    for first, second in (a, b):
-        out.append(jnp.where(narrow, first, pltpu.roll(second, 32, 1)))
-        out.append(jnp.where(narrow, pltpu.roll(first, 96, 1), second))
-    return out
+    low = lane < 64
+    even = (lane & 32) == 0
+    e01, e23, e30, e12 = (jnp.where(even, x[a], x[b]) for a, b in ((0, 1), (2, 3), (3, 0), (1, 2)))
+    return [jnp.where(low, a, b) for a, b in ((e01, e23), (e30, e12), (e23, e01), (e12, e30))]
+
+
+def roll_lanes(x, by):
+    return pltpu.roll(x, by, 1) if by else x
 
 
 def spectrum_kernel(recv_ref, xf_ref, y_ref, *refs):
-    out_ref, high_ref, low_ref, mid_ref = refs[-4:]
-    xf_high, xf_low = xf_ref[0], xf_ref[1]
+    out_ref, even_ref, odd_ref = refs[-3:]
     for k in range(3):
-        rows = []
+        total, delta = [], []
         for par in range(2):
             columns = []
             for gh in range(2):
-                pieces = [
-                    recv_ref[pl.ds((4 * gh + i) * 6 + k * 2 + par, 16, stride=48), :] for i in range(4)
-                ]
-                columns.append(swap_blocks(pieces))
-            rows += [jnp.concatenate([columns[0][p], columns[1][p]], axis=1) for p in range(4)]
-        high, low = split(jnp.concatenate(rows, axis=0))
-        out = dot(xf_high, high) + dot(xf_high, low) + dot(xf_low, high)
-        high, low = split(out)
-        high_ref[pl.ds(k * 128, 128), :] = high
-        low_ref[pl.ds(k * 128, 128), :] = low
-    y_high, y_low = y_ref[0], y_ref[1]
-    mid_ref[...] = dot(high_ref[...], y_high) + dot(low_ref[...], y_high) + dot(high_ref[...], y_low)
-    for k in range(3):
-        real, imag = pl.ds(k * 128, 64), pl.ds(k * 128 + 64, 64)
-        out_ref[real, :] = mid_ref[real, :256] + mid_ref[imag, 256:]
-        out_ref[imag, :] = mid_ref[imag, :256] - mid_ref[real, 256:]
+                pieces = [recv_ref[pl.ds((4 * gh + i) * 96 + k * 2 + par, 16, stride=6), :] for i in range(4)]
+                columns.append([roll_lanes(v, (128 - 32 * p) % 128) for p, v in enumerate(mix(pieces))])
+            for p in range(4):
+                both = jnp.concatenate([columns[0][p], columns[1][p]], axis=1)
+                total.append(both[:8] + both[8:])
+                delta.append(both[:8] - both[8:])
+        even = dot(xf_ref[0], stack3(jnp.concatenate(total, axis=0), 0))
+        odd = dot(xf_ref[1], stack3(jnp.concatenate(delta, axis=0), 0))
+        value = jnp.concatenate([even[:32], odd[:32], even[32:], odd[32:]], axis=0)
+        left, right = value[:, :128], value[:, 128:]
+        rows = pl.ds(k * 128, 128)
+        even_ref[rows, :] = stack3(left + right, 1)
+        odd_ref[rows, :] = stack3(left - right, 1)
+    for which, ref in enumerate((even_ref, odd_ref)):
+        mid = dot(ref[...], y_ref[which])
+        lanes = slice(which * 128, which * 128 + 128)
+        for k in range(3):
+            real, imag = mid[k * 128 : k * 128 + 64], mid[k * 128 + 64 : k * 128 + 128]
+            out_ref[pl.ds(k * 128, 64), lanes] = real[:, :128] + imag[:, 128:]
+            out_ref[pl.ds(k * 128 + 64, 64), lanes] = imag[:, :128] - real[:, 128:]
 
 
 def green_tile(re, im, wx, wy, omega, first, second, upper):
@@ -344,11 +358,11 @@
     return out
 
 
-def green_kernel(own_ref, other_ref, after_ref, par_ref, xi_ref, y_ref, send_ref, high_ref, low_ref, mid_ref):
+def green_kernel(own_ref, other_ref, after_ref, par_ref, xi_ref, y_ref, send_ref, even_ref, odd_ref):
     del after_ref
     x_index, y_index = lax.axis_index("gx"), lax.axis_index("gy")
     core = lax.rem(x_index, 2)
-    slab = lax.div(x_index, 2) * 8 + y_index
+    slab = y_index * 8 + lax.div(x_index, 2)
     omega = jnp.where(slab < 32, slab, 32 - slab).astype(F32) * (1.0 / 64.0)
     par = Params(par_ref)
     lam0 = jnp.concatenate([par.row(32), par.row(32)], axis=1)
@@ -356,13 +370,14 @@
     half_mu = 0.5 / mu0
     ratio = (lam0 + mu0) / (mu0 * (lam0 + 2.0 * mu0))
     lane = lax.broadcasted_iota(jnp.int32, (8, 256), 1)
-    index = jnp.where(lane >= 128, lane - 256, lane)
-    wy = jnp.where(lane == 128, 0, index).astype(F32) * (1.0 / 256.0)
+    index = jnp.where(lane < 128, 2 * lane, 2 * lane - 255)
+    index = jnp.where(index == 128, 0, jnp.where(index > 128, index - 256, index))
+    wy = index.astype(F32) * (1.0 / 256.0)
     row = lax.broadcasted_iota(jnp.int32, (8, 256), 0)
 
     def green(upper):
         for tile in range(8):
-            wx = (row + tile * 8).astype(F32) * (1.0 / 128.0)
+            wx = (2 * row + (tile % 4 * 16 + tile // 4)).astype(F32) * (1.0 / 128.0)
             q = wx * wx + wy * wy + omega * omega
             inverse = 1.0 / jnp.where(q == 0.0, 1.0, q)
             first = half_mu * inverse
@@ -376,10 +391,12 @@
             out = green_tile(re, im, wx, wy, omega, first, second, upper)
             for part in range(2):
                 for k in range(3):
-                    high, low = split(out[part][k])
                     at = pl.ds(k * 128 + part * 64 + tile * 8, 8)
-                    high_ref[at, :] = high
-                    low_ref[at, :] = low
+                    value = stack3(out[part][k], 0)
+                    for i in range(3):
+                        piece = value[i * 8 : i * 8 + 8]
+                        even_ref[at, i * 128 : i * 128 + 128] = piece[:, :128]
+                        odd_ref[at, i * 128 : i * 128 + 128] = piece[:, 128:]
 
     @pl.when(core == 0)
     def _():
@@ -389,29 +406,37 @@
     def _():
         green(True)
 
-    y_high, y_low = y_ref[0], y_ref[1]
-    mid_ref[...] = dot(high_ref[...], y_high) + dot(low_ref[...], y_high) + dot(high_ref[...], y_low)
-    xi_high, xi_low = xi_ref[0], xi_ref[1]
+    halves = []
+    for ref, table in ((even_ref, y_ref[0]), (odd_ref, y_ref[2])):
+        halves.append(dot(ref[...], table))
     for k in range(3):
-        r_rows, i_rows = pl.ds(k * 128, 64), pl.ds(k * 128 + 64, 64)
-        real = mid_ref[r_rows, :256] - mid_ref[i_rows, 256:]
-        imag = mid_ref[i_rows, :256] + mid_ref[r_rows, 256:]
-        high, low = split(jnp.concatenate([real, imag], axis=0))
-        out = dot(xi_high, high) + dot(xi_high, low) + dot(xi_low, high)
+        sums = []
+        for mid in halves:
+            real, imag = mid[k * 128 : k * 128 + 64], mid[k * 128 + 64 : k * 128 + 128]
+            sums.append((real[:, :128] - imag[:, 128:], imag[:, :128] + real[:, 128:]))
+        (re_e, im_e), (re_o, im_o) = sums
+        real = jnp.concatenate([re_e + re_o, re_e - re_o], axis=1)
+        imag = jnp.concatenate([im_e + im_o, im_e - im_o], axis=1)
+        even = dot(xi_ref[0], stack3(jnp.concatenate([real[:32], imag[:32]], axis=0), 0))
+        odd = dot(xi_ref[1], stack3(jnp.concatenate([real[32:], imag[32:]], axis=0), 0))
+        total, delta = even + odd, even - odd
         for parity in range(2):
             for gh in range(2):
                 lanes = slice(gh * 128, gh * 128 + 128)
-                pieces = [out[parity * 64 + p * 16 : parity * 64 + p * 16 + 16, lanes] for p in range(4)]
-                for i, value in enumerate(swap_blocks(pieces)):
-                    send_ref[pl.ds((4 * gh + i) * 6 + k * 2 + parity, 16, stride=48), :] = value
+                pieces = []
+                for p in range(4):
+                    rows = slice(parity * 32 + p * 8, parity * 32 + p * 8 + 8)
+                    pieces.append(
+                        roll_lanes(jnp.concatenate([total[rows, lanes], delta[rows, lanes]], axis=0), 32 * p)
+                    )
+                for i, value in enumerate(mix(pieces)):
+                    send_ref[pl.ds((4 * gh + i) * 96 + k * 2 + parity, 16, stride=6), :] = value
 
 
 def newton_kernel(
     conc_ref,
     phase_ref,
-    curvature,
-    quartic,
-    wells,
+    par_ref,
     after_ref,
     chem_ref,
     chemical_ref,
@@ -421,6 +446,8 @@
     yhigh_ref,
 ):
     del after_ref
+    par = Params(par_ref)
+    curvature, quartic, wells = ([par.row(34 + 4 * i + a) for a in range(4)] for i in range(3))
     for p in range(4):
         rows = pl.ds(p * 32, 32)
         conc = dense(conc_ref[p], conc_ref[p + 4])
@@ -527,7 +554,6 @@
 
 
 VMEM = pl.BlockSpec(memory_space=pltpu.VMEM)
-SMEM = pl.BlockSpec(memory_space=pltpu.SMEM)
 HBM = pl.BlockSpec(memory_space=pltpu.HBM)
 ANY = pl.BlockSpec(memory_space=pl.ANY)
 LIMIT = 12 * 1024 * 1024
@@ -554,19 +580,12 @@
 
 
 def step(labels, seed_noise, conc, curvature, quartic, wells, lame, eigen):
-    tables = [half for t in z_tables() for half in split_np(t)]
-    z_tab = jnp.asarray(np.stack(tables))
-    x_forward, x_inverse = x_tables()
-    xf = jnp.asarray(np.stack(split_np(x_forward)))
-    xi = jnp.asarray(np.stack(split_np(x_inverse)))
-    yt = jnp.asarray(np.stack(split_np(y_table())))
-
-    halves = [pltpu.VMEM((768, 128), BF16), pltpu.VMEM((768, 128), BF16)]
-    plane_scratch = [
-        pltpu.VMEM((384, 256), BF16),
-        pltpu.VMEM((384, 256), BF16),
-        pltpu.VMEM((384, 512), F32),
-    ]
+    z_tab, z_inv = (jnp.asarray(t) for t in z_tables())
+    xf, xi = (jnp.asarray(t) for t in x_tables())
+    yt = jnp.asarray(y_tables())
+
+    data = [pltpu.VMEM((768, 256), BF16)]
+    plane_scratch = [pltpu.VMEM((384, 384), BF16), pltpu.VMEM((384, 384), BF16)]
 
     def shift(value, axis, step):
         count = lax.axis_size(axis)
@@ -589,33 +608,36 @@
     def in_hbm(*arrays):
         return tuple(pltpu.with_memory_space_constraint(a, pltpu.HBM) for a in arrays)
 
-    phase, send, par = call(
+    phase, mat, send, par = call(
         first_kernel,
-        in_hbm(labels, seed_noise, lame, eigen, z_tab),
-        [(4, 128, 128), (768, 128), (40, 128)],
+        in_hbm(labels, seed_noise, lame, eigen, curvature, quartic, wells, z_tab),
+        [(4, 128, 128), (8, 128, 128), (768, 128), (48, 128)],
         [
             pltpu.VMEM((8, 32, 64), jnp.int32),
             pltpu.VMEM((4, 8, 32, 64), F32),
             pltpu.SMEM((2, 4), F32),
             pltpu.SMEM((4, 6), F32),
-            pltpu.VMEM((8, 128, 128), BF16),
-            *halves,
-            pltpu.SemaphoreType.DMA((5,)),
+            pltpu.SMEM((4,), F32),
+            pltpu.SMEM((4,), F32),
+            pltpu.SMEM((4,), F32),
+            pltpu.VMEM((2, 128, 384), BF16),
+            *data,
+            pltpu.SemaphoreType.DMA((8,)),
         ],
-        {i: HBM for i in range(5)},
+        {i: HBM for i in range(8)},
     )
     recv = exchange(send)
 
     own, other = spectrum(recv, ())
     chem, chemical, xlow, xhigh, ylow, yhigh = call(
         newton_kernel,
-        (conc, phase, curvature, quartic, wells, own),
+        (conc, phase, par, own),
         [(128, 128), (4, 128, 128), (96, 128), (96, 128), (24, 128), (24, 128)],
-        special={2: SMEM, 3: SMEM, 4: SMEM, 5: ANY},
+        special={3: ANY},
     )
     halo = [shift(xhigh, "gx", 1), shift(xlow, "gx", -1), shift(yhigh, "gy", 1), shift(ylow, "gy", -1)]
     back = update(own, other, ylow, par)
-    strain, send = call(middle_kernel, (back, phase, par, z_tab), [(6, 128, 128), (768, 128)], halves)
+    strain, send = call(middle_kernel, (back, mat, z_tab, z_inv), [(6, 128, 128), (768, 128)], data)
     own, other = spectrum(exchange(send), ())
     force, conc_next = call(
         laplace_kernel, (phase, chem, chemical, conc, *halo, own), [(4, 128, 128), (8, 32, 64)], special={8: ANY}
@@ -623,10 +645,9 @@
     back = update(own, other, force, par)
     phase_next, stress = call(
         last_kernel,
-        (back, phase, strain, force, par, z_tab),
+        (back, phase, mat, strain, force, par, z_inv),
         [(4, 8, 32, 64), (6, 8, 32, 64)],
         [
-            pltpu.VMEM((6, 128, 128), F32),
             pltpu.VMEM((4, 2, 4, 32, 64), F32),
             pltpu.VMEM((4, 2, 6, 32, 64), F32),
             pltpu.SemaphoreType.DMA((16,)),

time: 99.5 us -> 97.5 us (0.980)
  Pallas kernels: 12 us -> 9.65 us
    pallas_call x9, Pallas kernels: 12 us -> 9.65 us  [call(): pl.pallas_call(kernel, out_shape=shapes, in_specs=specs, out_specs=[out_s...]
  transfers between devices with their start and end apart: 6 -> 6, of which waited for: 1 -> 2; matrix products, arithmetic and copies ran while one was open for 0% -> 0% of each run, Pallas kernels for 3% -> 2%
where the time goes in v4:
time: 97.5 us; the launch traced here: 96.3 us
  blocking collectives  73.8 us (76%)
  starting transfers between devices  9.88 us (10%)
  Pallas kernels  9.65 us (10%)
  waiting for transfers between devices  2.12 us (2%)
    all_to_all x4, blocking collectives, exchange(): y = lax.all_to_all(x.reshape(128, 1, 768), BOTH, 0, 0, tiled=True)  73.8 us
    pallas_call x9, Pallas kernels, call(): pl.pallas_call(kernel, out_shape=shapes, in_specs=specs, out_specs=[out_s...  9.65 us
    ppermute x4, starting transfers between devices, shift(): lax.ppermute(value, axis, [(i, (i + step) % count) for i in range(count)])  9.49 us
  transfers between devices with their start and end apart: 6, of which 2 were waited for; matrix products, arithmetic and copies ran while one was open for 0% of the time, Pallas kernels for 2%

profile of v4, /device:TPU:0, one launch (start us, length us, event | category | flops | bytes accessed | tf_op | source)
XLA Modules:
  0.0 96.3 jit_solution(6509746895863821314)
XLA Ops:
  0.6 1.9 %shard_map.148 = (f32[4,128,128]{2,1,0:T(8,128)S(1)}, f32[8,128,128]{2,1,0:T(8,128)S(1)}, f32[768,128]{1,0:T(8,128)S(1)}, f32[48,128]{1,0:T(8,128)S(1)}) custom-call(s32[8,32,64]{2,1,0:T(8,128)} %refs_0_.1, f32[4,8,32,64]{3,2,1,0:T(8,128)} %refs_1_.1, f32[2,4]{1,0:T(2,128)} %refs_2_.1, f32[4,6]{1,0:T(4,128)} %refs_3_.1, f32[4]{0:T(128)} %refs_4_.1, ...), custom_call_target="tpu_custom_call" | custom-call | flops 4000000 | bytes 4000000 | tf_op jit(solution)/shard_map/pallas_call | solution.py:566
  2.6 0.0 copy-start
  2.6 0.0 copy-start.5
  2.6 22.9 %all_to_all.20 = f32[128,1,768]{2,1,0:T(1,128)S(1)} all-to-all(f32[128,1,768]{2,1,0:T(1,128)S(1)} %bitcast.14), channel_id=1, replica_groups=mesh['gx'=16,'gy'=8] {'gy','gx'}, dimensions={0} | all-to-all | bytes 786432 | tf_op jit(solution)/shard_map/all_to_all | solution.py:578
  25.5 0.0 copy-done
  25.5 0.0 copy-done.5
  25.5 0.0 copy-start.3
  25.5 0.6 shard_map.149.after_ref.own_ref
  26.1 0.2 collective-permute-start
  26.3 0.1 copy-done.3
  26.4 0.0 copy-start.4
  26.4 1.1 %shard_map.150 = (f32[128,128]{1,0:T(8,128)S(1)}, f32[4,128,128]{2,1,0:T(8,128)S(1)}, f32[96,128]{1,0:T(8,128)S(1)}, f32[96,128]{1,0:T(8,128)S(1)}, f32[24,128]{1,0:T(8,128)S(1)}, /*index=5*/f32[24,128]{1,0:T(8,128)S(1)}) custom-call(f32[8,32,64]{2,1,0:T(8,128)S(1)} %copy-done.3, f32[4,128,128]{2,1,0:T(8,128)S(1)} %get-tuple-element.20.phase_ref, ...), custom_call_target="tpu_custom_call" | custom-call | flops 4000000 | bytes 4000000 | tf_op jit(solution)/shard_map/pallas_call | solution.py:566
  27.5 0.4 collective-permute-done.other_ref
  27.9 0.0 copy-done.4
  27.9 0.9 shard_map.151
  28.9 0.0 copy-start.1
  28.9 0.0 copy-start.2
  28.9 16.5 %all_to_all.21 = f32[128,1,768]{2,1,0:T(1,128)S(1)} all-to-all(f32[128,1,768]{2,1,0:T(1,128)S(1)} %bitcast.9), channel_id=1, replica_groups=mesh['gx'=16,'gy'=8] {'gy','gx'}, dimensions={0} | all-to-all | bytes 786432 | tf_op jit(solution)/shard_map/all_to_all | solution.py:578
  45.4 0.0 copy-done.1
  45.4 0.0 copy-done.2
  45.4 0.7 shard_map.152
  46.1 16.5 %all_to_all.22 = f32[128,1,768]{2,1,0:T(1,128)S(1)} all-to-all(f32[128,1,768]{2,1,0:T(1,128)S(1)} %bitcast.15), channel_id=1, replica_groups=mesh['gx'=16,'gy'=8] {'gy','gx'}, dimensions={0} | all-to-all | bytes 786432 | tf_op jit(solution)/shard_map/all_to_all | solution.py:578
  62.6 0.6 shard_map.153.after_ref.own_ref
  63.2 0.2 collective-permute-start.1
  63.4 0.4 collective-permute-start.2
  63.8 5.0 %collective-permute-start.3 = (f32[96,128]{1,0:T(8,128)S(1)}, f32[96,128]{1,0:T(8,128)S(1)}, u32[]{:S(2)}, u32[]{:S(2)}) collective-permute-start(f32[96,128]{1,0:T(8,128)S(1)} %get-tuple-element.28), channel_id=1, source_target_pairs={{0,120},{8,0},{16,8},{24,16},{32,24},{40,32},{48,40},{56,48},{64,5... | collective-permute-start | bytes 147464 | tf_op jit(solution)/shard_map/ppermute | solution.py:592
  68.8 0.6 collective-permute-start.4
  69.4 3.6 %collective-permute-start.5 = (f32[24,128]{1,0:T(8,128)S(1)}, f32[24,128]{1,0:T(8,128)S(1)}, u32[]{:S(2)}, u32[]{:S(2)}) collective-permute-start(f32[24,128]{1,0:T(8,128)S(1)} %get-tuple-element.22.after_ref), channel_id=1, source_target_pairs={{0,7},{1,0},{2,1},{3,2},{4,3},{5,4},{6,5},{7,6},{8,15},{9,8},{10,9... | collective-permute-start | bytes 36872 | tf_op jit(solution)/shard_map/ppermute | solution.py:592
  72.9 1.7 %collective-permute-done.4.ylow_ref = f32[24,128]{1,0:T(8,128)S(1)} collective-permute-done((f32[24,128]{1,0:T(8,128)S(1)}, f32[24,128]{1,0:T(8,128)S(1)}, u32[]{:S(2)}, u32[]{:S(2)}) %collective-permute-start.4) | collective-permute-done | bytes 12320 | tf_op jit(solution)/shard_map/ppermute | solution.py:592
  74.6 0.0 collective-permute-done.5.yhigh_ref
  74.6 0.0 collective-permute-done.2.xlow_ref
  74.6 0.0 collective-permute-done.3.xhigh_ref
  74.6 1.2 %shard_map.154 = (f32[4,128,128]{2,1,0:T(8,128)S(1)}, f32[8,32,64]{2,1,0:T(8,128)}) custom-call(f32[4,128,128]{2,1,0:T(8,128)S(1)} %get-tuple-element.20.phase_ref, f32[128,128]{1,0:T(8,128)S(1)} %get-tuple-element.25.chem_ref, f32[4,128,128]{2,1,0:T(8,128)S(1)} %get-tuple-element.26.chemical_ref, f32[8,32,64]{2,1,0:T(8,128)S(1)} %copy-done.3, ...), custom_call_target="tpu_custom_call" | custom-call | flops 4000000 | bytes 4000000 | tf_op jit(solution)/shard_map/pallas_call | solution.py:566
  75.8 0.0 collective-permute-done.1.other_ref
  75.8 0.9 shard_map.155
  76.8 17.8 %all_to_all.23 = f32[128,1,768]{2,1,0:T(1,128)S(1)} all-to-all(f32[128,1,768]{2,1,0:T(1,128)S(1)} %bitcast.8), channel_id=1, replica_groups=mesh['gx'=16,'gy'=8] {'gy','gx'}, dimensions={0} | all-to-all | bytes 786432 | tf_op jit(solution)/shard_map/all_to_all | solution.py:578
  94.6 1.7 %shard_map.156 = (f32[4,8,32,64]{3,2,1,0:T(8,128)}, f32[6,8,32,64]{3,2,1,0:T(8,128)}) custom-call(f32[768,128]{1,0:T(8,128)S(1)} %bitcast.13, f32[4,128,128]{2,1,0:T(8,128)S(1)} %get-tuple-element.20.phase_ref, f32[8,128,128]{2,1,0:T(8,128)S(1)} %get-tuple-element.23.mat_ref, f32[6,128,128]{2,1,0:T(8,128)S(1)} %get-tuple-element.31.strain_ref, ...), custom_call_target="tpu_custom_call" | custom-call | flops 4000000 | bytes 4000000 | tf_op jit(solution)/shard_map/pallas_call | solution.py:566
Async XLA Ops:
  2.6 22.9 %copy-start = (bf16[3,384,256]{2,1,0:T(8,128)(2,1)S(1)}, bf16[3,384,256]{2,1,0:T(8,128)(2,1)}, u32[]{:S(2)}) copy-start(bf16[3,384,256]{2,1,0:T(8,128)(2,1)} %constant.14.clone.y_ref) | copy-start | bytes 1769476
  2.6 22.9 %copy-start.5 = (bf16[2,64,192]{2,1,0:T(8,128)(2,1)S(1)}, bf16[2,64,192]{2,1,0:T(8,128)(2,1)}, u32[]{:S(2)}) copy-start(bf16[2,64,192]{2,1,0:T(8,128)(2,1)} %constant.12.clone.xf_ref) | copy-start | bytes 147460
  25.5 0.9 copy-start.3
  26.1 1.8 %collective-permute-start = (f32[384,256]{1,0:T(8,128)S(1)}, f32[384,256]{1,0:T(8,128)S(1)}, u32[]{:S(2)}, u32[]{:S(2)}) collective-permute-start(f32[384,256]{1,0:T(8,128)S(1)} %shard_map.149.after_ref.own_ref), channel_id=1, source_target_pairs={{0,8},{8,0},{16,24},{24,16},{32,40},{40,32},{48,56},{56,48},{64,72... | collective-permute-start | bytes 1179656 | tf_op jit(solution)/shard_map/ppermute | solution.py:602
  26.4 1.5 %copy-start.4 = (bf16[2,64,192]{2,1,0:T(8,128)(2,1)S(1)}, bf16[2,64,192]{2,1,0:T(8,128)(2,1)}, u32[]{:S(2)}) copy-start(bf16[2,64,192]{2,1,0:T(8,128)(2,1)} %constant.13.clone.xi_ref) | copy-start | bytes 147460
  28.9 16.6 %copy-start.1 = (bf16[2,128,384]{2,1,0:T(8,128)(2,1)S(1)}, bf16[2,128,384]{2,1,0:T(8,128)(2,1)}, u32[]{:S(2)}) copy-start(bf16[2,128,384]{2,1,0:T(8,128)(2,1)} %constant.10.clone.refs_7_.tab_ref) | copy-start | bytes 589828
  28.9 16.6 %copy-start.2 = (bf16[2,384,128]{2,1,0:T(8,128)(2,1)S(1)}, bf16[2,384,128]{2,1,0:T(8,128)(2,1)}, u32[]{:S(2)}) copy-start(bf16[2,384,128]{2,1,0:T(8,128)(2,1)} %constant.11.clone.inv_ref) | copy-start | bytes 589828
  63.2 12.6 %collective-permute-start.1 = (f32[384,256]{1,0:T(8,128)S(1)}, f32[384,256]{1,0:T(8,128)S(1)}, u32[]{:S(2)}, u32[]{:S(2)}) collective-permute-start(f32[384,256]{1,0:T(8,128)S(1)} %shard_map.153.after_ref.own_ref), channel_id=1, source_target_pairs={{0,8},{8,0},{16,24},{24,16},{32,40},{40,32},{48,56},{56,48},{64,72... | collective-permute-start | bytes 1179656 | tf_op jit(solution)/shard_map/ppermute | solution.py:602
  63.4 11.2 %collective-permute-start.2 = (f32[96,128]{1,0:T(8,128)S(1)}, f32[96,128]{1,0:T(8,128)S(1)}, u32[]{:S(2)}, u32[]{:S(2)}) collective-permute-start(f32[96,128]{1,0:T(8,128)S(1)} %get-tuple-element.27), channel_id=1, source_target_pairs={{0,8},{8,16},{16,24},{24,32},{32,40},{40,48},{48,56},{56,64},{64,7... | collective-permute-start | bytes 147464 | tf_op jit(solution)/shard_map/ppermute | solution.py:592
  63.8 10.8 %collective-permute-start.3 = (f32[96,128]{1,0:T(8,128)S(1)}, f32[96,128]{1,0:T(8,128)S(1)}, u32[]{:S(2)}, u32[]{:S(2)}) collective-permute-start(f32[96,128]{1,0:T(8,128)S(1)} %get-tuple-element.28), channel_id=1, source_target_pairs={{0,120},{8,0},{16,8},{24,16},{32,24},{40,32},{48,40},{56,48},{64,5... | collective-permute-start | bytes 147464 | tf_op jit(solution)/shard_map/ppermute | solution.py:592
  68.8 5.8 %collective-permute-start.4 = (f32[24,128]{1,0:T(8,128)S(1)}, f32[24,128]{1,0:T(8,128)S(1)}, u32[]{:S(2)}, u32[]{:S(2)}) collective-permute-start(f32[24,128]{1,0:T(8,128)S(1)} %get-tuple-element.29), channel_id=1, source_target_pairs={{0,1},{1,2},{2,3},{3,4},{4,5},{5,6},{6,7},{7,0},{8,9},{9,10},{10,1... | collective-permute-start | bytes 36872 | tf_op jit(solution)/shard_map/ppermute | solution.py:592
  69.4 5.2 %collective-permute-start.5 = (f32[24,128]{1,0:T(8,128)S(1)}, f32[24,128]{1,0:T(8,128)S(1)}, u32[]{:S(2)}, u32[]{:S(2)}) collective-permute-start(f32[24,128]{1,0:T(8,128)S(1)} %get-tuple-element.22.after_ref), channel_id=1, source_target_pairs={{0,7},{1,0},{2,1},{3,2},{4,3},{5,4},{6,5},{7,6},{8,15},{9,8},{10,9... | collective-permute-start | bytes 36872 | tf_op jit(solution)/shard_map/ppermute | solution.py:592

commit v5 on v4

--- a/solution.py
+++ b/solution.py
@@ -233,15 +233,18 @@
     force_ref,
     par_ref,
     inv_ref,
+    conc_ref,
     next_hbm,
     stress_hbm,
+    conc_hbm,
     next_ref,
     stress_ref,
     sem,
 ):
     par = Params(par_ref)
+    copies = [pltpu.make_async_copy(conc_ref, conc_hbm, sem.at[8])]
+    copies[0].start()
     strain = [strain_ref[c] - z_inverse(inv_ref, recv_ref, c) for c in range(6)]
-    copies = []
     for b in range(4):
         p = cell_block(b)
         rows = block_rows(p)
@@ -249,13 +252,10 @@
         elastic = [strain[c][b * 32 : b * 32 + 32] - eig[c] for c in range(6)]
         stress = stress_from(elastic, lam, shear2)
         for c in range(6):
-            stress_ref[b, 0, c] = stress[c][:, :64]
-            stress_ref[b, 1, c] = stress[c][:, 64:]
-        for half in range(2):
-            x = p + 4 * half
-            at = 4 * b + 2 * half
-            copies.append(pltpu.make_async_copy(stress_ref.at[b, half], stress_hbm.at[:, x], sem.at[at]))
-            copies[-1].start()
+            stress_ref[b, c, 0] = stress[c][:, :64]
+            stress_ref[b, c, 1] = stress[c][:, 64:]
+        copies.append(pltpu.make_async_copy(stress_ref.at[b], stress_hbm.at[:, :, p], sem.at[2 * b]))
+        copies[-1].start()
         trace = elastic[0] + elastic[1] + elastic[2]
         trace = 0.5 * trace * trace
         squares = (
@@ -272,13 +272,10 @@
         mean = 0.25 * (force[0] + force[1] + force[2] + force[3])
         for a in range(4):
             new = phase_ref[a, rows, :] - STEP_PHASE * (force[a] - mean)
-            next_ref[b, 0, a] = new[:, :64]
-            next_ref[b, 1, a] = new[:, 64:]
-        for half in range(2):
-            x = p + 4 * half
-            at = 4 * b + 2 * half + 1
-            copies.append(pltpu.make_async_copy(next_ref.at[b, half], next_hbm.at[:, x], sem.at[at]))
-            copies[-1].start()
+            next_ref[b, a, 0] = new[:, :64]
+            next_ref[b, a, 1] = new[:, 64:]
+        copies.append(pltpu.make_async_copy(next_ref.at[b], next_hbm.at[:, :, p], sem.at[2 * b + 1]))
+        copies[-1].start()
     for copy in copies:
         copy.wait()
 
@@ -296,7 +293,7 @@
 
 
 def spectrum_kernel(recv_ref, xf_ref, y_ref, *refs):
-    out_ref, even_ref, odd_ref = refs[-3:]
+    *out_refs, even_ref, odd_ref = refs[-4:]
     for k in range(3):
         total, delta = [], []
         for par in range(2):
@@ -317,11 +314,10 @@
         odd_ref[rows, :] = stack3(left - right, 1)
     for which, ref in enumerate((even_ref, odd_ref)):
         mid = dot(ref[...], y_ref[which])
-        lanes = slice(which * 128, which * 128 + 128)
         for k in range(3):
             real, imag = mid[k * 128 : k * 128 + 64], mid[k * 128 + 64 : k * 128 + 128]
-            out_ref[pl.ds(k * 128, 64), lanes] = real[:, :128] + imag[:, 128:]
-            out_ref[pl.ds(k * 128 + 64, 64), lanes] = imag[:, :128] - real[:, 128:]
+            out_refs[which][pl.ds(k * 128, 64), :] = real[:, :128] + imag[:, 128:]
+            out_refs[which][pl.ds(k * 128 + 64, 64), :] = imag[:, :128] - real[:, 128:]
 
 
 def green_tile(re, im, wx, wy, omega, first, second, upper):
@@ -358,7 +354,9 @@
     return out
 
 
-def green_kernel(own_ref, other_ref, after_ref, par_ref, xi_ref, y_ref, send_ref, even_ref, odd_ref):
+def green_kernel(*refs):
+    own_refs, other_refs = refs[0:2], refs[2:4]
+    after_ref, par_ref, xi_ref, y_ref, send_ref, even_ref, odd_ref = refs[4:]
     del after_ref
     x_index, y_index = lax.axis_index("gx"), lax.axis_index("gy")
     core = lax.rem(x_index, 2)
@@ -383,10 +381,11 @@
             first = half_mu * inverse
             second = ratio * inverse * inverse
 
-            def get(ref, part):
-                return [ref[pl.ds(k * 128 + part * 64 + tile * 8, 8), :] for k in range(3)]
-
-            low, high = (other_ref, own_ref) if upper else (own_ref, other_ref)
+            def get(pair, part):
+                rows = [pl.ds(k * 128 + part * 64 + tile * 8, 8) for k in range(3)]
+                return [jnp.concatenate([ref[r, :] for ref in pair], axis=1) for r in rows]
+
+            low, high = (other_refs, own_refs) if upper else (own_refs, other_refs)
             re, im = (get(low, part) + get(high, part) for part in range(2))
             out = green_tile(re, im, wx, wy, omega, first, second, upper)
             for part in range(2):
@@ -591,18 +590,12 @@
         count = lax.axis_size(axis)
         return lax.ppermute(value, axis, [(i, (i + step) % count) for i in range(count)])
 
-    def spectrum(recv, after):
-        (own,) = call(
-            spectrum_kernel,
-            (recv, xf, yt, *after),
-            [(384, 256)],
-            plane_scratch,
-            {3 + i: ANY for i in range(len(after))},
-        )
-        return own, lax.ppermute(own, "gx", [(i, i ^ 1) for i in range(16)])
+    def spectrum(recv):
+        own = call(spectrum_kernel, (recv, xf, yt), [(384, 128)] * 2, plane_scratch)
+        return own, [lax.ppermute(v, "gx", [(i, i ^ 1) for i in range(16)]) for v in own]
 
     def update(own, other, after, par):
-        (back,) = call(green_kernel, (own, other, after, par, xi, yt), [(768, 128)], plane_scratch, {2: ANY})
+        (back,) = call(green_kernel, (*own, *other, after, par, xi, yt), [(768, 128)], plane_scratch, {4: ANY})
         return exchange(back)
 
     def in_hbm(*arrays):
@@ -628,33 +621,33 @@
     )
     recv = exchange(send)
 
-    own, other = spectrum(recv, ())
+    own, other = spectrum(recv)
     chem, chemical, xlow, xhigh, ylow, yhigh = call(
         newton_kernel,
-        (conc, phase, par, own),
+        (conc, phase, par, own[0]),
         [(128, 128), (4, 128, 128), (96, 128), (96, 128), (24, 128), (24, 128)],
         special={3: ANY},
     )
     halo = [shift(xhigh, "gx", 1), shift(xlow, "gx", -1), shift(yhigh, "gy", 1), shift(ylow, "gy", -1)]
     back = update(own, other, ylow, par)
     strain, send = call(middle_kernel, (back, mat, z_tab, z_inv), [(6, 128, 128), (768, 128)], data)
-    own, other = spectrum(exchange(send), ())
+    own, other = spectrum(exchange(send))
     force, conc_next = call(
-        laplace_kernel, (phase, chem, chemical, conc, *halo, own), [(4, 128, 128), (8, 32, 64)], special={8: ANY}
+        laplace_kernel, (phase, chem, chemical, conc, *halo, own[0]), [(4, 128, 128), (8, 32, 64)], special={8: ANY}
     )
     back = update(own, other, force, par)
-    phase_next, stress = call(
+    phase_next, stress, conc_next = call(
         last_kernel,
-        (back, phase, mat, strain, force, par, z_inv),
-        [(4, 8, 32, 64), (6, 8, 32, 64)],
+        (back, phase, mat, strain, force, par, z_inv, conc_next),
+        [(4, 2, 4, 32, 64), (6, 2, 4, 32, 64), (8, 32, 64)],
         [
-            pltpu.VMEM((4, 2, 4, 32, 64), F32),
-            pltpu.VMEM((4, 2, 6, 32, 64), F32),
-            pltpu.SemaphoreType.DMA((16,)),
+            pltpu.VMEM((4, 4, 2, 32, 64), F32),
+            pltpu.VMEM((4, 6, 2, 32, 64), F32),
+            pltpu.SemaphoreType.DMA((9,)),
         ],
         out_spec=HBM,
     )
-    return (phase_next, conc_next, stress)
+    return (phase_next.reshape(4, 8, 32, 64), conc_next, stress.reshape(6, 8, 32, 64))
 
 
 def solution(mesh):

time: 97.5 us -> 99 us (1.015)
  waiting for transfers between devices: 2.12 us -> 9.06 us
  starting transfers between devices: 9.88 us -> 7.12 us
  blocking collectives: 73.8 us -> 71.9 us
    ppermute x4, waiting for transfers between devices: 1.68 us -> 8.92 us  [shift(): lax.ppermute(value, axis, [(i, (i + step) % count) for i in range(count)])]
    ppermute x4, starting transfers between devices: 9.49 us -> 5.94 us  [shift(): lax.ppermute(value, axis, [(i, (i + step) % count) for i in range(count)])]
    all_to_all x4, blocking collectives: 73.8 us -> 71.9 us  [exchange(): y = lax.all_to_all(x.reshape(128, 1, 768), BOTH, 0, 0, tiled=True)]
  transfers between devices with their start and end apart: 6 -> 8, of which waited for: 2 -> 3; matrix products, arithmetic and copies ran while one was open for 0% -> 0% of each run, Pallas kernels for 2% -> 2%
where the time goes in v5:
time: 99 us; the launch traced here: 97.8 us
  blocking collectives  71.9 us (73%)
  waiting for transfers between devices  9.06 us (9%)
  Pallas kernels  8.96 us (9%)
  starting transfers between devices  7.12 us (7%)
    all_to_all x4, blocking collectives, exchange(): y = lax.all_to_all(x.reshape(128, 1, 768), BOTH, 0, 0, tiled=True)  71.9 us
    pallas_call x9, Pallas kernels, call(): pl.pallas_call(kernel, out_shape=shapes, in_specs=specs, out_specs=[out_s...  8.96 us
    ppermute x4, waiting for transfers between devices, shift(): lax.ppermute(value, axis, [(i, (i + step) % count) for i in range(count)])  8.92 us
    ppermute x4, starting transfers between devices, shift(): lax.ppermute(value, axis, [(i, (i + step) % count) for i in range(count)])  5.94 us
  transfers between devices with their start and end apart: 8, of which 3 were waited for; matrix products, arithmetic and copies ran while one was open for 0% of the time, Pallas kernels for 2%

profile of v5, /device:TPU:0, one launch (start us, length us, event | category | flops | bytes accessed | tf_op | source)
XLA Modules:
  0.0 97.8 jit_solution(535605719028395648)
XLA Ops:
  0.6 1.9 %shard_map.148 = (f32[4,128,128]{2,1,0:T(8,128)S(1)}, f32[8,128,128]{2,1,0:T(8,128)S(1)}, f32[768,128]{1,0:T(8,128)S(1)}, f32[48,128]{1,0:T(8,128)S(1)}) custom-call(s32[8,32,64]{2,1,0:T(8,128)} %refs_0_.1, f32[4,8,32,64]{3,2,1,0:T(8,128)} %refs_1_.1, f32[2,4]{1,0:T(2,128)} %refs_2_.1, f32[4,6]{1,0:T(4,128)} %refs_3_.1, f32[4]{0:T(128)} %refs_4_.1, ...), custom_call_target="tpu_custom_call" | custom-call | flops 4000000 | bytes 4000000 | tf_op jit(solution)/shard_map/pallas_call | solution.py:565
  2.6 0.0 copy-start
  2.6 0.0 copy-start.5
  2.6 22.9 %all_to_all.20 = f32[128,1,768]{2,1,0:T(1,128)S(1)} all-to-all(f32[128,1,768]{2,1,0:T(1,128)S(1)} %bitcast.16), channel_id=1, replica_groups=mesh['gx'=16,'gy'=8] {'gy','gx'}, dimensions={0} | all-to-all | bytes 786432 | tf_op jit(solution)/shard_map/all_to_all | solution.py:577
  25.5 0.0 copy-done
  25.5 0.0 copy-done.5
  25.5 0.0 copy-start.3
  25.5 0.6 shard_map.149
  26.1 0.2 collective-permute-start.1
  26.3 0.4 collective-permute-start
  26.7 0.0 copy-done.3
  26.7 0.0 copy-start.4
  26.7 1.1 %shard_map.150 = (f32[128,128]{1,0:T(8,128)S(1)}, f32[4,128,128]{2,1,0:T(8,128)S(1)}, f32[96,128]{1,0:T(8,128)S(1)}, f32[96,128]{1,0:T(8,128)S(1)}, f32[24,128]{1,0:T(8,128)S(1)}, /*index=5*/f32[24,128]{1,0:T(8,128)S(1)}) custom-call(f32[8,32,64]{2,1,0:T(8,128)S(1)} %copy-done.3, f32[4,128,128]{2,1,0:T(8,128)S(1)} %get-tuple-element.27.phase_ref, ...), custom_call_target="tpu_custom_call" | custom-call | flops 4000000 | bytes 4000000 | tf_op jit(solution)/shard_map/pallas_call | solution.py:565
  27.8 0.0 collective-permute-done.1.refs_3_
  27.8 0.1 collective-permute-done.refs_2_
  27.9 0.0 copy-done.4
  27.9 0.9 shard_map.151
  28.9 0.0 copy-start.1
  28.9 0.0 copy-start.2
  28.9 16.5 %all_to_all.21 = f32[128,1,768]{2,1,0:T(1,128)S(1)} all-to-all(f32[128,1,768]{2,1,0:T(1,128)S(1)} %bitcast.11), channel_id=1, replica_groups=mesh['gx'=16,'gy'=8] {'gy','gx'}, dimensions={0} | all-to-all | bytes 786432 | tf_op jit(solution)/shard_map/all_to_all | solution.py:577
  45.4 0.0 copy-done.1
  45.4 0.0 copy-done.2
  45.4 0.7 shard_map.152
  46.1 16.5 %all_to_all.22 = f32[128,1,768]{2,1,0:T(1,128)S(1)} all-to-all(f32[128,1,768]{2,1,0:T(1,128)S(1)} %bitcast.17), channel_id=1, replica_groups=mesh['gx'=16,'gy'=8] {'gy','gx'}, dimensions={0} | all-to-all | bytes 786432 | tf_op jit(solution)/shard_map/all_to_all | solution.py:577
  62.6 0.6 shard_map.153
  63.2 0.2 collective-permute-start.3
  63.4 0.4 collective-permute-start.2
  63.8 0.1 collective-permute-start.4
  63.9 5.2 %collective-permute-start.5 = (f32[96,128]{1,0:T(8,128)S(1)}, f32[96,128]{1,0:T(8,128)S(1)}, u32[]{:S(2)}, u32[]{:S(2)}) collective-permute-start(f32[96,128]{1,0:T(8,128)S(1)} %get-tuple-element.37), channel_id=1, source_target_pairs={{0,120},{8,0},{16,8},{24,16},{32,24},{40,32},{48,40},{56,48},{64,5... | collective-permute-start | bytes 147464 | tf_op jit(solution)/shard_map/ppermute | solution.py:591
  69.2 0.6 collective-permute-start.6
  69.8 5.2 %collective-permute-done.6.ylow_ref = f32[24,128]{1,0:T(8,128)S(1)} collective-permute-done((f32[24,128]{1,0:T(8,128)S(1)}, f32[24,128]{1,0:T(8,128)S(1)}, u32[]{:S(2)}, u32[]{:S(2)}) %collective-permute-start.6) | collective-permute-done | bytes 12320 | tf_op jit(solution)/shard_map/ppermute | solution.py:591
  75.0 0.0 collective-permute-start.7
  75.0 3.7 %collective-permute-done.7.yhigh_ref = f32[24,128]{1,0:T(8,128)S(1)} collective-permute-done((f32[24,128]{1,0:T(8,128)S(1)}, f32[24,128]{1,0:T(8,128)S(1)}, u32[]{:S(2)}, u32[]{:S(2)}) %collective-permute-start.7) | collective-permute-done | bytes 12320 | tf_op jit(solution)/shard_map/ppermute | solution.py:591
  78.7 0.0 collective-permute-done.4.xlow_ref
  78.7 0.0 collective-permute-done.5.xhigh_ref
  78.7 0.5 shard_map.154
  79.2 0.0 collective-permute-done.3.refs_3_
  79.2 0.0 collective-permute-done.2.refs_2_
  79.3 0.9 shard_map.155
  80.2 15.9 %all_to_all.23 = f32[128,1,768]{2,1,0:T(1,128)S(1)} all-to-all(f32[128,1,768]{2,1,0:T(1,128)S(1)} %bitcast.10), channel_id=1, replica_groups=mesh['gx'=16,'gy'=8] {'gy','gx'}, dimensions={0} | all-to-all | bytes 786432 | tf_op jit(solution)/shard_map/all_to_all | solution.py:577
  96.1 1.7 %shard_map.156 = (f32[4,2,4,32,64]{4,3,2,1,0:T(8,128)}, f32[6,2,4,32,64]{4,3,2,1,0:T(8,128)}, f32[8,32,64]{2,1,0:T(8,128)}) custom-call(f32[768,128]{1,0:T(8,128)S(1)} %bitcast.15, f32[4,128,128]{2,1,0:T(8,128)S(1)} %get-tuple-element.27.phase_ref, f32[8,128,128]{2,1,0:T(8,128)S(1)} %get-tuple-element.30.mat_ref, ...), custom_call_target="tpu_custom_call" | custom-call | flops 4000000 | bytes 4000000 | tf_op jit(solution)/shard_map/pallas_call | solution.py:565
Async XLA Ops:
  2.6 22.9 %copy-start = (bf16[3,384,256]{2,1,0:T(8,128)(2,1)S(1)}, bf16[3,384,256]{2,1,0:T(8,128)(2,1)}, u32[]{:S(2)}) copy-start(bf16[3,384,256]{2,1,0:T(8,128)(2,1)} %constant.14.clone.y_ref.refs_7_) | copy-start | bytes 1769476
  2.6 22.9 %copy-start.5 = (bf16[2,64,192]{2,1,0:T(8,128)(2,1)S(1)}, bf16[2,64,192]{2,1,0:T(8,128)(2,1)}, u32[]{:S(2)}) copy-start(bf16[2,64,192]{2,1,0:T(8,128)(2,1)} %constant.12.clone.xf_ref) | copy-start | bytes 147460
  25.5 1.2 %copy-start.3 = (f32[8,32,64]{2,1,0:T(8,128)S(1)}, f32[8,32,64]{2,1,0:T(8,128)}, u32[]{:S(2)}) copy-start(f32[8,32,64]{2,1,0:T(8,128)} %conc_ref.3) | copy-start | bytes 196612
  26.1 1.7 %collective-permute-start.1 = (f32[384,128]{1,0:T(8,128)S(1)}, f32[384,128]{1,0:T(8,128)S(1)}, u32[]{:S(2)}, u32[]{:S(2)}) collective-permute-start(f32[384,128]{1,0:T(8,128)S(1)} %get-tuple-element.26.refs_1_), channel_id=1, source_target_pairs={{0,8},{8,0},{16,24},{24,16},{32,40},{40,32},{48,56},{56,48},{64,72... | collective-permute-start | bytes 589832 | tf_op jit(solution)/shard_map/ppermute | solution.py:595
  26.3 1.6 %collective-permute-start = (f32[384,128]{1,0:T(8,128)S(1)}, f32[384,128]{1,0:T(8,128)S(1)}, u32[]{:S(2)}, u32[]{:S(2)}) collective-permute-start(f32[384,128]{1,0:T(8,128)S(1)} %get-tuple-element.25.after_ref.refs_0_), channel_id=1, source_target_pairs={{0,8},{8,0},{16,24},{24,16},{32,40},{40,32},{48,56},{56,48},{64,72... | collective-permute-start | bytes 589832 | tf_op jit(solution)/shard_map/ppermute | solution.py:595
  26.7 1.2 %copy-start.4 = (bf16[2,64,192]{2,1,0:T(8,128)(2,1)S(1)}, bf16[2,64,192]{2,1,0:T(8,128)(2,1)}, u32[]{:S(2)}) copy-start(bf16[2,64,192]{2,1,0:T(8,128)(2,1)} %constant.13.clone.refs_6_) | copy-start | bytes 147460
  28.9 16.6 %copy-start.1 = (bf16[2,384,128]{2,1,0:T(8,128)(2,1)S(1)}, bf16[2,384,128]{2,1,0:T(8,128)(2,1)}, u32[]{:S(2)}) copy-start(bf16[2,384,128]{2,1,0:T(8,128)(2,1)} %constant.11.clone.inv_ref) | copy-start | bytes 589828
  28.9 16.5 %copy-start.2 = (bf16[2,128,384]{2,1,0:T(8,128)(2,1)S(1)}, bf16[2,128,384]{2,1,0:T(8,128)(2,1)}, u32[]{:S(2)}) copy-start(bf16[2,128,384]{2,1,0:T(8,128)(2,1)} %constant.10.clone.refs_7_.tab_ref) | copy-start | bytes 589828
  63.2 16.0 %collective-permute-start.3 = (f32[384,128]{1,0:T(8,128)S(1)}, f32[384,128]{1,0:T(8,128)S(1)}, u32[]{:S(2)}, u32[]{:S(2)}) collective-permute-start(f32[384,128]{1,0:T(8,128)S(1)} %get-tuple-element.33.refs_1_), channel_id=1, source_target_pairs={{0,8},{8,0},{16,24},{24,16},{32,40},{40,32},{48,56},{56,48},{64,72... | collective-permute-start | bytes 589832 | tf_op jit(solution)/shard_map/ppermute | solution.py:595
  63.4 15.8 %collective-permute-start.2 = (f32[384,128]{1,0:T(8,128)S(1)}, f32[384,128]{1,0:T(8,128)S(1)}, u32[]{:S(2)}, u32[]{:S(2)}) collective-permute-start(f32[384,128]{1,0:T(8,128)S(1)} %get-tuple-element.32.after_ref.refs_0_), channel_id=1, source_target_pairs={{0,8},{8,0},{16,24},{24,16},{32,40},{40,32},{48,56},{56,48},{64,72... | collective-permute-start | bytes 589832 | tf_op jit(solution)/shard_map/ppermute | solution.py:595
  63.8 14.9 %collective-permute-start.4 = (f32[96,128]{1,0:T(8,128)S(1)}, f32[96,128]{1,0:T(8,128)S(1)}, u32[]{:S(2)}, u32[]{:S(2)}) collective-permute-start(f32[96,128]{1,0:T(8,128)S(1)} %get-tuple-element.36), channel_id=1, source_target_pairs={{0,8},{8,16},{16,24},{24,32},{32,40},{40,48},{48,56},{56,64},{64,7... | collective-permute-start | bytes 147464 | tf_op jit(solution)/shard_map/ppermute | solution.py:591
  63.9 14.8 %collective-permute-start.5 = (f32[96,128]{1,0:T(8,128)S(1)}, f32[96,128]{1,0:T(8,128)S(1)}, u32[]{:S(2)}, u32[]{:S(2)}) collective-permute-start(f32[96,128]{1,0:T(8,128)S(1)} %get-tuple-element.37), channel_id=1, source_target_pairs={{0,120},{8,0},{16,8},{24,16},{32,24},{40,32},{48,40},{56,48},{64,5... | collective-permute-start | bytes 147464 | tf_op jit(solution)/shard_map/ppermute | solution.py:591
  69.2 5.8 %collective-permute-start.6 = (f32[24,128]{1,0:T(8,128)S(1)}, f32[24,128]{1,0:T(8,128)S(1)}, u32[]{:S(2)}, u32[]{:S(2)}) collective-permute-start(f32[24,128]{1,0:T(8,128)S(1)} %get-tuple-element.38), channel_id=1, source_target_pairs={{0,1},{1,2},{2,3},{3,4},{4,5},{5,6},{6,7},{7,0},{8,9},{9,10},{10,1... | collective-permute-start | bytes 36872 | tf_op jit(solution)/shard_map/ppermute | solution.py:591
  75.0 3.7 %collective-permute-start.7 = (f32[24,128]{1,0:T(8,128)S(1)}, f32[24,128]{1,0:T(8,128)S(1)}, u32[]{:S(2)}, u32[]{:S(2)}) collective-permute-start(f32[24,128]{1,0:T(8,128)S(1)} %get-tuple-element.29.refs_4_), channel_id=1, source_target_pairs={{0,7},{1,0},{2,1},{3,2},{4,3},{5,4},{6,5},{7,6},{8,15},{9,8},{10,9... | collective-permute-start | bytes 36872 | tf_op jit(solution)/shard_map/ppermute | solution.py:591

commit v6 on v5

--- a/solution.py
+++ b/solution.py
@@ -178,8 +178,8 @@
 def first_kernel(*refs):
     sources, (phase_ref, mat_ref, send_ref, par_ref), targets, (data_ref, sem) = refs[:8], refs[8:12], refs[12:20], refs[20:]
     copies = [pltpu.make_async_copy(a, b, sem.at[i]) for i, (a, b) in enumerate(zip(sources, targets))]
-    for copy in copies:
-        copy.start()
+    for i in (1, 0, 2, 3, 7, 4, 5, 6):
+        copies[i].start()
     labels_ref, noise_ref, lame_ref, eigen_ref, *others, tab_ref = targets
     for copy in copies[:4]:
         copy.wait()
@@ -372,11 +372,12 @@
     index = jnp.where(index == 128, 0, jnp.where(index > 128, index - 256, index))
     wy = index.astype(F32) * (1.0 / 256.0)
     row = lax.broadcasted_iota(jnp.int32, (8, 256), 0)
+    rest = wy * wy + omega * omega
 
     def green(upper):
         for tile in range(8):
             wx = (2 * row + (tile % 4 * 16 + tile // 4)).astype(F32) * (1.0 / 128.0)
-            q = wx * wx + wy * wy + omega * omega
+            q = wx * wx + rest
             inverse = 1.0 / jnp.where(q == 0.0, 1.0, q)
             first = half_mu * inverse
             second = ratio * inverse * inverse

time: 99 us -> 98.9 us (level)
  no operation moved by 1% of the time
where the time goes in v6:
time: 98.9 us; the launch traced here: 97.7 us
  blocking collectives  71.9 us (73%)
  waiting for transfers between devices  9.06 us (9%)
  Pallas kernels  8.9 us (9%)
  starting transfers between devices  7.12 us (7%)
    all_to_all x4, blocking collectives, exchange(): y = lax.all_to_all(x.reshape(128, 1, 768), BOTH, 0, 0, tiled=True)  71.9 us
    ppermute x4, waiting for transfers between devices, shift(): lax.ppermute(value, axis, [(i, (i + step) % count) for i in range(count)])  8.92 us
    pallas_call x9, Pallas kernels, call(): pl.pallas_call(kernel, out_shape=shapes, in_specs=specs, out_specs=[out_s...  8.9 us
    ppermute x4, starting transfers between devices, shift(): lax.ppermute(value, axis, [(i, (i + step) % count) for i in range(count)])  5.94 us
  transfers between devices with their start and end apart: 8, of which 3 were waited for; matrix products, arithmetic and copies ran while one was open for 0% of the time, Pallas kernels for 2%

profile of v6, /device:TPU:0, one launch (start us, length us, event | category | flops | bytes accessed | tf_op | source)
XLA Modules:
  0.0 97.7 jit_solution(5565749671903183148)
XLA Ops:
  0.6 1.9 %shard_map.148 = (f32[4,128,128]{2,1,0:T(8,128)S(1)}, f32[8,128,128]{2,1,0:T(8,128)S(1)}, f32[768,128]{1,0:T(8,128)S(1)}, f32[48,128]{1,0:T(8,128)S(1)}) custom-call(s32[8,32,64]{2,1,0:T(8,128)} %refs_0_.1, f32[4,8,32,64]{3,2,1,0:T(8,128)} %refs_1_.1, f32[2,4]{1,0:T(2,128)} %refs_2_.1, f32[4,6]{1,0:T(4,128)} %refs_3_.1, f32[4]{0:T(128)} %refs_4_.1, ...), custom_call_target="tpu_custom_call" | custom-call | flops 4000000 | bytes 4000000 | tf_op jit(solution)/shard_map/pallas_call | solution.py:566
  2.5 0.0 copy-start
  2.5 0.0 copy-start.5
  2.5 22.9 %all_to_all.20 = f32[128,1,768]{2,1,0:T(1,128)S(1)} all-to-all(f32[128,1,768]{2,1,0:T(1,128)S(1)} %bitcast.16), channel_id=1, replica_groups=mesh['gx'=16,'gy'=8] {'gy','gx'}, dimensions={0} | all-to-all | bytes 786432 | tf_op jit(solution)/shard_map/all_to_all | solution.py:578
  25.4 0.0 copy-done
  25.5 0.0 copy-done.5
  25.5 0.0 copy-start.3
  25.5 0.6 shard_map.149
  26.1 0.2 collective-permute-start.1
  26.3 0.4 collective-permute-start
  26.7 0.0 copy-done.3
  26.7 0.0 copy-start.4
  26.7 1.1 %shard_map.150 = (f32[128,128]{1,0:T(8,128)S(1)}, f32[4,128,128]{2,1,0:T(8,128)S(1)}, f32[96,128]{1,0:T(8,128)S(1)}, f32[96,128]{1,0:T(8,128)S(1)}, f32[24,128]{1,0:T(8,128)S(1)}, /*index=5*/f32[24,128]{1,0:T(8,128)S(1)}) custom-call(f32[8,32,64]{2,1,0:T(8,128)S(1)} %copy-done.3, f32[4,128,128]{2,1,0:T(8,128)S(1)} %get-tuple-element.27.phase_ref, ...), custom_call_target="tpu_custom_call" | custom-call | flops 4000000 | bytes 4000000 | tf_op jit(solution)/shard_map/pallas_call | solution.py:566
  27.7 0.0 collective-permute-done.1.refs_3_
  27.7 0.1 collective-permute-done.refs_2_
  27.9 0.0 copy-done.4
  27.9 0.9 shard_map.151
  28.8 0.0 copy-start.1
  28.8 0.0 copy-start.2
  28.8 16.5 %all_to_all.21 = f32[128,1,768]{2,1,0:T(1,128)S(1)} all-to-all(f32[128,1,768]{2,1,0:T(1,128)S(1)} %bitcast.11), channel_id=1, replica_groups=mesh['gx'=16,'gy'=8] {'gy','gx'}, dimensions={0} | all-to-all | bytes 786432 | tf_op jit(solution)/shard_map/all_to_all | solution.py:578
  45.4 0.0 copy-done.1
  45.4 0.0 copy-done.2
  45.4 0.7 shard_map.152
  46.1 16.5 %all_to_all.22 = f32[128,1,768]{2,1,0:T(1,128)S(1)} all-to-all(f32[128,1,768]{2,1,0:T(1,128)S(1)} %bitcast.17), channel_id=1, replica_groups=mesh['gx'=16,'gy'=8] {'gy','gx'}, dimensions={0} | all-to-all | bytes 786432 | tf_op jit(solution)/shard_map/all_to_all | solution.py:578
  62.6 0.6 shard_map.153
  63.2 0.2 collective-permute-start.3
  63.4 0.4 collective-permute-start.2
  63.8 0.1 collective-permute-start.4
  63.9 5.2 %collective-permute-start.5 = (f32[96,128]{1,0:T(8,128)S(1)}, f32[96,128]{1,0:T(8,128)S(1)}, u32[]{:S(2)}, u32[]{:S(2)}) collective-permute-start(f32[96,128]{1,0:T(8,128)S(1)} %get-tuple-element.37), channel_id=1, source_target_pairs={{0,120},{8,0},{16,8},{24,16},{32,24},{40,32},{48,40},{56,48},{64,5... | collective-permute-start | bytes 147464 | tf_op jit(solution)/shard_map/ppermute | solution.py:592
  69.1 0.6 collective-permute-start.6
  69.7 5.2 %collective-permute-done.6.ylow_ref = f32[24,128]{1,0:T(8,128)S(1)} collective-permute-done((f32[24,128]{1,0:T(8,128)S(1)}, f32[24,128]{1,0:T(8,128)S(1)}, u32[]{:S(2)}, u32[]{:S(2)}) %collective-permute-start.6) | collective-permute-done | bytes 12320 | tf_op jit(solution)/shard_map/ppermute | solution.py:592
  74.9 0.0 collective-permute-start.7
  74.9 3.7 %collective-permute-done.7.yhigh_ref = f32[24,128]{1,0:T(8,128)S(1)} collective-permute-done((f32[24,128]{1,0:T(8,128)S(1)}, f32[24,128]{1,0:T(8,128)S(1)}, u32[]{:S(2)}, u32[]{:S(2)}) %collective-permute-start.7) | collective-permute-done | bytes 12320 | tf_op jit(solution)/shard_map/ppermute | solution.py:592
  78.6 0.0 collective-permute-done.4.xlow_ref
  78.6 0.0 collective-permute-done.5.xhigh_ref
  78.6 0.5 shard_map.154
  79.2 0.0 collective-permute-done.3.refs_3_
  79.2 0.0 collective-permute-done.2.refs_2_
  79.2 0.9 shard_map.155
  80.2 15.9 %all_to_all.23 = f32[128,1,768]{2,1,0:T(1,128)S(1)} all-to-all(f32[128,1,768]{2,1,0:T(1,128)S(1)} %bitcast.10), channel_id=1, replica_groups=mesh['gx'=16,'gy'=8] {'gy','gx'}, dimensions={0} | all-to-all | bytes 786432 | tf_op jit(solution)/shard_map/all_to_all | solution.py:578
  96.0 1.7 %shard_map.156 = (f32[4,2,4,32,64]{4,3,2,1,0:T(8,128)}, f32[6,2,4,32,64]{4,3,2,1,0:T(8,128)}, f32[8,32,64]{2,1,0:T(8,128)}) custom-call(f32[768,128]{1,0:T(8,128)S(1)} %bitcast.15, f32[4,128,128]{2,1,0:T(8,128)S(1)} %get-tuple-element.27.phase_ref, f32[8,128,128]{2,1,0:T(8,128)S(1)} %get-tuple-element.30.mat_ref, ...), custom_call_target="tpu_custom_call" | custom-call | flops 4000000 | bytes 4000000 | tf_op jit(solution)/shard_map/pallas_call | solution.py:566
Async XLA Ops:
  2.5 22.9 %copy-start = (bf16[3,384,256]{2,1,0:T(8,128)(2,1)S(1)}, bf16[3,384,256]{2,1,0:T(8,128)(2,1)}, u32[]{:S(2)}) copy-start(bf16[3,384,256]{2,1,0:T(8,128)(2,1)} %constant.14.clone.y_ref.refs_7_) | copy-start | bytes 1769476
  2.5 22.9 %copy-start.5 = (bf16[2,64,192]{2,1,0:T(8,128)(2,1)S(1)}, bf16[2,64,192]{2,1,0:T(8,128)(2,1)}, u32[]{:S(2)}) copy-start(bf16[2,64,192]{2,1,0:T(8,128)(2,1)} %constant.12.clone.xf_ref) | copy-start | bytes 147460
  25.5 1.2 %copy-start.3 = (f32[8,32,64]{2,1,0:T(8,128)S(1)}, f32[8,32,64]{2,1,0:T(8,128)}, u32[]{:S(2)}) copy-start(f32[8,32,64]{2,1,0:T(8,128)} %conc_ref.3) | copy-start | bytes 196612
  26.1 1.7 %collective-permute-start.1 = (f32[384,128]{1,0:T(8,128)S(1)}, f32[384,128]{1,0:T(8,128)S(1)}, u32[]{:S(2)}, u32[]{:S(2)}) collective-permute-start(f32[384,128]{1,0:T(8,128)S(1)} %get-tuple-element.26.refs_1_), channel_id=1, source_target_pairs={{0,8},{8,0},{16,24},{24,16},{32,40},{40,32},{48,56},{56,48},{64,72... | collective-permute-start | bytes 589832 | tf_op jit(solution)/shard_map/ppermute | solution.py:596
  26.3 1.6 %collective-permute-start = (f32[384,128]{1,0:T(8,128)S(1)}, f32[384,128]{1,0:T(8,128)S(1)}, u32[]{:S(2)}, u32[]{:S(2)}) collective-permute-start(f32[384,128]{1,0:T(8,128)S(1)} %get-tuple-element.25.after_ref.refs_0_), channel_id=1, source_target_pairs={{0,8},{8,0},{16,24},{24,16},{32,40},{40,32},{48,56},{56,48},{64,72... | collective-permute-start | bytes 589832 | tf_op jit(solution)/shard_map/ppermute | solution.py:596
  26.7 1.2 %copy-start.4 = (bf16[2,64,192]{2,1,0:T(8,128)(2,1)S(1)}, bf16[2,64,192]{2,1,0:T(8,128)(2,1)}, u32[]{:S(2)}) copy-start(bf16[2,64,192]{2,1,0:T(8,128)(2,1)} %constant.13.clone.refs_6_) | copy-start | bytes 147460
  28.8 16.6 %copy-start.1 = (bf16[2,384,128]{2,1,0:T(8,128)(2,1)S(1)}, bf16[2,384,128]{2,1,0:T(8,128)(2,1)}, u32[]{:S(2)}) copy-start(bf16[2,384,128]{2,1,0:T(8,128)(2,1)} %constant.11.clone.inv_ref) | copy-start | bytes 589828
  28.8 16.5 %copy-start.2 = (bf16[2,128,384]{2,1,0:T(8,128)(2,1)S(1)}, bf16[2,128,384]{2,1,0:T(8,128)(2,1)}, u32[]{:S(2)}) copy-start(bf16[2,128,384]{2,1,0:T(8,128)(2,1)} %constant.10.clone.refs_7_.tab_ref) | copy-start | bytes 589828
  63.2 16.0 %collective-permute-start.3 = (f32[384,128]{1,0:T(8,128)S(1)}, f32[384,128]{1,0:T(8,128)S(1)}, u32[]{:S(2)}, u32[]{:S(2)}) collective-permute-start(f32[384,128]{1,0:T(8,128)S(1)} %get-tuple-element.33.refs_1_), channel_id=1, source_target_pairs={{0,8},{8,0},{16,24},{24,16},{32,40},{40,32},{48,56},{56,48},{64,72... | collective-permute-start | bytes 589832 | tf_op jit(solution)/shard_map/ppermute | solution.py:596
  63.4 15.8 %collective-permute-start.2 = (f32[384,128]{1,0:T(8,128)S(1)}, f32[384,128]{1,0:T(8,128)S(1)}, u32[]{:S(2)}, u32[]{:S(2)}) collective-permute-start(f32[384,128]{1,0:T(8,128)S(1)} %get-tuple-element.32.after_ref.refs_0_), channel_id=1, source_target_pairs={{0,8},{8,0},{16,24},{24,16},{32,40},{40,32},{48,56},{56,48},{64,72... | collective-permute-start | bytes 589832 | tf_op jit(solution)/shard_map/ppermute | solution.py:596
  63.8 14.9 %collective-permute-start.4 = (f32[96,128]{1,0:T(8,128)S(1)}, f32[96,128]{1,0:T(8,128)S(1)}, u32[]{:S(2)}, u32[]{:S(2)}) collective-permute-start(f32[96,128]{1,0:T(8,128)S(1)} %get-tuple-element.36), channel_id=1, source_target_pairs={{0,8},{8,16},{16,24},{24,32},{32,40},{40,48},{48,56},{56,64},{64,7... | collective-permute-start | bytes 147464 | tf_op jit(solution)/shard_map/ppermute | solution.py:592
  63.9 14.8 %collective-permute-start.5 = (f32[96,128]{1,0:T(8,128)S(1)}, f32[96,128]{1,0:T(8,128)S(1)}, u32[]{:S(2)}, u32[]{:S(2)}) collective-permute-start(f32[96,128]{1,0:T(8,128)S(1)} %get-tuple-element.37), channel_id=1, source_target_pairs={{0,120},{8,0},{16,8},{24,16},{32,24},{40,32},{48,40},{56,48},{64,5... | collective-permute-start | bytes 147464 | tf_op jit(solution)/shard_map/ppermute | solution.py:592
  69.1 5.8 %collective-permute-start.6 = (f32[24,128]{1,0:T(8,128)S(1)}, f32[24,128]{1,0:T(8,128)S(1)}, u32[]{:S(2)}, u32[]{:S(2)}) collective-permute-start(f32[24,128]{1,0:T(8,128)S(1)} %get-tuple-element.38), channel_id=1, source_target_pairs={{0,1},{1,2},{2,3},{3,4},{4,5},{5,6},{6,7},{7,0},{8,9},{9,10},{10,1... | collective-permute-start | bytes 36872 | tf_op jit(solution)/shard_map/ppermute | solution.py:592
  74.9 3.7 %collective-permute-start.7 = (f32[24,128]{1,0:T(8,128)S(1)}, f32[24,128]{1,0:T(8,128)S(1)}, u32[]{:S(2)}, u32[]{:S(2)}) collective-permute-start(f32[24,128]{1,0:T(8,128)S(1)} %get-tuple-element.29.refs_4_), channel_id=1, source_target_pairs={{0,7},{1,0},{2,1},{3,2},{4,3},{5,4},{6,5},{7,6},{8,15},{9,8},{10,9... | collective-permute-start | bytes 36872 | tf_op jit(solution)/shard_map/ppermute | solution.py:592
